TPU v7x, 128 devices: a whole 4x4x4 slice. The times are simulated.
128 devices in a mesh: chain: 32 (over x, z, core), arc: 4 (over y).
Axes of the slice: x: 4, y: 4, z: 4, core: 2. Of those that a mesh axis runs over, the one named last changes fastest.
Arguments:
- design: bfloat16 [262144, 512], P(('chain', 'arc')), may hold values from -0.125 to 0.125
- observed: bfloat16 [262144, 512], P(('chain', 'arc')), may hold values from -6 to 6
- row_interval: int32 [262144], P(('chain', 'arc')), may hold values from 0 to 3
- prior_ridge: float32 [128, 512], P(('chain', 'arc')), may hold values from 0.1 to 1
- coupling: float32 [128, 512], P(('chain', 'arc')), may hold values from 1 to 8
Outputs:
- solution: float32 [128, 512, 512], P(('chain', 'arc'))
- residual: float32 [262144, 512], P(('chain', 'arc'))
Inputs may be any that keep to these rules, and one draw needn't show every extreme that they name: `row_interval`: every row's interval lies in the arc of the device that holds the row.
All inputs are finite; a program needn't handle non-finite values.
Results may differ from a plain program's by a relative error of at most 0.00046.
Values may be sent and summed in bfloat16 or wider, within the bound.
No kernel may reach another device: no remote copies, remote signals or barrier semaphores. Data moves between devices by JAX's collectives and lax.ppermute only.
A program may use at most 128 MiB of HBM per device.

v0:
```python
import functools

import jax
import jax.numpy as jnp
from jax import lax
from jax.experimental import pallas as pl
from jax.experimental.pallas import tpu as pltpu
from jax.sharding import PartitionSpec as P

F32 = jnp.float32
BF16 = jnp.bfloat16
PAIR = ("chain", "arc")


SLOTS = 4
LINE = 2 * SLOTS


def seat(t):
    line, spot = t // LINE, t % LINE
    return (2 * line + spot % 2) * SLOTS + spot // 2


def carry(value, source_of, target_of):
    count = lax.axis_size(PAIR)
    pairs = [(source_of(t), target_of(t)) for t in range(count)]
    return lax.ppermute(value, PAIR, [pair for pair in pairs if pair[1] is not None])


def along(value, steps):
    count = lax.axis_size(PAIR)
    return carry(value, seat, lambda t: seat(t + steps) if 0 <= t + steps < count else None)


def home(t):
    return t


def to_seat(value, m):
    return carry(value, lambda t: t - t % SLOTS + (t % SLOTS ^ m), seat)


def to_arc(value, m):
    return carry(value, seat, lambda t: t - t % SLOTS + (t % SLOTS ^ m))


def dot1(a, b):
    return lax.dot_general(a, b, (((1,), (0,)), ((), ())), preferred_element_type=F32)


def split(x):
    high = x.astype(BF16)
    return high, (x - high.astype(F32)).astype(BF16)


def dot3(a, b):
    (ah, al), (bh, bl) = a, b
    return dot1(ah, bh) + (dot1(ah, bl) + dot1(al, bh))


def dot_full(a, b):
    return lax.dot_general(
        a, b, (((1,), (0,)), ((), ())), precision=lax.Precision.HIGHEST, preferred_element_type=F32
    )


def eye_mask(n):
    return lax.broadcasted_iota(jnp.int32, (n, n), 0) == lax.broadcasted_iota(jnp.int32, (n, n), 1)


def to_column(row, eye):
    return jnp.sum(jnp.where(eye, row, 0.0), axis=1, keepdims=True)


def invert(x_ref, q_rows, slots, r_ref, q_ref, bh_ref, bl_ref):
    n = x_ref.shape[0]
    b_ref = slots.at[0]
    eye = eye_mask(n)
    one = jnp.where(eye, 1.0, 0.0).astype(F32)
    b = b_ref[...]
    picked = jnp.where(eye, b, 0.0)
    s_row = lax.rsqrt(jnp.sum(picked, axis=0, keepdims=True))
    s_col = lax.rsqrt(jnp.sum(picked, axis=1, keepdims=True))
    b = b * s_row * s_col
    b_ref[...] = b
    high, low = split(b)
    bh_ref[...] = high
    bl_ref[...] = low
    x_ref[...] = one - b
    r0 = x_ref[...].astype(BF16)
    square = dot1(r0, r0)
    r_ref[...] = square.astype(BF16)
    fourth = dot1(r_ref[...], r_ref[...])
    well = jnp.sum(fourth * fourth) < 0.9
    q_ref[...] = fourth.astype(BF16)

    @pl.when(well)
    def _():
        x_ref[...] += jnp.where(eye_mask(n), 1.0, 0.0)
        x_ref[...] += dot1(x_ref[...].astype(BF16), r_ref[...])
        x_ref[...] += dot1(x_ref[...].astype(BF16), q_ref[...])

        def step(carry):
            count, _ = carry
            residual = jnp.where(eye_mask(n), 1.0, 0.0) - dot3(
                (bh_ref[...], bl_ref[...]), split(x_ref[...])
            )
            r_ref[...] = residual.astype(BF16)
            x_ref[...] += dot1(x_ref[...].astype(BF16), r_ref[...])
            return count + 1, jnp.sum(residual * residual)

        lax.while_loop(
            lambda carry: jnp.logical_and(carry[0] < 12, carry[1] > 4e-5),
            step,
            (jnp.int32(0), jnp.float32(1.0)),
        )

    @pl.when(jnp.logical_not(well))
    def _():
        def rows_of(i, size=PART):
            return pl.ds(pl.multiple_of(i * size, size), size)

        def ones_of(i):
            spot = lax.broadcasted_iota(jnp.int32, (PART, n), 0) + i * PART
            return jnp.where(spot == lax.broadcasted_iota(jnp.int32, (PART, n), 1), 1.0, 0.0)

        def widest(i, largest):
            return jnp.maximum(largest, jnp.max(jnp.sum(jnp.abs(slots[0, rows_of(i), :]), axis=1, keepdims=True)))

        alpha = 2.0 / (1.0 + lax.fori_loop(0, n // PART, widest, jnp.float32(1.0)))

        def start(i, _):
            slots[1, rows_of(i), :] = alpha * ones_of(i)
            return 0

        lax.fori_loop(0, n // PART, start, 0)

        def phase(number, total):
            first, second = number // (n // PART), number % (n // PART)
            row = rows_of(second)
            pl.when(first == 0)(lambda: slots.__setitem__((2, row, slice(None)), ones_of(second)))
            q_rows[...] = slots[first, row, :]
            sign = (2 * first - 1).astype(F32)

            def add(k, _):
                slots[2 - first, row, :] += sign * dot_full(
                    q_rows[:, rows_of(k, STEP)], slots[1 + first, rows_of(k, STEP), :]
                )
                return 0

            lax.fori_loop(0, n // STEP, add, 0)
            return total + jnp.where(first == 0, jnp.sum(slots[2, row, :] * slots[2, row, :]), 0.0)

        lax.while_loop(
            lambda carry: jnp.logical_and(carry[0] < 60, carry[1] > 1e-7),
            lambda carry: (carry[0] + 1, lax.fori_loop(0, 2 * (n // PART), phase, jnp.float32(0.0))),
            (jnp.int32(0), jnp.float32(1.0)),
        )

        def finish(i, _):
            x_ref[rows_of(i), :] = slots[1, rows_of(i), :]
            return 0

        lax.fori_loop(0, n // PART, finish, 0)

    x_ref[...] = x_ref[...] * s_row * s_col


STEP = 128
PART = 64
GRAIN = 1.0 / 128.0
FULL = 32767.0
FINE = 4194304.0
SHIFT = 13000.0
MATRIX = ((0, 80, ((384, 4), (0, 1))), (5, 81, ((256, 3), (128, 2))))
SIDE = ((0, 128, ((0, 4), (128, 4), (256, 4), (384, 4))),)
MATRIX_MSG = (82, 16, 128)
SIDE_MSG = (129, 16, 128)


def power_of(size):
    return jnp.ceil(jnp.log2(jnp.maximum(size, 1e-30)) * STEP)


def to_tiles(value):
    return jnp.clip(jnp.round(value), -FULL, FULL).astype(jnp.int32).astype(jnp.int16)


def encode(msg, plan, piece_of):
    lane = lax.broadcasted_iota(jnp.int32, (STEP, STEP), 1)
    eye = eye_mask(STEP)
    for first, spot, pieces in plan:
        scales = jnp.zeros((STEP, STEP), F32)
        place = 8 * first
        for number, (row, wide) in enumerate(pieces):
            piece = piece_of(row, wide * STEP)
            blocks = [piece[:, i * STEP : i * STEP + STEP] for i in range(wide)]
            if plan is MATRIX:
                own = jnp.sum(jnp.where(eye, blocks[-1], 0.0), axis=1, keepdims=True)
                blocks[-1] = jnp.where(eye, 0.0, blocks[-1])
                power = power_of(jnp.abs(own))
                fine = (own * jnp.exp2(power * (-GRAIN)) - 1.0) * FINE
                scales = jnp.where(lane == 4 + number, power + SHIFT, scales)
                scales = jnp.where(lane == 6 + number, fine, scales)
            size = functools.reduce(jnp.maximum, [jnp.abs(block) for block in blocks])
            power = power_of(jnp.max(size, axis=1, keepdims=True))
            unit = jnp.exp2(power * (-GRAIN)) * FULL
            scales = jnp.where(lane == number, power + SHIFT, scales)
            for block in blocks:
                msg[place : place + 8] = to_tiles(block * unit).reshape(8, 16, STEP)
                place += 8
        msg[spot] = to_tiles(scales.T[0:16, :])


def encode_ref(msg, plan, ref):
    encode(msg, plan, lambda row, width: ref[row : row + STEP, 0:width])


def decode(msg, plan):
    eye = eye_mask(STEP)
    for first, spot, pieces in plan:
        flat = msg[spot].astype(jnp.int32).astype(F32)
        codes = jnp.concatenate([flat, jnp.zeros((STEP - 16, STEP), F32)], axis=0).T
        powers = jnp.exp2((codes - SHIFT) * GRAIN)
        place = 8 * first
        for number, (row, wide) in enumerate(pieces):
            unit = powers[:, number : number + 1] * (1.0 / FULL)
            blocks = []
            for _ in range(wide):
                blocks.append(msg[place : place + 8].reshape(STEP, STEP).astype(jnp.int32).astype(F32) * unit)
                place += 8
            if plan is MATRIX:
                own = powers[:, 4 + number : 5 + number] * (1.0 + codes[:, 6 + number : 7 + number] * (1.0 / FINE))
                blocks[-1] = jnp.where(eye, own, blocks[-1])
            yield row, wide * STEP, jnp.concatenate(blocks, axis=1)


def unpack(msgs, plan, target):
    for pieces in zip(*(decode(msg, plan) for msg in msgs)):
        row, width, _ = pieces[0]
        target[row : row + STEP, 0:width] = functools.reduce(lambda p, q: p + q, [piece[2] for piece in pieces])
    if plan is MATRIX:
        for i in range(4):
            for j in range(i):
                target[j * STEP : j * STEP + STEP, i * STEP : i * STEP + STEP] = target[
                    i * STEP : i * STEP + STEP, j * STEP : j * STEP + STEP
                ].T


def scratch_of(n):
    return [
        pltpu.VMEM((PART, n), F32),
        pltpu.VMEM((3, n, n), F32),
        pltpu.VMEM((n, n), BF16),
        pltpu.VMEM((n, n), BF16),
        pltpu.VMEM((n, n), BF16),
        pltpu.VMEM((n, n), BF16),
    ]


def masked(slot, row_interval, turned):
    pick = jnp.where(row_interval[...] == slot, 1.0, 0.0).astype(BF16)
    return turned[...] * pick


ROUNDS = (3, 2, 1, 0)


def each_round(base, place, row_interval, turned, plan, other, msgs, buf, sems):
    def out(i):
        return pltpu.make_async_copy(buf.at[i], msgs[i], sems.at[i])

    def one(i, _):
        left = masked(place[0] ^ (base - i), row_interval, turned)
        encode(buf.at[i], plan, lambda row, width: dot1(left[row : row + STEP, :], other[:, 0:width]))
        for j in range(len(msgs)):
            pl.when(i == j)(lambda: out(j).start())
        return 0

    lax.fori_loop(0, len(msgs), one, 0)
    for j in range(len(msgs)):
        out(j).wait()


def gram_matrix(place, row_interval, design, turned, *rest):
    turned[...] = design[...].T
    each_round(3, place, row_interval, turned, MATRIX, design, rest[:-2], *rest[-2:])


def gram_side(base, place, row_interval, turned, observed, *rest):
    each_round(base, place, row_interval, turned, SIDE, observed, rest[:-2], *rest[-2:])


def first_matrix(one, two, three, four, vec, b_out, x_out, msg, q_rows, slots, r_ref, q_ref, bh, bl):
    b_ref = slots.at[0]
    n = b_out.shape[0]
    unpack((one, two, three, four), MATRIX, b_ref)
    b_ref[...] += jnp.where(eye_mask(n), vec[0:1, :] + vec[1:2, :] + vec[2:3, :], 0.0)
    b_out[...] = b_ref[...]
    invert(x_out, q_rows, slots, r_ref, q_ref, bh, bl)
    encode_ref(msg, MATRIX, x_out)


def first_side(x, one, two, three, four, f_out, msg, t_ref):
    unpack((one, two, three, four), SIDE, f_out)
    t_ref[...] = dot3(split(x[...]), split(f_out[...]))
    encode_ref(msg, SIDE, t_ref)


def second_matrix(b, low, high, vec, b_out, x_out, up, down, q_rows, slots, r_ref, q_ref, bh, bl):
    b_ref = slots.at[0]
    n = b.shape[0]
    eye = eye_mask(n)
    left, right = vec[1:2, :], vec[2:3, :]
    left_col, right_col = to_column(left, eye), to_column(right, eye)
    unpack((low,), MATRIX, b_ref)
    b_out[...] = b[...] - (left_col * b_ref[...]) * left
    unpack((high,), MATRIX, b_ref)
    b_out[...] -= (right_col * b_ref[...]) * right
    b_ref[...] = b_out[...]
    invert(x_out, q_rows, slots, r_ref, q_ref, bh, bl)
    b_ref[...] = (right_col * x_out[...]) * right
    encode_ref(up, MATRIX, b_ref)
    b_ref[...] = (left_col * x_out[...]) * left
    encode_ref(down, MATRIX, b_ref)


def second_side(x, f, low, high, vec, f_out, up, down, t_ref):
    eye = eye_mask(f.shape[0])
    left_col, right_col = to_column(vec[1:2, :], eye), to_column(vec[2:3, :], eye)
    unpack((low,), SIDE, t_ref)
    f_out[...] = f[...] + left_col * t_ref[...]
    unpack((high,), SIDE, t_ref)
    f_out[...] += right_col * t_ref[...]
    value = dot3(split(x[...]), split(f_out[...]))
    t_ref[...] = right_col * value
    encode_ref(up, SIDE, t_ref)
    t_ref[...] = left_col * value
    encode_ref(down, SIDE, t_ref)


def third_matrix(b, low, high, far_low, far_high, vec, x_out, g_ref, h_ref, q_rows, slots, r_ref, q_ref, bh, bl):
    b_ref = slots.at[0]
    n = b.shape[0]
    eye = eye_mask(n)
    b_ref[...] = b[...]
    for near, far, link in ((low, far_low, vec[1:2, :]), (high, far_high, vec[2:3, :])):
        unpack((near,), MATRIX, g_ref)
        unpack((far,), MATRIX, h_ref)
        g = split(g_ref[...])
        half = dot3(g, split(h_ref[...]))
        b_ref[...] -= (to_column(link, eye) * dot3(split(half), g)) * link
    invert(x_out, q_rows, slots, r_ref, q_ref, bh, bl)


def third_side(x, f, low, high, far_low, far_high, vec, msg, out16, g_ref, t_ref, s_ref):
    eye = eye_mask(f.shape[0])
    s_ref[...] = f[...]
    for near, far, link in ((low, far_low, vec[1:2, :]), (high, far_high, vec[2:3, :])):
        unpack((near,), MATRIX, g_ref)
        unpack((far,), SIDE, t_ref)
        s_ref[...] += to_column(link, eye) * dot3(split(g_ref[...]), split(t_ref[...]))
    t_ref[...] = dot3(split(x[...]), split(s_ref[...]))
    encode_ref(msg, SIDE, t_ref)
    out16[...] = t_ref[...].astype(BF16)


def arrive(msg, out, out16):
    unpack((msg,), SIDE, out)
    out16[...] = out[...].astype(BF16)


def call(kernel, outs, scratch, *args):
    return pl.pallas_call(kernel, out_shape=outs, scratch_shapes=scratch)(*args)


def gram(kernel, kept, msgs, place, *args):
    space = pl.BlockSpec(memory_space=pltpu.VMEM)
    specs = [pl.BlockSpec(memory_space=pltpu.SMEM)] + [space] * len(args)
    return pl.pallas_call(
        kernel,
        out_shape=kept + msgs,
        in_specs=specs,
        out_specs=(space,) * len(kept) + (pl.BlockSpec(memory_space=pl.ANY),) * len(msgs),
        scratch_shapes=[
            pltpu.VMEM((len(msgs),) + msgs[0].shape, jnp.int16),
            pltpu.SemaphoreType.DMA((len(msgs),)),
        ],
    )(place, *args)


def step_of(design, observed, row_interval, prior_ridge, coupling):
    row_count, n = design.shape
    count = lax.axis_size(PAIR)
    chain, place = lax.axis_index("chain"), lax.axis_index("arc")
    time = LINE * (chain // 2) + 2 * place + chain % 2
    square = jax.ShapeDtypeStruct((n, n), F32)
    half = jax.ShapeDtypeStruct((n, n), BF16)
    matrix_msg = jax.ShapeDtypeStruct(MATRIX_MSG, jnp.int16)
    side_msg = jax.ShapeDtypeStruct(SIDE_MSG, jnp.int16)
    flat = row_interval.reshape(1, row_count)
    where = place.astype(jnp.int32).reshape(1)
    plain = [pltpu.VMEM((n, n), F32)]
    work = scratch_of(n)

    turned, *parts = gram(
        gram_matrix, (jax.ShapeDtypeStruct((n, row_count), BF16),), (matrix_msg,) * 4, where, flat, design
    )
    for i, m in enumerate(ROUNDS):
        parts[i] = to_seat(parts[i], m)
    side_parts = []
    for i in (0, 2):
        rounds = ROUNDS[i : i + 2]
        msgs = gram(functools.partial(gram_side, 3 - i), (), (side_msg,) * 2, where, flat, turned, observed)
        for j, m in enumerate(rounds):
            side_parts.append(to_seat(msgs[j], m))
    mine = carry(jnp.concatenate([prior_ridge, coupling], axis=0), home, seat)
    left_link = carry(coupling, home, lambda t: seat(t + 1) if t + 1 < count else None)
    right_link = jnp.where(time == count - 1, 0.0, mine[1:2])
    vec = jnp.concatenate([mine[0:1], left_link, right_link, jnp.zeros((5, n), F32)], axis=0)
    block, inverse, near = call(first_matrix, (square, square, matrix_msg), work, *parts, vec)
    low, high = along(near, 1), along(near, -1)
    side, near_side = call(first_side, (square, side_msg), plain, inverse, *side_parts)
    low_side, high_side = along(near_side, 1), along(near_side, -1)
    block_one, inverse_one, up, down = call(
        second_matrix, (square, square, matrix_msg, matrix_msg), work, block, low, high, vec
    )
    far_low, far_high = along(up, 2), along(down, -2)
    side_one, up_side, down_side = call(
        second_side, (square, side_msg, side_msg), plain, inverse_one, side, low_side, high_side, vec
    )
    far_low_side, far_high_side = along(up_side, 2), along(down_side, -2)
    inverse_two = call(third_matrix, square, plain * 2 + work, block_one, low, high, far_low, far_high, vec)
    code, rounded = call(
        third_side, (side_msg, half), plain * 3, inverse_two, side_one, low, high, far_low_side, far_high_side, vec
    )
    states = []
    for m in range(SLOTS):
        states.append(to_arc(rounded if m else code, m))
    solution, states[0] = call(arrive, (square, half), [], states[0])
    residual = observed.astype(F32)
    for m in range(SLOTS):
        picked = jnp.where((row_interval == (place ^ m))[:, None], design, jnp.zeros((), design.dtype))
        residual = residual - jnp.dot(picked, states[m], preferred_element_type=F32)
    return (solution[None], residual)


def solution(mesh):
    placed = (P(PAIR, None), P(PAIR, None), P(PAIR), P(PAIR, None), P(PAIR, None))
    return jax.shard_map(
        step_of,
        mesh=mesh,
        in_specs=placed,
        out_specs=(P(PAIR, None, None), P(PAIR, None)),
        check_vma=False,
    )
```

profile of v0, /device:TPU:96, one launch (start us, length us, event | category | flops | bytes accessed | tf_op | source)
XLA Modules:
  0.0 197.6 jit_solution(10862596709654029399)
XLA Ops:
  0.7 9.5 %shard_map.68 = (bf16[512,2048]{1,0:T(8,128)(2,1)}, s16[82,16,128]{2,1,0:T(8,128)(2,1)}, s16[82,16,128]{2,1,0:T(8,128)(2,1)}, s16[82,16,128]{2,1,0:T(8,128)(2,1)}, s16[82,16,128]{2,1,0:T(8,128)(2,1)}) custom-call(s32[1]{0:T(128)} %bitcast.place, s32[1,2048]{1,0:T(1,128)} %bitcast.7, bf16[2048,512]{1,0:T(8,128)(2,1)} %design.1), custom_call_target="tpu_custom_call" | custom-call | tf_op jit(solution)/shard_map/pallas_call | solution.py:380
  10.2 2.9 %collective-permute-start = (s16[82,16,128]{2,1,0:T(8,128)(2,1)}, s16[82,16,128]{2,1,0:T(8,128)(2,1)S(1)}, u32[]{:S(2)}, u32[]{:S(2)}) collective-permute-start(s16[82,16,128]{2,1,0:T(8,128)(2,1)} %get-tuple-element.27), channel_id=1, source_target_pairs={{3,0},{2,4},{1,1},{0,5},{7,2},{6,6},{5,3},{4,7},{11,8},{10,12},{9,... | collective-permute-start | bytes 1007624 | tf_op jit(solution)/shard_map/ppermute | solution.py:27
  13.4 2.1 %collective-permute-start.2 = (s16[82,16,128]{2,1,0:T(8,128)(2,1)}, s16[82,16,128]{2,1,0:T(8,128)(2,1)S(1)}, u32[]{:S(2)}, u32[]{:S(2)}) collective-permute-start(s16[82,16,128]{2,1,0:T(8,128)(2,1)} %get-tuple-element.29), channel_id=1, source_target_pairs={{1,0},{0,4},{3,1},{2,5},{5,2},{4,6},{7,3},{6,7},{9,8},{8,12},{11,9... | collective-permute-start | bytes 1007624 | tf_op jit(solution)/shard_map/ppermute | solution.py:27
  16.2 6.0 %collective-permute-start.5 = (f32[1,512]{1,0:T(1,128)S(1)}, f32[1,512]{1,0:T(1,128)S(1)}, u32[]{:S(2)}, u32[]{:S(2)}) collective-permute-start(f32[1,512]{1,0:T(1,128)S(1)} %copy-done.23), channel_id=1, source_target_pairs={{0,4},{1,1},{2,5},{3,2},{4,6},{5,3},{6,7},{7,8},{8,12},{9,9},{10,1... | collective-permute-start | bytes 6152 | tf_op jit(solution)/shard_map/ppermute | solution.py:27
  22.3 5.9 %shard_map.73 = (s16[129,16,128]{2,1,0:T(8,128)(2,1)}, s16[129,16,128]{2,1,0:T(8,128)(2,1)}) custom-call(s32[1]{0:T(128)} %bitcast.place, s32[1,2048]{1,0:T(1,128)} %bitcast.8, bf16[512,2048]{1,0:T(8,128)(2,1)} %get-tuple-element.38.turned, bf16[2048,512]{1,0:T(8,128)(2,1)} %observed.3), custom_call_target="tpu_custom_call" | custom-call | tf_op jit(solution)/shard_map/pallas_call | solution.py:380
  28.2 5.9 %shard_map.72 = (s16[129,16,128]{2,1,0:T(8,128)(2,1)}, s16[129,16,128]{2,1,0:T(8,128)(2,1)}) custom-call(s32[1]{0:T(128)} %bitcast.place, s32[1,2048]{1,0:T(1,128)} %bitcast.9, bf16[512,2048]{1,0:T(8,128)(2,1)} %get-tuple-element.38.turned, bf16[2048,512]{1,0:T(8,128)(2,1)} %observed.3), custom_call_target="tpu_custom_call" | custom-call | tf_op jit(solution)/shard_map/pallas_call | solution.py:380
  37.7 1.9 collective-permute-start.10
  44.4 7.5 %shard_map.69 = (f32[512,512]{1,0:T(8,128)}, f32[512,512]{1,0:T(8,128)}, s16[82,16,128]{2,1,0:T(8,128)(2,1)}) custom-call(s16[82,16,128]{2,1,0:T(8,128)(2,1)} %copy-done.15, s16[82,16,128]{2,1,0:T(8,128)(2,1)} %copy-done.16, s16[82,16,128]{2,1,0:T(8,128)(2,1)} %copy-done.17, s16[82,16,128]{2,1,0:T(8,128)(2,1)} %copy-done.18, f32[8,512]{1,0:T(8,128)} %maximum_maximum_fusion.vec), custom_call_target="tpu_custom_call" | custom-call | tf_op jit(solution)/shard_map/pallas_call | solution.py:374
  51.9 2.1 %collective-permute-done.10.one = s16[129,16,128]{2,1,0:T(8,128)(2,1)S(1)} collective-permute-done((s16[129,16,128]{2,1,0:T(8,128)(2,1)}, s16[129,16,128]{2,1,0:T(8,128)(2,1)S(1)}, u32[]{:S(2)}, u32[]{:S(2)}) %collective-permute-start.10) | collective-permute-done | bytes 528416 | tf_op jit(solution)/shard_map/ppermute | solution.py:27
  54.0 9.6 %collective-permute-done.11.two = s16[129,16,128]{2,1,0:T(8,128)(2,1)S(1)} collective-permute-done((s16[129,16,128]{2,1,0:T(8,128)(2,1)}, s16[129,16,128]{2,1,0:T(8,128)(2,1)S(1)}, u32[]{:S(2)}, u32[]{:S(2)}) %collective-permute-start.11) | collective-permute-done | bytes 528416 | tf_op jit(solution)/shard_map/ppermute | solution.py:27
  64.5 4.5 %shard_map.74 = (f32[512,512]{1,0:T(8,128)}, s16[129,16,128]{2,1,0:T(8,128)(2,1)}) custom-call(f32[512,512]{1,0:T(8,128)} %get-tuple-element.37.x, s16[129,16,128]{2,1,0:T(8,128)(2,1)} %copy-done.9, s16[129,16,128]{2,1,0:T(8,128)(2,1)} %copy-done.10, s16[129,16,128]{2,1,0:T(8,128)(2,1)} %copy-done.7, s16[129,16,128]{2,1,0:T(8,128)(2,1)} %copy-done.8), custom_call_target="tpu_custom_call" | custom-call | tf_op jit(solution)/shard_map/pallas_call | solution.py:374
  68.9 4.5 %collective-permute-start.15 = (s16[129,16,128]{2,1,0:T(8,128)(2,1)}, s16[129,16,128]{2,1,0:T(8,128)(2,1)S(1)}, u32[]{:S(2)}, u32[]{:S(2)}) collective-permute-start(s16[129,16,128]{2,1,0:T(8,128)(2,1)} %get-tuple-element.44), channel_id=1, source_target_pairs={{4,0},{1,4},{5,1},{2,5},{6,2},{3,6},{7,3},{8,7},{12,8},{9,12},{13,... | collective-permute-start | bytes 1585160 | tf_op jit(solution)/shard_map/ppermute | solution.py:27
  73.5 6.8 %collective-permute-start.14 = (s16[129,16,128]{2,1,0:T(8,128)(2,1)}, s16[129,16,128]{2,1,0:T(8,128)(2,1)S(1)}, u32[]{:S(2)}, u32[]{:S(2)}) collective-permute-start(s16[129,16,128]{2,1,0:T(8,128)(2,1)} %get-tuple-element.44), channel_id=1, source_target_pairs={{0,4},{4,1},{1,5},{5,2},{2,6},{6,3},{3,7},{7,8},{8,12},{12,9},{9,1... | collective-permute-start | bytes 1585160 | tf_op jit(solution)/shard_map/ppermute | solution.py:27
  80.3 1.9 collective-permute-start.7
  82.2 6.9 %collective-permute-start.6 = (s16[82,16,128]{2,1,0:T(8,128)(2,1)S(1)}, s16[82,16,128]{2,1,0:T(8,128)(2,1)S(1)}, u32[]{:S(2)}, u32[]{:S(2)}) collective-permute-start(s16[82,16,128]{2,1,0:T(8,128)(2,1)S(1)} %copy-done.24), channel_id=1, source_target_pairs={{0,4},{4,1},{1,5},{5,2},{2,6},{6,3},{3,7},{7,8},{8,12},{12,9},{9,1... | collective-permute-start | bytes 1007624 | tf_op jit(solution)/shard_map/ppermute | solution.py:27
  89.2 6.1 %collective-permute-done.6.low = s16[82,16,128]{2,1,0:T(8,128)(2,1)S(1)} collective-permute-done((s16[82,16,128]{2,1,0:T(8,128)(2,1)S(1)}, s16[82,16,128]{2,1,0:T(8,128)(2,1)S(1)}, u32[]{:S(2)}, u32[]{:S(2)}) %collective-permute-start.6) | collective-permute-done | bytes 335904 | tf_op jit(solution)/shard_map/ppermute | solution.py:27
  96.1 7.8 %shard_map.70 = (f32[512,512]{1,0:T(8,128)}, f32[512,512]{1,0:T(8,128)}, s16[82,16,128]{2,1,0:T(8,128)(2,1)}, s16[82,16,128]{2,1,0:T(8,128)(2,1)}) custom-call(f32[512,512]{1,0:T(8,128)} %get-tuple-element.31.b, s16[82,16,128]{2,1,0:T(8,128)(2,1)} %copy-done.5, s16[82,16,128]{2,1,0:T(8,128)(2,1)} %copy-done.4, f32[8,512]{1,0:T(8,128)} %maximum_maximum_fusion.vec), custom_call_target="tpu_custom_call" | custom-call | tf_op jit(solution)/shard_map/pallas_call | solution.py:374
  104.9 4.9 %shard_map.75 = (f32[512,512]{1,0:T(8,128)}, s16[129,16,128]{2,1,0:T(8,128)(2,1)}, s16[129,16,128]{2,1,0:T(8,128)(2,1)}) custom-call(f32[512,512]{1,0:T(8,128)} %get-tuple-element.36.x, f32[512,512]{1,0:T(8,128)} %get-tuple-element.43.f, s16[129,16,128]{2,1,0:T(8,128)(2,1)} %copy-done.12, s16[129,16,128]{2,1,0:T(8,128)(2,1)} %copy-done.11, ...), custom_call_target="tpu_custom_call" | custom-call | tf_op jit(solution)/shard_map/pallas_call | solution.py:374
  109.8 4.2 %collective-permute-start.16 = (s16[129,16,128]{2,1,0:T(8,128)(2,1)}, s16[129,16,128]{2,1,0:T(8,128)(2,1)S(1)}, u32[]{:S(2)}, u32[]{:S(2)}) collective-permute-start(s16[129,16,128]{2,1,0:T(8,128)(2,1)} %get-tuple-element.46), channel_id=1, source_target_pairs={{0,1},{4,5},{1,2},{5,6},{2,3},{6,7},{3,8},{7,12},{8,9},{12,13},{9,... | collective-permute-start | bytes 1585160 | tf_op jit(solution)/shard_map/ppermute | solution.py:27
  114.0 3.7 %collective-permute-start.17 = (s16[129,16,128]{2,1,0:T(8,128)(2,1)}, s16[129,16,128]{2,1,0:T(8,128)(2,1)S(1)}, u32[]{:S(2)}, u32[]{:S(2)}) collective-permute-start(s16[129,16,128]{2,1,0:T(8,128)(2,1)} %get-tuple-element.47), channel_id=1, source_target_pairs={{1,0},{5,4},{2,1},{6,5},{3,2},{7,6},{8,3},{12,7},{9,8},{13,12},{10... | collective-permute-start | bytes 1585160 | tf_op jit(solution)/shard_map/ppermute | solution.py:27
  117.7 2.1 %collective-permute-start.8 = (s16[82,16,128]{2,1,0:T(8,128)(2,1)S(1)}, s16[82,16,128]{2,1,0:T(8,128)(2,1)S(1)}, u32[]{:S(2)}, u32[]{:S(2)}) collective-permute-start(s16[82,16,128]{2,1,0:T(8,128)(2,1)S(1)} %copy-done.26), channel_id=1, source_target_pairs={{0,1},{4,5},{1,2},{5,6},{2,3},{6,7},{3,8},{7,12},{8,9},{12,13},{9,... | collective-permute-start | bytes 1007624 | tf_op jit(solution)/shard_map/ppermute | solution.py:27
  119.9 6.0 %collective-permute-start.9 = (s16[82,16,128]{2,1,0:T(8,128)(2,1)S(1)}, s16[82,16,128]{2,1,0:T(8,128)(2,1)S(1)}, u32[]{:S(2)}, u32[]{:S(2)}) collective-permute-start(s16[82,16,128]{2,1,0:T(8,128)(2,1)S(1)} %copy-done.25), channel_id=1, source_target_pairs={{1,0},{5,4},{2,1},{6,5},{3,2},{7,6},{8,3},{12,7},{9,8},{13,12},{10... | collective-permute-start | bytes 1007624 | tf_op jit(solution)/shard_map/ppermute | solution.py:27
  125.9 9.1 %collective-permute-done.8.far_low = s16[82,16,128]{2,1,0:T(8,128)(2,1)S(1)} collective-permute-done((s16[82,16,128]{2,1,0:T(8,128)(2,1)S(1)}, s16[82,16,128]{2,1,0:T(8,128)(2,1)S(1)}, u32[]{:S(2)}, u32[]{:S(2)}) %collective-permute-start.8) | collective-permute-done | bytes 335904 | tf_op jit(solution)/shard_map/ppermute | solution.py:27
  137.0 10.3 %shard_map.71.x = f32[512,512]{1,0:T(8,128)} custom-call(f32[512,512]{1,0:T(8,128)} %get-tuple-element.33.b, s16[82,16,128]{2,1,0:T(8,128)(2,1)} %copy-done.5, s16[82,16,128]{2,1,0:T(8,128)(2,1)} %copy-done.4, s16[82,16,128]{2,1,0:T(8,128)(2,1)} %copy-done.19, s16[82,16,128]{2,1,0:T(8,128)(2,1)} %copy-done.20, f32[8,512]{1,0:T(8,128)} %maximum_maximum_fusion.vec), custom_call_target="tpu_custom_call" | custom-call | tf_op jit(solution)/shard_map/pallas_call | solution.py:374
  148.2 6.6 %shard_map.76 = (s16[129,16,128]{2,1,0:T(8,128)(2,1)}, bf16[512,512]{1,0:T(8,128)(2,1)}) custom-call(f32[512,512]{1,0:T(8,128)} %shard_map.71.x, f32[512,512]{1,0:T(8,128)} %get-tuple-element.45.f, s16[82,16,128]{2,1,0:T(8,128)(2,1)} %copy-done.5, s16[82,16,128]{2,1,0:T(8,128)(2,1)} %copy-done.4, s16[129,16,128]{2,1,0:T(8,128)(2,1)} %copy-done.13, ...), custom_call_target="tpu_custom_call" | custom-call | tf_op jit(solution)/shard_map/pallas_call | solution.py:374
  156.4 6.3 %collective-permute-start.21 = (bf16[512,512]{1,0:T(8,128)(2,1)}, bf16[512,512]{1,0:T(8,128)(2,1)S(1)}, u32[]{:S(2)}, u32[]{:S(2)}) collective-permute-start(bf16[512,512]{1,0:T(8,128)(2,1)} %get-tuple-element.51), channel_id=1, source_target_pairs={{0,3},{4,2},{1,1},{5,0},{2,7},{6,6},{3,5},{7,4},{8,11},{12,10},{9,... | collective-permute-start | bytes 1572872 | tf_op jit(solution)/shard_map/ppermute | solution.py:27
  164.3 4.0 %fusion.6 = f32[2048,512]{1,0:T(8,128)} fusion(bf16[512,512]{1,0:T(8,128)(2,1)} %collective-permute-done.19, bf16[2048,512]{1,0:T(8,128)(2,1)S(1)} %copy-done.1, pred[2048]{0:T(1024)(128)(4,1)S(1)} %get-tuple-element.53), kind=kOutput, calls=%fused_computation.5 | convolution fusion | flops 1074790400 | bytes 6817792 | tf_op jit(solution)/shard_map/dot_general | solution.py:444
  168.3 15.8 %collective-permute-done.20 = bf16[512,512]{1,0:T(8,128)(2,1)S(1)} collective-permute-done((bf16[512,512]{1,0:T(8,128)(2,1)}, bf16[512,512]{1,0:T(8,128)(2,1)S(1)}, u32[]{:S(2)}, u32[]{:S(2)}) %collective-permute-start.20) | collective-permute-done | bytes 524320 | tf_op jit(solution)/shard_map/ppermute | solution.py:27
  184.1 2.9 %fusion.4 = f32[2048,512]{1,0:T(8,128)} fusion(bf16[512,512]{1,0:T(8,128)(2,1)S(1)} %collective-permute-done.20, bf16[2048,512]{1,0:T(8,128)(2,1)S(1)} %copy-done.1, pred[2048]{0:T(1024)(128)(4,1)S(1)} %get-tuple-element.55), kind=kOutput, calls=%fused_computation.3 | convolution fusion | flops 1074790400 | bytes 6817792 | tf_op jit(solution)/shard_map/dot_general | solution.py:444
  187.8 2.5 %shard_map.77 = (f32[512,512]{1,0:T(8,128)}, bf16[512,512]{1,0:T(8,128)(2,1)}) custom-call(s16[129,16,128]{2,1,0:T(8,128)(2,1)} %copy-done.6), custom_call_target="tpu_custom_call" | custom-call | tf_op jit(solution)/shard_map/pallas_call | solution.py:374
  190.2 2.5 %fusion.8 = f32[2048,512]{1,0:T(8,128)S(1)} fusion(bf16[512,512]{1,0:T(8,128)(2,1)} %get-tuple-element.50, bf16[2048,512]{1,0:T(8,128)(2,1)S(1)} %copy-done.1, pred[2048]{0:T(1024)(128)(4,1)S(1)} %get-tuple-element.54), kind=kOutput, calls=%fused_computation.7 | convolution fusion | flops 1074790400 | bytes 6817792 | tf_op jit(solution)/shard_map/dot_general | solution.py:444
  194.4 3.1 %subtract_subtract_fusion = f32[2048,512]{1,0:T(8,128)} fusion(f32[2048,512]{1,0:T(8,128)S(1)} %copy-done.3, f32[2048,512]{1,0:T(8,128)S(1)} %copy-done.2, f32[2048,512]{1,0:T(8,128)S(1)} %fusion.8, bf16[2048,512]{1,0:T(8,128)(2,1)S(1)} %copy-done, bf16[512,512]{1,0:T(8,128)(2,1)S(1)} %collective-permute-done.21, bf16[2048,512]{1,0:T(8,128)(2,1)S(1)} %copy-done.1, ...), kind=kOutput, calls=%fused_computation | convolution fusion | flops 1080033280 | bytes 21497856 | tf_op jit(solution)/shard_map/dot_general | solution.py:444
  (86 shorter events, 20.4 us)
Async XLA Ops:
  0.6 14.9 %copy-start.23 = (f32[1,512]{1,0:T(1,128)S(1)}, f32[1,512]{1,0:T(1,128)}, u32[]{:S(2)}) copy-start(f32[1,512]{1,0:T(1,128)} %param.9) | copy-start | bytes 6148
  0.6 14.9 %copy-start.22 = (f32[1,512]{1,0:T(1,128)S(1)}, f32[1,512]{1,0:T(1,128)}, u32[]{:S(2)}) copy-start(f32[1,512]{1,0:T(1,128)} %param.8) | copy-start | bytes 6148
  10.2 27.5 %collective-permute-start = (s16[82,16,128]{2,1,0:T(8,128)(2,1)}, s16[82,16,128]{2,1,0:T(8,128)(2,1)S(1)}, u32[]{:S(2)}, u32[]{:S(2)}) collective-permute-start(s16[82,16,128]{2,1,0:T(8,128)(2,1)} %get-tuple-element.27), channel_id=1, source_target_pairs={{3,0},{2,4},{1,1},{0,5},{7,2},{6,6},{5,3},{4,7},{11,8},{10,12},{9,... | collective-permute-start | bytes 1007624 | tf_op jit(solution)/shard_map/ppermute | solution.py:27
  13.1 26.5 %collective-permute-start.1 = (s16[82,16,128]{2,1,0:T(8,128)(2,1)}, s16[82,16,128]{2,1,0:T(8,128)(2,1)S(1)}, u32[]{:S(2)}, u32[]{:S(2)}) collective-permute-start(s16[82,16,128]{2,1,0:T(8,128)(2,1)} %get-tuple-element.28), channel_id=1, source_target_pairs={{2,0},{3,4},{0,1},{1,5},{6,2},{7,6},{4,3},{5,7},{10,8},{11,12},{8,... | collective-permute-start | bytes 1007624 | tf_op jit(solution)/shard_map/ppermute | solution.py:27
  13.4 27.9 %collective-permute-start.2 = (s16[82,16,128]{2,1,0:T(8,128)(2,1)}, s16[82,16,128]{2,1,0:T(8,128)(2,1)S(1)}, u32[]{:S(2)}, u32[]{:S(2)}) collective-permute-start(s16[82,16,128]{2,1,0:T(8,128)(2,1)} %get-tuple-element.29), channel_id=1, source_target_pairs={{1,0},{0,4},{3,1},{2,5},{5,2},{4,6},{7,3},{6,7},{9,8},{8,12},{11,9... | collective-permute-start | bytes 1007624 | tf_op jit(solution)/shard_map/ppermute | solution.py:27
  15.5 20.4 %collective-permute-start.4 = (f32[2,512]{1,0:T(2,128)S(1)}, f32[2,512]{1,0:T(2,128)S(1)}, u32[]{:S(2)}, u32[]{:S(2)}) collective-permute-start(f32[2,512]{1,0:T(2,128)S(1)} %pad_maximum_fusion), channel_id=1, source_target_pairs={{0,0},{1,4},{2,1},{3,5},{4,2},{5,6},{6,3},{7,7},{8,8},{9,12},{10,9... | collective-permute-start | bytes 12296 | tf_op jit(solution)/shard_map/ppermute | solution.py:27
  16.2 17.9 %collective-permute-start.5 = (f32[1,512]{1,0:T(1,128)S(1)}, f32[1,512]{1,0:T(1,128)S(1)}, u32[]{:S(2)}, u32[]{:S(2)}) collective-permute-start(f32[1,512]{1,0:T(1,128)S(1)} %copy-done.23), channel_id=1, source_target_pairs={{0,4},{1,1},{2,5},{3,2},{4,6},{5,3},{6,7},{7,8},{8,12},{9,9},{10,1... | collective-permute-start | bytes 6152 | tf_op jit(solution)/shard_map/ppermute | solution.py:27
  34.2 17.7 %collective-permute-start.12 = (s16[129,16,128]{2,1,0:T(8,128)(2,1)}, s16[129,16,128]{2,1,0:T(8,128)(2,1)S(1)}, u32[]{:S(2)}, u32[]{:S(2)}) collective-permute-start(s16[129,16,128]{2,1,0:T(8,128)(2,1)} %get-tuple-element.41), channel_id=1, source_target_pairs={{1,0},{0,4},{3,1},{2,5},{5,2},{4,6},{7,3},{6,7},{9,8},{8,12},{11,9... | collective-permute-start | bytes 1585160 | tf_op jit(solution)/shard_map/ppermute | solution.py:27
  36.0 15.9 %collective-permute-start.13 = (s16[129,16,128]{2,1,0:T(8,128)(2,1)}, s16[129,16,128]{2,1,0:T(8,128)(2,1)S(1)}, u32[]{:S(2)}, u32[]{:S(2)}) collective-permute-start(s16[129,16,128]{2,1,0:T(8,128)(2,1)} %get-tuple-element.42), channel_id=1, source_target_pairs={{0,0},{1,4},{2,1},{3,5},{4,2},{5,6},{6,3},{7,7},{8,8},{9,12},{10,9... | collective-permute-start | bytes 1585160 | tf_op jit(solution)/shard_map/ppermute | solution.py:27
  37.7 16.3 %collective-permute-start.10 = (s16[129,16,128]{2,1,0:T(8,128)(2,1)}, s16[129,16,128]{2,1,0:T(8,128)(2,1)S(1)}, u32[]{:S(2)}, u32[]{:S(2)}) collective-permute-start(s16[129,16,128]{2,1,0:T(8,128)(2,1)} %get-tuple-element.39), channel_id=1, source_target_pairs={{3,0},{2,4},{1,1},{0,5},{7,2},{6,6},{5,3},{4,7},{11,8},{10,12},{9,... | collective-permute-start | bytes 1585160 | tf_op jit(solution)/shard_map/ppermute | solution.py:27
  39.6 24.1 %collective-permute-start.11 = (s16[129,16,128]{2,1,0:T(8,128)(2,1)}, s16[129,16,128]{2,1,0:T(8,128)(2,1)S(1)}, u32[]{:S(2)}, u32[]{:S(2)}) collective-permute-start(s16[129,16,128]{2,1,0:T(8,128)(2,1)} %get-tuple-element.40), channel_id=1, source_target_pairs={{2,0},{3,4},{0,1},{1,5},{6,2},{7,6},{4,3},{5,7},{10,8},{11,12},{8,... | collective-permute-start | bytes 1585160 | tf_op jit(solution)/shard_map/ppermute | solution.py:27
  41.3 2.3 %collective-permute-start.3 = (s16[82,16,128]{2,1,0:T(8,128)(2,1)}, s16[82,16,128]{2,1,0:T(8,128)(2,1)S(1)}, u32[]{:S(2)}, u32[]{:S(2)}) collective-permute-start(s16[82,16,128]{2,1,0:T(8,128)(2,1)} %get-tuple-element.30), channel_id=1, source_target_pairs={{0,0},{1,4},{2,1},{3,5},{4,2},{5,6},{6,3},{7,7},{8,8},{9,12},{10,9... | collective-permute-start | bytes 1007624 | tf_op jit(solution)/shard_map/ppermute | solution.py:27
  51.8 28.5 %copy-start.24 = (s16[82,16,128]{2,1,0:T(8,128)(2,1)S(1)}, s16[82,16,128]{2,1,0:T(8,128)(2,1)}, u32[]{:S(2)}) copy-start(s16[82,16,128]{2,1,0:T(8,128)(2,1)} %get-tuple-element.32) | copy-start | bytes 1007620
  51.8 11.8 %copy-start.7 = (s16[129,16,128]{2,1,0:T(8,128)(2,1)}, s16[129,16,128]{2,1,0:T(8,128)(2,1)S(1)}, u32[]{:S(2)}) copy-start(s16[129,16,128]{2,1,0:T(8,128)(2,1)S(1)} %collective-permute-done.12.three) | copy-start | bytes 1585156
  51.9 11.8 %copy-start.8 = (s16[129,16,128]{2,1,0:T(8,128)(2,1)}, s16[129,16,128]{2,1,0:T(8,128)(2,1)S(1)}, u32[]{:S(2)}) copy-start(s16[129,16,128]{2,1,0:T(8,128)(2,1)S(1)} %collective-permute-done.13.four) | copy-start | bytes 1585156
  54.0 9.7 %copy-start.9 = (s16[129,16,128]{2,1,0:T(8,128)(2,1)}, s16[129,16,128]{2,1,0:T(8,128)(2,1)S(1)}, u32[]{:S(2)}) copy-start(s16[129,16,128]{2,1,0:T(8,128)(2,1)S(1)} %collective-permute-done.10.one) | copy-start | bytes 1585156
  68.9 35.0 %collective-permute-start.15 = (s16[129,16,128]{2,1,0:T(8,128)(2,1)}, s16[129,16,128]{2,1,0:T(8,128)(2,1)S(1)}, u32[]{:S(2)}, u32[]{:S(2)}) collective-permute-start(s16[129,16,128]{2,1,0:T(8,128)(2,1)} %get-tuple-element.44), channel_id=1, source_target_pairs={{4,0},{1,4},{5,1},{2,5},{6,2},{3,6},{7,3},{8,7},{12,8},{9,12},{13,... | collective-permute-start | bytes 1585160 | tf_op jit(solution)/shard_map/ppermute | solution.py:27
  73.5 30.4 %collective-permute-start.14 = (s16[129,16,128]{2,1,0:T(8,128)(2,1)}, s16[129,16,128]{2,1,0:T(8,128)(2,1)S(1)}, u32[]{:S(2)}, u32[]{:S(2)}) collective-permute-start(s16[129,16,128]{2,1,0:T(8,128)(2,1)} %get-tuple-element.44), channel_id=1, source_target_pairs={{0,4},{4,1},{1,5},{5,2},{2,6},{6,3},{3,7},{7,8},{8,12},{12,9},{9,1... | collective-permute-start | bytes 1585160 | tf_op jit(solution)/shard_map/ppermute | solution.py:27
  80.3 8.9 %collective-permute-start.7 = (s16[82,16,128]{2,1,0:T(8,128)(2,1)S(1)}, s16[82,16,128]{2,1,0:T(8,128)(2,1)S(1)}, u32[]{:S(2)}, u32[]{:S(2)}) collective-permute-start(s16[82,16,128]{2,1,0:T(8,128)(2,1)S(1)} %copy-done.24), channel_id=1, source_target_pairs={{4,0},{1,4},{5,1},{2,5},{6,2},{3,6},{7,3},{8,7},{12,8},{9,12},{13,... | collective-permute-start | bytes 1007624 | tf_op jit(solution)/shard_map/ppermute | solution.py:27
  82.2 13.1 %collective-permute-start.6 = (s16[82,16,128]{2,1,0:T(8,128)(2,1)S(1)}, s16[82,16,128]{2,1,0:T(8,128)(2,1)S(1)}, u32[]{:S(2)}, u32[]{:S(2)}) collective-permute-start(s16[82,16,128]{2,1,0:T(8,128)(2,1)S(1)} %copy-done.24), channel_id=1, source_target_pairs={{0,4},{4,1},{1,5},{5,2},{2,6},{6,3},{3,7},{7,8},{8,12},{12,9},{9,1... | collective-permute-start | bytes 1007624 | tf_op jit(solution)/shard_map/ppermute | solution.py:27
  103.9 13.8 %copy-start.26 = (s16[82,16,128]{2,1,0:T(8,128)(2,1)S(1)}, s16[82,16,128]{2,1,0:T(8,128)(2,1)}, u32[]{:S(2)}) copy-start(s16[82,16,128]{2,1,0:T(8,128)(2,1)} %get-tuple-element.34) | copy-start | bytes 1007620
  103.9 16.0 %copy-start.25 = (s16[82,16,128]{2,1,0:T(8,128)(2,1)S(1)}, s16[82,16,128]{2,1,0:T(8,128)(2,1)}, u32[]{:S(2)}) copy-start(s16[82,16,128]{2,1,0:T(8,128)(2,1)} %get-tuple-element.35) | copy-start | bytes 1007620
  109.8 37.5 %collective-permute-start.16 = (s16[129,16,128]{2,1,0:T(8,128)(2,1)}, s16[129,16,128]{2,1,0:T(8,128)(2,1)S(1)}, u32[]{:S(2)}, u32[]{:S(2)}) collective-permute-start(s16[129,16,128]{2,1,0:T(8,128)(2,1)} %get-tuple-element.46), channel_id=1, source_target_pairs={{0,1},{4,5},{1,2},{5,6},{2,3},{6,7},{3,8},{7,12},{8,9},{12,13},{9,... | collective-permute-start | bytes 1585160 | tf_op jit(solution)/shard_map/ppermute | solution.py:27
  114.0 33.3 %collective-permute-start.17 = (s16[129,16,128]{2,1,0:T(8,128)(2,1)}, s16[129,16,128]{2,1,0:T(8,128)(2,1)S(1)}, u32[]{:S(2)}, u32[]{:S(2)}) collective-permute-start(s16[129,16,128]{2,1,0:T(8,128)(2,1)} %get-tuple-element.47), channel_id=1, source_target_pairs={{1,0},{5,4},{2,1},{6,5},{3,2},{7,6},{8,3},{12,7},{9,8},{13,12},{10... | collective-permute-start | bytes 1585160 | tf_op jit(solution)/shard_map/ppermute | solution.py:27
  117.7 17.3 %collective-permute-start.8 = (s16[82,16,128]{2,1,0:T(8,128)(2,1)S(1)}, s16[82,16,128]{2,1,0:T(8,128)(2,1)S(1)}, u32[]{:S(2)}, u32[]{:S(2)}) collective-permute-start(s16[82,16,128]{2,1,0:T(8,128)(2,1)S(1)} %copy-done.26), channel_id=1, source_target_pairs={{0,1},{4,5},{1,2},{5,6},{2,3},{6,7},{3,8},{7,12},{8,9},{12,13},{9,... | collective-permute-start | bytes 1007624 | tf_op jit(solution)/shard_map/ppermute | solution.py:27
  119.9 16.4 %collective-permute-start.9 = (s16[82,16,128]{2,1,0:T(8,128)(2,1)S(1)}, s16[82,16,128]{2,1,0:T(8,128)(2,1)S(1)}, u32[]{:S(2)}, u32[]{:S(2)}) collective-permute-start(s16[82,16,128]{2,1,0:T(8,128)(2,1)S(1)} %copy-done.25), channel_id=1, source_target_pairs={{1,0},{5,4},{2,1},{6,5},{3,2},{7,6},{8,3},{12,7},{9,8},{13,12},{10... | collective-permute-start | bytes 1007624 | tf_op jit(solution)/shard_map/ppermute | solution.py:27
  147.3 9.1 %copy-start.21 = (s32[2048]{0:T(1024)S(1)}, s32[2048]{0:T(1024)}, u32[]{:S(2)}) copy-start(s32[2048]{0:T(1024)} %param.7) | copy-start | bytes 24580
  147.3 17.1 %copy-start.1 = (bf16[2048,512]{1,0:T(8,128)(2,1)S(1)}, bf16[2048,512]{1,0:T(8,128)(2,1)}, u32[]{:S(2)}) copy-start(bf16[2048,512]{1,0:T(8,128)(2,1)} %design.1) | copy-start | bytes 6291460
  154.8 9.5 %collective-permute-start.19 = (bf16[512,512]{1,0:T(8,128)(2,1)}, bf16[512,512]{1,0:T(8,128)(2,1)}, u32[]{:S(2)}, u32[]{:S(2)}) collective-permute-start(bf16[512,512]{1,0:T(8,128)(2,1)} %get-tuple-element.51), channel_id=1, source_target_pairs={{0,1},{4,0},{1,3},{5,2},{2,5},{6,4},{3,7},{7,6},{8,9},{12,8},{9,11... | collective-permute-start | bytes 1572872 | tf_op jit(solution)/shard_map/ppermute | solution.py:27
  156.0 28.1 %collective-permute-start.20 = (bf16[512,512]{1,0:T(8,128)(2,1)}, bf16[512,512]{1,0:T(8,128)(2,1)S(1)}, u32[]{:S(2)}, u32[]{:S(2)}) collective-permute-start(bf16[512,512]{1,0:T(8,128)(2,1)} %get-tuple-element.51), channel_id=1, source_target_pairs={{0,2},{4,3},{1,0},{5,1},{2,6},{6,7},{3,4},{7,5},{8,10},{12,11},{9,... | collective-permute-start | bytes 1572872 | tf_op jit(solution)/shard_map/ppermute | solution.py:27
  156.4 36.4 %collective-permute-start.21 = (bf16[512,512]{1,0:T(8,128)(2,1)}, bf16[512,512]{1,0:T(8,128)(2,1)S(1)}, u32[]{:S(2)}, u32[]{:S(2)}) collective-permute-start(bf16[512,512]{1,0:T(8,128)(2,1)} %get-tuple-element.51), channel_id=1, source_target_pairs={{0,3},{4,2},{1,1},{5,0},{2,7},{6,6},{3,5},{7,4},{8,11},{12,10},{9,... | collective-permute-start | bytes 1572872 | tf_op jit(solution)/shard_map/ppermute | solution.py:27
  162.6 24.3 %collective-permute-start.18 = (s16[129,16,128]{2,1,0:T(8,128)(2,1)}, s16[129,16,128]{2,1,0:T(8,128)(2,1)S(1)}, u32[]{:S(2)}, u32[]{:S(2)}) collective-permute-start(s16[129,16,128]{2,1,0:T(8,128)(2,1)} %get-tuple-element.48), channel_id=1, source_target_pairs={{0,0},{4,1},{1,2},{5,3},{2,4},{6,5},{3,6},{7,7},{8,8},{12,9},{9,10... | collective-permute-start | bytes 1585160 | tf_op jit(solution)/shard_map/ppermute | solution.py:27
  (17 other events, 36.7 us)
where the time goes:
time: 198 us
  starting transfers between devices  66.5 us (34%)
  Pallas kernels  65.4 us (33%)
  waiting for transfers between devices  44 us (22%)
  matrix products  12.5 us (6%)
  local copies, waits for them, and re-layouts  7.5 us (4%)
    ppermute x22, starting transfers between devices, carry(): lax.ppermute(value, PAIR, [pair for pair in pairs if pair[1] is not None])  66.5 us
    ppermute x22, waiting for transfers between devices, carry(): lax.ppermute(value, PAIR, [pair for pair in pairs if pair[1] is not None])  44 us
    pallas_call x7, Pallas kernels, call(): return pl.pallas_call(kernel, out_shape=outs, scratch_shapes=scratch)(*args)  44 us
    pallas_call x3, Pallas kernels, gram(): pl.pallas_call(kernel, out_shape=kept + msgs, in_specs=specs, out_specs=(...  21.4 us
    dot_general x4, matrix products, step_of(): residual = residual - jnp.dot(picked, states[m], preferred_element_type=F32)  12.5 us
    unnamed x54, local copies, waits for them, and re-layouts  7.42 us
  transfers between devices with their start and end apart: 22, of which 6 were waited for; matrix products, arithmetic and copies ran while one was open for 5% of the time, Pallas kernels for 20%

commit v1 on v0

--- a/solution.py
+++ b/solution.py
@@ -277,7 +277,7 @@
             pl.when(i == j)(lambda: out(j).start())
         return 0
 
-    lax.fori_loop(0, len(msgs), one, 0)
+    lax.fori_loop(0, len(msgs), one, 0, unroll=2 if plan is MATRIX else 1)
     for j in range(len(msgs)):
         out(j).wait()
 
@@ -365,9 +365,23 @@
     out16[...] = t_ref[...].astype(BF16)
 
 
-def arrive(msg, out, out16):
-    unpack((msg,), SIDE, out)
-    out16[...] = out[...].astype(BF16)
+def predict(place, column, design, partial, code, two, three, out, residual, x_ref):
+    n = out.shape[0]
+
+    @pl.when(pl.program_id(0) == 0)
+    def _():
+        unpack((code,), SIDE, out)
+        x_ref[0:n, :] = out[...].astype(BF16)
+        x_ref[n : 2 * n, :] = two[...]
+        x_ref[2 * n : 3 * n, :] = three[...]
+
+    d = design[...]
+    picked = []
+    for m in (0, 2, 3):
+        pick = jnp.where(column[...] == (place[0] ^ m), 1.0, 0.0)
+        pick = jnp.broadcast_to(pick, (d.shape[0], STEP)).astype(BF16)
+        picked.append(d * jnp.concatenate([pick] * (n // STEP), axis=1))
+    residual[...] = partial[...] - dot1(jnp.concatenate(picked, axis=1), x_ref[...])
 
 
 def call(kernel, outs, scratch, *args):
@@ -437,11 +451,19 @@
     states = []
     for m in range(SLOTS):
         states.append(to_arc(rounded if m else code, m))
-    solution, states[0] = call(arrive, (square, half), [], states[0])
-    residual = observed.astype(F32)
-    for m in range(SLOTS):
-        picked = jnp.where((row_interval == (place ^ m))[:, None], design, jnp.zeros((), design.dtype))
-        residual = residual - jnp.dot(picked, states[m], preferred_element_type=F32)
+    picked = jnp.where((row_interval == (place ^ 1))[:, None], design, jnp.zeros((), design.dtype))
+    partial = observed.astype(F32) - jnp.dot(picked, states[1], preferred_element_type=F32)
+    chunk = row_count // SLOTS
+    whole = pl.BlockSpec(memory_space=pltpu.VMEM)
+    rows = lambda width: pl.BlockSpec((chunk, width), lambda i: (i, 0))
+    solution, residual = pl.pallas_call(
+        predict,
+        grid=(SLOTS,),
+        out_shape=(square, jax.ShapeDtypeStruct((row_count, n), F32)),
+        in_specs=[pl.BlockSpec(memory_space=pltpu.SMEM), rows(1), rows(n), rows(n), whole, whole, whole],
+        out_specs=(pl.BlockSpec((n, n), lambda i: (0, 0)), rows(n)),
+        scratch_shapes=[pltpu.VMEM((3 * n, n), BF16)],
+    )(where, row_interval.reshape(row_count, 1), design, partial, states[0], states[2], states[3])
     return (solution[None], residual)
 
 

time: 198 us -> 197 us (level)
  the two profiles are of different devices: /device:TPU:96 before, /device:TPU:1 now
where the time goes in v1:
time: 197 us; the launch traced here: 195 us
  Pallas kernels  71.1 us (36%)
  starting transfers between devices  63.8 us (32%)
  waiting for transfers between devices  45.2 us (23%)
  local copies, waits for them, and re-layouts  7.72 us (4%)
  matrix products  4.99 us (3%)
    ppermute x22, starting transfers between devices, carry(): lax.ppermute(value, PAIR, [pair for pair in pairs if pair[1] is not None])  63.8 us
    ppermute x22, waiting for transfers between devices, carry(): lax.ppermute(value, PAIR, [pair for pair in pairs if pair[1] is not None])  45.2 us
    pallas_call x6, Pallas kernels, call(): return pl.pallas_call(kernel, out_shape=outs, scratch_shapes=scratch)(*args)  41.6 us
    pallas_call x3, Pallas kernels, gram(): pl.pallas_call(kernel, out_shape=kept + msgs, in_specs=specs, out_specs=(...  20.8 us
    pallas_call x1, Pallas kernels, step_of(): pl.pallas_call(predict, grid=(SLOTS,), out_shape=(square, jax.ShapeDtypeS...  8.63 us
    unnamed x50, local copies, waits for them, and re-layouts  6.27 us
    dot_general x1, matrix products, step_of(): jnp.dot(picked, states[1], preferred_element_type=F32)  4.99 us
  transfers between devices with their start and end apart: 22, of which 6 were waited for; matrix products, arithmetic and copies ran while one was open for 4% of the time, Pallas kernels for 19%

profile of v1, /device:TPU:1, one launch (start us, length us, event | category | flops | bytes accessed | tf_op | source)
XLA Modules:
  0.0 194.5 jit_solution(9816778483721902991)
XLA Ops:
  0.7 9.0 %shard_map.68 = (bf16[512,2048]{1,0:T(8,128)(2,1)}, s16[82,16,128]{2,1,0:T(8,128)(2,1)}, s16[82,16,128]{2,1,0:T(8,128)(2,1)}, s16[82,16,128]{2,1,0:T(8,128)(2,1)}, s16[82,16,128]{2,1,0:T(8,128)(2,1)}) custom-call(s32[1]{0:T(128)} %bitcast.place, s32[1,2048]{1,0:T(1,128)} %bitcast.5, bf16[2048,512]{1,0:T(8,128)(2,1)} %design.3), custom_call_target="tpu_custom_call" | custom-call | tf_op jit(solution)/shard_map/pallas_call | solution.py:394
  9.6 5.5 %collective-permute-start = (s16[82,16,128]{2,1,0:T(8,128)(2,1)}, s16[82,16,128]{2,1,0:T(8,128)(2,1)S(1)}, u32[]{:S(2)}, u32[]{:S(2)}) collective-permute-start(s16[82,16,128]{2,1,0:T(8,128)(2,1)} %get-tuple-element.27), channel_id=1, source_target_pairs={{3,0},{2,4},{1,1},{0,5},{7,2},{6,6},{5,3},{4,7},{11,8},{10,12},{9,... | collective-permute-start | bytes 1007624 | tf_op jit(solution)/shard_map/ppermute | solution.py:27
  16.1 4.7 %collective-permute-start.4 = (f32[2,512]{1,0:T(2,128)S(1)}, f32[2,512]{1,0:T(2,128)S(1)}, u32[]{:S(2)}, u32[]{:S(2)}) collective-permute-start(f32[2,512]{1,0:T(2,128)S(1)} %pad_maximum_fusion), channel_id=1, source_target_pairs={{0,0},{1,4},{2,1},{3,5},{4,2},{5,6},{6,3},{7,7},{8,8},{9,12},{10,9... | collective-permute-start | bytes 12296 | tf_op jit(solution)/shard_map/ppermute | solution.py:27
  20.8 3.6 %collective-permute-start.5 = (f32[1,512]{1,0:T(1,128)S(1)}, f32[1,512]{1,0:T(1,128)S(1)}, u32[]{:S(2)}, u32[]{:S(2)}) collective-permute-start(f32[1,512]{1,0:T(1,128)S(1)} %copy-done.21), channel_id=1, source_target_pairs={{0,4},{1,1},{2,5},{3,2},{4,6},{5,3},{6,7},{7,8},{8,12},{9,9},{10,1... | collective-permute-start | bytes 6152 | tf_op jit(solution)/shard_map/ppermute | solution.py:27
  24.4 5.9 %shard_map.73 = (s16[129,16,128]{2,1,0:T(8,128)(2,1)}, s16[129,16,128]{2,1,0:T(8,128)(2,1)}) custom-call(s32[1]{0:T(128)} %bitcast.place, s32[1,2048]{1,0:T(1,128)} %bitcast.6, bf16[512,2048]{1,0:T(8,128)(2,1)} %get-tuple-element.38.turned, bf16[2048,512]{1,0:T(8,128)(2,1)} %observed.3), custom_call_target="tpu_custom_call" | custom-call | tf_op jit(solution)/shard_map/pallas_call | solution.py:394
  30.4 5.9 %shard_map.72 = (s16[129,16,128]{2,1,0:T(8,128)(2,1)}, s16[129,16,128]{2,1,0:T(8,128)(2,1)}) custom-call(s32[1]{0:T(128)} %bitcast.place, s32[1,2048]{1,0:T(1,128)} %bitcast.7, bf16[512,2048]{1,0:T(8,128)(2,1)} %get-tuple-element.38.turned, bf16[2048,512]{1,0:T(8,128)(2,1)} %observed.3), custom_call_target="tpu_custom_call" | custom-call | tf_op jit(solution)/shard_map/pallas_call | solution.py:394
  36.4 3.6 %collective-permute-start.13 = (s16[129,16,128]{2,1,0:T(8,128)(2,1)}, s16[129,16,128]{2,1,0:T(8,128)(2,1)S(1)}, u32[]{:S(2)}, u32[]{:S(2)}) collective-permute-start(s16[129,16,128]{2,1,0:T(8,128)(2,1)} %get-tuple-element.42), channel_id=1, source_target_pairs={{0,0},{1,4},{2,1},{3,5},{4,2},{5,6},{6,3},{7,7},{8,8},{9,12},{10,9... | collective-permute-start | bytes 1585160 | tf_op jit(solution)/shard_map/ppermute | solution.py:27
  40.0 1.9 collective-permute-start.10
  43.5 3.8 %collective-permute-start.3 = (s16[82,16,128]{2,1,0:T(8,128)(2,1)}, s16[82,16,128]{2,1,0:T(8,128)(2,1)S(1)}, u32[]{:S(2)}, u32[]{:S(2)}) collective-permute-start(s16[82,16,128]{2,1,0:T(8,128)(2,1)} %get-tuple-element.30), channel_id=1, source_target_pairs={{0,0},{1,4},{2,1},{3,5},{4,2},{5,6},{6,3},{7,7},{8,8},{9,12},{10,9... | collective-permute-start | bytes 1007624 | tf_op jit(solution)/shard_map/ppermute | solution.py:27
  48.0 14.9 %collective-permute-done.3.four = s16[82,16,128]{2,1,0:T(8,128)(2,1)S(1)} collective-permute-done((s16[82,16,128]{2,1,0:T(8,128)(2,1)}, s16[82,16,128]{2,1,0:T(8,128)(2,1)S(1)}, u32[]{:S(2)}, u32[]{:S(2)}) %collective-permute-start.3) | collective-permute-done | bytes 335904 | tf_op jit(solution)/shard_map/ppermute | solution.py:27
  63.6 7.5 %shard_map.69 = (f32[512,512]{1,0:T(8,128)}, f32[512,512]{1,0:T(8,128)}, s16[82,16,128]{2,1,0:T(8,128)(2,1)}) custom-call(s16[82,16,128]{2,1,0:T(8,128)(2,1)} %copy-done.13, s16[82,16,128]{2,1,0:T(8,128)(2,1)} %copy-done.14, s16[82,16,128]{2,1,0:T(8,128)(2,1)} %copy-done.15, s16[82,16,128]{2,1,0:T(8,128)(2,1)} %copy-done.16, f32[8,512]{1,0:T(8,128)} %maximum_maximum_fusion.vec), custom_call_target="tpu_custom_call" | custom-call | tf_op jit(solution)/shard_map/pallas_call | solution.py:388
  72.5 4.5 %shard_map.74 = (f32[512,512]{1,0:T(8,128)}, s16[129,16,128]{2,1,0:T(8,128)(2,1)}) custom-call(f32[512,512]{1,0:T(8,128)} %get-tuple-element.37.x, s16[129,16,128]{2,1,0:T(8,128)(2,1)} %copy-done.6, s16[129,16,128]{2,1,0:T(8,128)(2,1)} %copy-done.7, s16[129,16,128]{2,1,0:T(8,128)(2,1)} %copy-done.4, s16[129,16,128]{2,1,0:T(8,128)(2,1)} %copy-done.5), custom_call_target="tpu_custom_call" | custom-call | tf_op jit(solution)/shard_map/pallas_call | solution.py:388
  77.0 1.9 collective-permute-start.15
  78.9 6.9 %collective-permute-start.14 = (s16[129,16,128]{2,1,0:T(8,128)(2,1)}, s16[129,16,128]{2,1,0:T(8,128)(2,1)S(1)}, u32[]{:S(2)}, u32[]{:S(2)}) collective-permute-start(s16[129,16,128]{2,1,0:T(8,128)(2,1)} %get-tuple-element.44), channel_id=1, source_target_pairs={{0,4},{4,1},{1,5},{5,2},{2,6},{6,3},{3,7},{7,8},{8,12},{12,9},{9,1... | collective-permute-start | bytes 1585160 | tf_op jit(solution)/shard_map/ppermute | solution.py:27
  85.9 1.9 collective-permute-start.7
  87.8 3.6 %collective-permute-start.6 = (s16[82,16,128]{2,1,0:T(8,128)(2,1)S(1)}, s16[82,16,128]{2,1,0:T(8,128)(2,1)S(1)}, u32[]{:S(2)}, u32[]{:S(2)}) collective-permute-start(s16[82,16,128]{2,1,0:T(8,128)(2,1)S(1)} %copy-done.22), channel_id=1, source_target_pairs={{0,4},{4,1},{1,5},{5,2},{2,6},{6,3},{3,7},{7,8},{8,12},{12,9},{9,1... | collective-permute-start | bytes 1007624 | tf_op jit(solution)/shard_map/ppermute | solution.py:27
  91.4 3.2 %collective-permute-done.7.high = s16[82,16,128]{2,1,0:T(8,128)(2,1)S(1)} collective-permute-done((s16[82,16,128]{2,1,0:T(8,128)(2,1)S(1)}, s16[82,16,128]{2,1,0:T(8,128)(2,1)S(1)}, u32[]{:S(2)}, u32[]{:S(2)}) %collective-permute-start.7) | collective-permute-done | bytes 335904 | tf_op jit(solution)/shard_map/ppermute | solution.py:27
  96.5 7.8 %shard_map.70 = (f32[512,512]{1,0:T(8,128)}, f32[512,512]{1,0:T(8,128)}, s16[82,16,128]{2,1,0:T(8,128)(2,1)}, s16[82,16,128]{2,1,0:T(8,128)(2,1)}) custom-call(f32[512,512]{1,0:T(8,128)} %get-tuple-element.31.b, s16[82,16,128]{2,1,0:T(8,128)(2,1)} %copy-done.2, s16[82,16,128]{2,1,0:T(8,128)(2,1)} %copy-done.1, f32[8,512]{1,0:T(8,128)} %maximum_maximum_fusion.vec), custom_call_target="tpu_custom_call" | custom-call | tf_op jit(solution)/shard_map/pallas_call | solution.py:388
  105.3 4.9 %shard_map.75 = (f32[512,512]{1,0:T(8,128)}, s16[129,16,128]{2,1,0:T(8,128)(2,1)}, s16[129,16,128]{2,1,0:T(8,128)(2,1)}) custom-call(f32[512,512]{1,0:T(8,128)} %get-tuple-element.36.x, f32[512,512]{1,0:T(8,128)} %get-tuple-element.43.f, s16[129,16,128]{2,1,0:T(8,128)(2,1)} %copy-done.9, s16[129,16,128]{2,1,0:T(8,128)(2,1)} %copy-done.8, ...), custom_call_target="tpu_custom_call" | custom-call | tf_op jit(solution)/shard_map/pallas_call | solution.py:388
  110.2 2.4 %collective-permute-start.16 = (s16[129,16,128]{2,1,0:T(8,128)(2,1)}, s16[129,16,128]{2,1,0:T(8,128)(2,1)S(1)}, u32[]{:S(2)}, u32[]{:S(2)}) collective-permute-start(s16[129,16,128]{2,1,0:T(8,128)(2,1)} %get-tuple-element.46), channel_id=1, source_target_pairs={{0,1},{4,5},{1,2},{5,6},{2,3},{6,7},{3,8},{7,12},{8,9},{12,13},{9,... | collective-permute-start | bytes 1585160 | tf_op jit(solution)/shard_map/ppermute | solution.py:27
  114.0 4.3 %collective-permute-start.8 = (s16[82,16,128]{2,1,0:T(8,128)(2,1)S(1)}, s16[82,16,128]{2,1,0:T(8,128)(2,1)S(1)}, u32[]{:S(2)}, u32[]{:S(2)}) collective-permute-start(s16[82,16,128]{2,1,0:T(8,128)(2,1)S(1)} %copy-done.24), channel_id=1, source_target_pairs={{0,1},{4,5},{1,2},{5,6},{2,3},{6,7},{3,8},{7,12},{8,9},{12,13},{9,... | collective-permute-start | bytes 1007624 | tf_op jit(solution)/shard_map/ppermute | solution.py:27
  119.8 9.5 %collective-permute-done.8.far_low = s16[82,16,128]{2,1,0:T(8,128)(2,1)S(1)} collective-permute-done((s16[82,16,128]{2,1,0:T(8,128)(2,1)S(1)}, s16[82,16,128]{2,1,0:T(8,128)(2,1)S(1)}, u32[]{:S(2)}, u32[]{:S(2)}) %collective-permute-start.8) | collective-permute-done | bytes 335904 | tf_op jit(solution)/shard_map/ppermute | solution.py:27
  129.3 4.5 %collective-permute-done.9.far_high = s16[82,16,128]{2,1,0:T(8,128)(2,1)S(1)} collective-permute-done((s16[82,16,128]{2,1,0:T(8,128)(2,1)S(1)}, s16[82,16,128]{2,1,0:T(8,128)(2,1)S(1)}, u32[]{:S(2)}, u32[]{:S(2)}) %collective-permute-start.9) | collective-permute-done | bytes 335904 | tf_op jit(solution)/shard_map/ppermute | solution.py:27
  134.5 10.3 %shard_map.71.x = f32[512,512]{1,0:T(8,128)} custom-call(f32[512,512]{1,0:T(8,128)} %get-tuple-element.33.b, s16[82,16,128]{2,1,0:T(8,128)(2,1)} %copy-done.2, s16[82,16,128]{2,1,0:T(8,128)(2,1)} %copy-done.1, s16[82,16,128]{2,1,0:T(8,128)(2,1)} %copy-done.17, s16[82,16,128]{2,1,0:T(8,128)(2,1)} %copy-done.18, f32[8,512]{1,0:T(8,128)} %maximum_maximum_fusion.vec), custom_call_target="tpu_custom_call" | custom-call | tf_op jit(solution)/shard_map/pallas_call | solution.py:388
  145.8 6.7 %shard_map.76 = (s16[129,16,128]{2,1,0:T(8,128)(2,1)}, bf16[512,512]{1,0:T(8,128)(2,1)}) custom-call(f32[512,512]{1,0:T(8,128)} %shard_map.71.x, f32[512,512]{1,0:T(8,128)} %get-tuple-element.45.f, s16[82,16,128]{2,1,0:T(8,128)(2,1)} %copy-done.2, s16[82,16,128]{2,1,0:T(8,128)(2,1)} %copy-done.1, s16[129,16,128]{2,1,0:T(8,128)(2,1)} %copy-done.10, ...), custom_call_target="tpu_custom_call" | custom-call | tf_op jit(solution)/shard_map/pallas_call | solution.py:388
  152.5 2.9 %collective-permute-start.18 = (bf16[512,512]{1,0:T(8,128)(2,1)}, bf16[512,512]{1,0:T(8,128)(2,1)}, u32[]{:S(2)}, u32[]{:S(2)}) collective-permute-start(bf16[512,512]{1,0:T(8,128)(2,1)} %get-tuple-element.48), channel_id=1, source_target_pairs={{0,1},{4,0},{1,3},{5,2},{2,5},{6,4},{3,7},{7,6},{8,9},{12,8},{9,11... | collective-permute-start | bytes 1572872 | tf_op jit(solution)/shard_map/ppermute | solution.py:27
  155.4 4.7 %collective-permute-start.21 = (bf16[512,512]{1,0:T(8,128)(2,1)}, bf16[512,512]{1,0:T(8,128)(2,1)S(1)}, u32[]{:S(2)}, u32[]{:S(2)}) collective-permute-start(bf16[512,512]{1,0:T(8,128)(2,1)} %get-tuple-element.48), channel_id=1, source_target_pairs={{0,3},{4,2},{1,1},{5,0},{2,7},{6,6},{3,5},{7,4},{8,11},{12,10},{9,... | collective-permute-start | bytes 1572872 | tf_op jit(solution)/shard_map/ppermute | solution.py:27
  160.1 2.5 %collective-permute-start.20 = (bf16[512,512]{1,0:T(8,128)(2,1)}, bf16[512,512]{1,0:T(8,128)(2,1)}, u32[]{:S(2)}, u32[]{:S(2)}) collective-permute-start(bf16[512,512]{1,0:T(8,128)(2,1)} %get-tuple-element.48), channel_id=1, source_target_pairs={{0,2},{4,3},{1,0},{5,1},{2,6},{6,7},{3,4},{7,5},{8,10},{12,11},{9,... | collective-permute-start | bytes 1572872 | tf_op jit(solution)/shard_map/ppermute | solution.py:27
  162.5 4.2 %collective-permute-start.19 = (s16[129,16,128]{2,1,0:T(8,128)(2,1)}, s16[129,16,128]{2,1,0:T(8,128)(2,1)S(1)}, u32[]{:S(2)}, u32[]{:S(2)}) collective-permute-start(s16[129,16,128]{2,1,0:T(8,128)(2,1)} %get-tuple-element.49), channel_id=1, source_target_pairs={{0,0},{4,1},{1,2},{5,3},{2,4},{6,5},{3,6},{7,7},{8,8},{12,9},{9,10... | collective-permute-start | bytes 1585160 | tf_op jit(solution)/shard_map/ppermute | solution.py:27
  168.1 5.0 %convert_subtract_fusion.partial = f32[2048,512]{1,0:T(8,128)} fusion(bf16[2048,512]{1,0:T(8,128)(2,1)S(1)} %copy-done, bf16[512,512]{1,0:T(8,128)(2,1)} %collective-permute-done.18, bf16[2048,512]{1,0:T(8,128)(2,1)} %design.3, pred[2048]{0:T(1024)(128)(4,1)S(1)} %broadcast_compare_fusion), kind=kOutput, calls=%fused_computation | convolution fusion | flops 1076887552 | bytes 8914944 | tf_op jit(solution)/shard_map/dot_general | solution.py:455
  173.1 12.0 %collective-permute-done.20.two = bf16[512,512]{1,0:T(8,128)(2,1)} collective-permute-done((bf16[512,512]{1,0:T(8,128)(2,1)}, bf16[512,512]{1,0:T(8,128)(2,1)}, u32[]{:S(2)}, u32[]{:S(2)}) %collective-permute-start.20) | collective-permute-done | bytes 524320 | tf_op jit(solution)/shard_map/ppermute | solution.py:27
  185.9 8.6 %shard_map.77 = (f32[512,512]{1,0:T(8,128)}, f32[2048,512]{1,0:T(8,128)}) custom-call(s32[1]{0:T(128)} %bitcast.place, s32[2048,1]{1,0:T(8,128)} %copy.7.column, bf16[2048,512]{1,0:T(8,128)(2,1)} %design.3, f32[2048,512]{1,0:T(8,128)} %convert_subtract_fusion.partial, s16[129,16,128]{2,1,0:T(8,128)(2,1)} %copy-done.3, ...), custom_call_target="tpu_custom_call" | custom-call | tf_op jit(solution)/shard_map/pallas_call | solution.py:459
  (80 shorter events, 14.9 us)
Async XLA Ops:
  0.6 15.4 %copy-start.21 = (f32[1,512]{1,0:T(1,128)S(1)}, f32[1,512]{1,0:T(1,128)}, u32[]{:S(2)}) copy-start(f32[1,512]{1,0:T(1,128)} %param.9) | copy-start | bytes 6148
  0.6 15.4 %copy-start.20 = (f32[1,512]{1,0:T(1,128)S(1)}, f32[1,512]{1,0:T(1,128)}, u32[]{:S(2)}) copy-start(f32[1,512]{1,0:T(1,128)} %param.8) | copy-start | bytes 6148
  9.6 30.4 %collective-permute-start = (s16[82,16,128]{2,1,0:T(8,128)(2,1)}, s16[82,16,128]{2,1,0:T(8,128)(2,1)S(1)}, u32[]{:S(2)}, u32[]{:S(2)}) collective-permute-start(s16[82,16,128]{2,1,0:T(8,128)(2,1)} %get-tuple-element.27), channel_id=1, source_target_pairs={{3,0},{2,4},{1,1},{0,5},{7,2},{6,6},{5,3},{4,7},{11,8},{10,12},{9,... | collective-permute-start | bytes 1007624 | tf_op jit(solution)/shard_map/ppermute | solution.py:27
  15.1 26.8 %collective-permute-start.1 = (s16[82,16,128]{2,1,0:T(8,128)(2,1)}, s16[82,16,128]{2,1,0:T(8,128)(2,1)S(1)}, u32[]{:S(2)}, u32[]{:S(2)}) collective-permute-start(s16[82,16,128]{2,1,0:T(8,128)(2,1)} %get-tuple-element.28), channel_id=1, source_target_pairs={{2,0},{3,4},{0,1},{1,5},{6,2},{7,6},{4,3},{5,7},{10,8},{11,12},{8,... | collective-permute-start | bytes 1007624 | tf_op jit(solution)/shard_map/ppermute | solution.py:27
  15.9 27.7 %collective-permute-start.2 = (s16[82,16,128]{2,1,0:T(8,128)(2,1)}, s16[82,16,128]{2,1,0:T(8,128)(2,1)S(1)}, u32[]{:S(2)}, u32[]{:S(2)}) collective-permute-start(s16[82,16,128]{2,1,0:T(8,128)(2,1)} %get-tuple-element.29), channel_id=1, source_target_pairs={{1,0},{0,4},{3,1},{2,5},{5,2},{4,6},{7,3},{6,7},{9,8},{8,12},{11,9... | collective-permute-start | bytes 1007624 | tf_op jit(solution)/shard_map/ppermute | solution.py:27
  16.1 20.3 %collective-permute-start.4 = (f32[2,512]{1,0:T(2,128)S(1)}, f32[2,512]{1,0:T(2,128)S(1)}, u32[]{:S(2)}, u32[]{:S(2)}) collective-permute-start(f32[2,512]{1,0:T(2,128)S(1)} %pad_maximum_fusion), channel_id=1, source_target_pairs={{0,0},{1,4},{2,1},{3,5},{4,2},{5,6},{6,3},{7,7},{8,8},{9,12},{10,9... | collective-permute-start | bytes 12296 | tf_op jit(solution)/shard_map/ppermute | solution.py:27
  20.8 15.5 %collective-permute-start.5 = (f32[1,512]{1,0:T(1,128)S(1)}, f32[1,512]{1,0:T(1,128)S(1)}, u32[]{:S(2)}, u32[]{:S(2)}) collective-permute-start(f32[1,512]{1,0:T(1,128)S(1)} %copy-done.21), channel_id=1, source_target_pairs={{0,4},{1,1},{2,5},{3,2},{4,6},{5,3},{6,7},{7,8},{8,12},{9,9},{10,1... | collective-permute-start | bytes 6152 | tf_op jit(solution)/shard_map/ppermute | solution.py:27
  36.3 34.8 %collective-permute-start.12 = (s16[129,16,128]{2,1,0:T(8,128)(2,1)}, s16[129,16,128]{2,1,0:T(8,128)(2,1)S(1)}, u32[]{:S(2)}, u32[]{:S(2)}) collective-permute-start(s16[129,16,128]{2,1,0:T(8,128)(2,1)} %get-tuple-element.41), channel_id=1, source_target_pairs={{1,0},{0,4},{3,1},{2,5},{5,2},{4,6},{7,3},{6,7},{9,8},{8,12},{11,9... | collective-permute-start | bytes 1585160 | tf_op jit(solution)/shard_map/ppermute | solution.py:27
  36.4 34.7 %collective-permute-start.13 = (s16[129,16,128]{2,1,0:T(8,128)(2,1)}, s16[129,16,128]{2,1,0:T(8,128)(2,1)S(1)}, u32[]{:S(2)}, u32[]{:S(2)}) collective-permute-start(s16[129,16,128]{2,1,0:T(8,128)(2,1)} %get-tuple-element.42), channel_id=1, source_target_pairs={{0,0},{1,4},{2,1},{3,5},{4,2},{5,6},{6,3},{7,7},{8,8},{9,12},{10,9... | collective-permute-start | bytes 1585160 | tf_op jit(solution)/shard_map/ppermute | solution.py:27
  40.0 22.9 %copy-start.13 = (s16[82,16,128]{2,1,0:T(8,128)(2,1)}, s16[82,16,128]{2,1,0:T(8,128)(2,1)S(1)}, u32[]{:S(2)}) copy-start(s16[82,16,128]{2,1,0:T(8,128)(2,1)S(1)} %collective-permute-done.one) | copy-start | bytes 1007620
  40.0 31.1 %collective-permute-start.10 = (s16[129,16,128]{2,1,0:T(8,128)(2,1)}, s16[129,16,128]{2,1,0:T(8,128)(2,1)S(1)}, u32[]{:S(2)}, u32[]{:S(2)}) collective-permute-start(s16[129,16,128]{2,1,0:T(8,128)(2,1)} %get-tuple-element.39), channel_id=1, source_target_pairs={{3,0},{2,4},{1,1},{0,5},{7,2},{6,6},{5,3},{4,7},{11,8},{10,12},{9,... | collective-permute-start | bytes 1585160 | tf_op jit(solution)/shard_map/ppermute | solution.py:27
  42.0 20.9 %copy-start.14 = (s16[82,16,128]{2,1,0:T(8,128)(2,1)}, s16[82,16,128]{2,1,0:T(8,128)(2,1)S(1)}, u32[]{:S(2)}) copy-start(s16[82,16,128]{2,1,0:T(8,128)(2,1)S(1)} %collective-permute-done.1.two) | copy-start | bytes 1007620
  42.0 29.2 %collective-permute-start.11 = (s16[129,16,128]{2,1,0:T(8,128)(2,1)}, s16[129,16,128]{2,1,0:T(8,128)(2,1)S(1)}, u32[]{:S(2)}, u32[]{:S(2)}) collective-permute-start(s16[129,16,128]{2,1,0:T(8,128)(2,1)} %get-tuple-element.40), channel_id=1, source_target_pairs={{2,0},{3,4},{0,1},{1,5},{6,2},{7,6},{4,3},{5,7},{10,8},{11,12},{8,... | collective-permute-start | bytes 1585160 | tf_op jit(solution)/shard_map/ppermute | solution.py:27
  43.5 19.4 %copy-start.15 = (s16[82,16,128]{2,1,0:T(8,128)(2,1)}, s16[82,16,128]{2,1,0:T(8,128)(2,1)S(1)}, u32[]{:S(2)}) copy-start(s16[82,16,128]{2,1,0:T(8,128)(2,1)S(1)} %collective-permute-done.2.three) | copy-start | bytes 1007620
  43.5 19.4 %collective-permute-start.3 = (s16[82,16,128]{2,1,0:T(8,128)(2,1)}, s16[82,16,128]{2,1,0:T(8,128)(2,1)S(1)}, u32[]{:S(2)}, u32[]{:S(2)}) collective-permute-start(s16[82,16,128]{2,1,0:T(8,128)(2,1)} %get-tuple-element.30), channel_id=1, source_target_pairs={{0,0},{1,4},{2,1},{3,5},{4,2},{5,6},{6,3},{7,7},{8,8},{9,12},{10,9... | collective-permute-start | bytes 1007624 | tf_op jit(solution)/shard_map/ppermute | solution.py:27
  71.1 14.7 %copy-start.22 = (s16[82,16,128]{2,1,0:T(8,128)(2,1)S(1)}, s16[82,16,128]{2,1,0:T(8,128)(2,1)}, u32[]{:S(2)}) copy-start(s16[82,16,128]{2,1,0:T(8,128)(2,1)} %get-tuple-element.32) | copy-start | bytes 1007620
  77.0 27.4 %collective-permute-start.15 = (s16[129,16,128]{2,1,0:T(8,128)(2,1)}, s16[129,16,128]{2,1,0:T(8,128)(2,1)S(1)}, u32[]{:S(2)}, u32[]{:S(2)}) collective-permute-start(s16[129,16,128]{2,1,0:T(8,128)(2,1)} %get-tuple-element.44), channel_id=1, source_target_pairs={{4,0},{1,4},{5,1},{2,5},{6,2},{3,6},{7,3},{8,7},{12,8},{9,12},{13,... | collective-permute-start | bytes 1585160 | tf_op jit(solution)/shard_map/ppermute | solution.py:27
  78.9 25.5 %collective-permute-start.14 = (s16[129,16,128]{2,1,0:T(8,128)(2,1)}, s16[129,16,128]{2,1,0:T(8,128)(2,1)S(1)}, u32[]{:S(2)}, u32[]{:S(2)}) collective-permute-start(s16[129,16,128]{2,1,0:T(8,128)(2,1)} %get-tuple-element.44), channel_id=1, source_target_pairs={{0,4},{4,1},{1,5},{5,2},{2,6},{6,3},{3,7},{7,8},{8,12},{12,9},{9,1... | collective-permute-start | bytes 1585160 | tf_op jit(solution)/shard_map/ppermute | solution.py:27
  85.9 8.8 %collective-permute-start.7 = (s16[82,16,128]{2,1,0:T(8,128)(2,1)S(1)}, s16[82,16,128]{2,1,0:T(8,128)(2,1)S(1)}, u32[]{:S(2)}, u32[]{:S(2)}) collective-permute-start(s16[82,16,128]{2,1,0:T(8,128)(2,1)S(1)} %copy-done.22), channel_id=1, source_target_pairs={{4,0},{1,4},{5,1},{2,5},{6,2},{3,6},{7,3},{8,7},{12,8},{9,12},{13,... | collective-permute-start | bytes 1007624 | tf_op jit(solution)/shard_map/ppermute | solution.py:27
  87.8 8.0 %collective-permute-start.6 = (s16[82,16,128]{2,1,0:T(8,128)(2,1)S(1)}, s16[82,16,128]{2,1,0:T(8,128)(2,1)S(1)}, u32[]{:S(2)}, u32[]{:S(2)}) collective-permute-start(s16[82,16,128]{2,1,0:T(8,128)(2,1)S(1)} %copy-done.22), channel_id=1, source_target_pairs={{0,4},{4,1},{1,5},{5,2},{2,6},{6,3},{3,7},{7,8},{8,12},{12,9},{9,1... | collective-permute-start | bytes 1007624 | tf_op jit(solution)/shard_map/ppermute | solution.py:27
  104.3 14.0 %copy-start.23 = (s16[82,16,128]{2,1,0:T(8,128)(2,1)S(1)}, s16[82,16,128]{2,1,0:T(8,128)(2,1)}, u32[]{:S(2)}) copy-start(s16[82,16,128]{2,1,0:T(8,128)(2,1)} %get-tuple-element.35) | copy-start | bytes 1007620
  110.2 34.6 %collective-permute-start.16 = (s16[129,16,128]{2,1,0:T(8,128)(2,1)}, s16[129,16,128]{2,1,0:T(8,128)(2,1)S(1)}, u32[]{:S(2)}, u32[]{:S(2)}) collective-permute-start(s16[129,16,128]{2,1,0:T(8,128)(2,1)} %get-tuple-element.46), channel_id=1, source_target_pairs={{0,1},{4,5},{1,2},{5,6},{2,3},{6,7},{3,8},{7,12},{8,9},{12,13},{9,... | collective-permute-start | bytes 1585160 | tf_op jit(solution)/shard_map/ppermute | solution.py:27
  112.7 32.2 %collective-permute-start.17 = (s16[129,16,128]{2,1,0:T(8,128)(2,1)}, s16[129,16,128]{2,1,0:T(8,128)(2,1)S(1)}, u32[]{:S(2)}, u32[]{:S(2)}) collective-permute-start(s16[129,16,128]{2,1,0:T(8,128)(2,1)} %get-tuple-element.47), channel_id=1, source_target_pairs={{1,0},{5,4},{2,1},{6,5},{3,2},{7,6},{8,3},{12,7},{9,8},{13,12},{10... | collective-permute-start | bytes 1585160 | tf_op jit(solution)/shard_map/ppermute | solution.py:27
  114.0 15.3 %collective-permute-start.8 = (s16[82,16,128]{2,1,0:T(8,128)(2,1)S(1)}, s16[82,16,128]{2,1,0:T(8,128)(2,1)S(1)}, u32[]{:S(2)}, u32[]{:S(2)}) collective-permute-start(s16[82,16,128]{2,1,0:T(8,128)(2,1)S(1)} %copy-done.24), channel_id=1, source_target_pairs={{0,1},{4,5},{1,2},{5,6},{2,3},{6,7},{3,8},{7,12},{8,9},{12,13},{9,... | collective-permute-start | bytes 1007624 | tf_op jit(solution)/shard_map/ppermute | solution.py:27
  118.3 15.5 %collective-permute-start.9 = (s16[82,16,128]{2,1,0:T(8,128)(2,1)S(1)}, s16[82,16,128]{2,1,0:T(8,128)(2,1)S(1)}, u32[]{:S(2)}, u32[]{:S(2)}) collective-permute-start(s16[82,16,128]{2,1,0:T(8,128)(2,1)S(1)} %copy-done.23), channel_id=1, source_target_pairs={{1,0},{5,4},{2,1},{6,5},{3,2},{7,6},{8,3},{12,7},{9,8},{13,12},{10... | collective-permute-start | bytes 1007624 | tf_op jit(solution)/shard_map/ppermute | solution.py:27
  144.8 21.9 %copy-start.19 = (s32[2048]{0:T(1024)S(1)}, s32[2048]{0:T(1024)}, u32[]{:S(2)}) copy-start(s32[2048]{0:T(1024)} %param.7) | copy-start | bytes 24580
  145.8 22.3 %copy-start = (bf16[2048,512]{1,0:T(8,128)(2,1)S(1)}, bf16[2048,512]{1,0:T(8,128)(2,1)}, u32[]{:S(2)}) copy-start(bf16[2048,512]{1,0:T(8,128)(2,1)} %observed.3) | copy-start | bytes 6291460
  152.5 15.6 %collective-permute-start.18 = (bf16[512,512]{1,0:T(8,128)(2,1)}, bf16[512,512]{1,0:T(8,128)(2,1)}, u32[]{:S(2)}, u32[]{:S(2)}) collective-permute-start(bf16[512,512]{1,0:T(8,128)(2,1)} %get-tuple-element.48), channel_id=1, source_target_pairs={{0,1},{4,0},{1,3},{5,2},{2,5},{6,4},{3,7},{7,6},{8,9},{12,8},{9,11... | collective-permute-start | bytes 1572872 | tf_op jit(solution)/shard_map/ppermute | solution.py:27
  155.4 17.7 %collective-permute-start.21 = (bf16[512,512]{1,0:T(8,128)(2,1)}, bf16[512,512]{1,0:T(8,128)(2,1)S(1)}, u32[]{:S(2)}, u32[]{:S(2)}) collective-permute-start(bf16[512,512]{1,0:T(8,128)(2,1)} %get-tuple-element.48), channel_id=1, source_target_pairs={{0,3},{4,2},{1,1},{5,0},{2,7},{6,6},{3,5},{7,4},{8,11},{12,10},{9,... | collective-permute-start | bytes 1572872 | tf_op jit(solution)/shard_map/ppermute | solution.py:27
  160.1 25.0 %collective-permute-start.20 = (bf16[512,512]{1,0:T(8,128)(2,1)}, bf16[512,512]{1,0:T(8,128)(2,1)}, u32[]{:S(2)}, u32[]{:S(2)}) collective-permute-start(bf16[512,512]{1,0:T(8,128)(2,1)} %get-tuple-element.48), channel_id=1, source_target_pairs={{0,2},{4,3},{1,0},{5,1},{2,6},{6,7},{3,4},{7,5},{8,10},{12,11},{9,... | collective-permute-start | bytes 1572872 | tf_op jit(solution)/shard_map/ppermute | solution.py:27
  162.5 22.5 %collective-permute-start.19 = (s16[129,16,128]{2,1,0:T(8,128)(2,1)}, s16[129,16,128]{2,1,0:T(8,128)(2,1)S(1)}, u32[]{:S(2)}, u32[]{:S(2)}) collective-permute-start(s16[129,16,128]{2,1,0:T(8,128)(2,1)} %get-tuple-element.49), channel_id=1, source_target_pairs={{0,0},{4,1},{1,2},{5,3},{2,4},{6,5},{3,6},{7,7},{8,8},{12,9},{9,10... | collective-permute-start | bytes 1585160 | tf_op jit(solution)/shard_map/ppermute | solution.py:27
  173.1 12.0 %copy-start.12 = (bf16[512,512]{1,0:T(8,128)(2,1)}, bf16[512,512]{1,0:T(8,128)(2,1)S(1)}, u32[]{:S(2)}) copy-start(bf16[512,512]{1,0:T(8,128)(2,1)S(1)} %collective-permute-done.21.three) | copy-start | bytes 1572868
  (15 other events, 26.1 us)

commit v2 on v1

--- a/solution.py
+++ b/solution.py
@@ -18,7 +18,8 @@
 
 def seat(t):
     line, spot = t // LINE, t % LINE
-    return (2 * line + spot % 2) * SLOTS + spot // 2
+    chip = spot // 2 if line % 2 == 0 else SLOTS - 1 - spot // 2
+    return (2 * line + spot % 2) * SLOTS + chip
 
 
 def carry(value, source_of, target_of):
@@ -277,14 +278,18 @@
             pl.when(i == j)(lambda: out(j).start())
         return 0
 
-    lax.fori_loop(0, len(msgs), one, 0, unroll=2 if plan is MATRIX else 1)
+    lax.fori_loop(0, len(msgs), one, 0)
     for j in range(len(msgs)):
         out(j).wait()
 
 
-def gram_matrix(place, row_interval, design, turned, *rest):
+def gram_first(base, place, row_interval, design, turned, *rest):
     turned[...] = design[...].T
-    each_round(3, place, row_interval, turned, MATRIX, design, rest[:-2], *rest[-2:])
+    each_round(base, place, row_interval, turned, MATRIX, design, rest[:-2], *rest[-2:])
+
+
+def gram_matrix(base, place, row_interval, turned, design, *rest):
+    each_round(base, place, row_interval, turned, MATRIX, design, rest[:-2], *rest[-2:])
 
 
 def gram_side(base, place, row_interval, turned, observed, *rest):
@@ -407,7 +412,8 @@
     row_count, n = design.shape
     count = lax.axis_size(PAIR)
     chain, place = lax.axis_index("chain"), lax.axis_index("arc")
-    time = LINE * (chain // 2) + 2 * place + chain % 2
+    line = chain // 2
+    time = LINE * line + 2 * jnp.where(line % 2 == 0, place, SLOTS - 1 - place) + chain % 2
     square = jax.ShapeDtypeStruct((n, n), F32)
     half = jax.ShapeDtypeStruct((n, n), BF16)
     matrix_msg = jax.ShapeDtypeStruct(MATRIX_MSG, jnp.int16)
@@ -417,9 +423,16 @@
     plain = [pltpu.VMEM((n, n), F32)]
     work = scratch_of(n)
 
-    turned, *parts = gram(
-        gram_matrix, (jax.ShapeDtypeStruct((n, row_count), BF16),), (matrix_msg,) * 4, where, flat, design
-    )
+    turned, *first = gram(
+        functools.partial(gram_first, 3),
+        (jax.ShapeDtypeStruct((n, row_count), BF16),),
+        (matrix_msg,) * 2,
+        where,
+        flat,
+        design,
+    )
+    rest = gram(functools.partial(gram_matrix, 1), (), (matrix_msg,) * 2, where, flat, turned, design)
+    parts = first + list(rest)
     for i, m in enumerate(ROUNDS):
         parts[i] = to_seat(parts[i], m)
     side_parts = []

time: 197 us -> 204 us (1.036)
  the two profiles are of different devices: /device:TPU:1 before, /device:TPU:98 now
where the time goes in v2:
time: 204 us; the launch traced here: 203 us
  Pallas kernels  74.6 us (37%)
  starting transfers between devices  68.7 us (34%)
  waiting for transfers between devices  45.7 us (22%)
  local copies, waits for them, and re-layouts  8.48 us (4%)
  matrix products  4.28 us (2%)
    ppermute x22, starting transfers between devices, carry(): lax.ppermute(value, PAIR, [pair for pair in pairs if pair[1] is not None])  68.7 us
    ppermute x22, waiting for transfers between devices, carry(): lax.ppermute(value, PAIR, [pair for pair in pairs if pair[1] is not None])  45.7 us
    pallas_call x6, Pallas kernels, call(): return pl.pallas_call(kernel, out_shape=outs, scratch_shapes=scratch)(*args)  41.6 us
    pallas_call x4, Pallas kernels, gram(): pl.pallas_call(kernel, out_shape=kept + msgs, in_specs=specs, out_specs=(...  24.4 us
    pallas_call x1, Pallas kernels, step_of(): pl.pallas_call(predict, grid=(SLOTS,), out_shape=(square, jax.ShapeDtypeS...  8.62 us
    unnamed x50, local copies, waits for them, and re-layouts  7.04 us
    dot_general x1, matrix products, step_of(): jnp.dot(picked, states[1], preferred_element_type=F32)  4.28 us
  transfers between devices with their start and end apart: 22, of which 5 were waited for; matrix products, arithmetic and copies ran while one was open for 3% of the time, Pallas kernels for 21%

profile of v2, /device:TPU:98, one launch (start us, length us, event | category | flops | bytes accessed | tf_op | source)
XLA Modules:
  0.0 203.4 jit_solution(9185713243137939671)
XLA Ops:
  0.6 6.9 %shard_map.68 = (bf16[512,2048]{1,0:T(8,128)(2,1)}, s16[82,16,128]{2,1,0:T(8,128)(2,1)}, s16[82,16,128]{2,1,0:T(8,128)(2,1)}) custom-call(s32[1]{0:T(128)} %bitcast.place, s32[1,2048]{1,0:T(1,128)} %bitcast.5, bf16[2048,512]{1,0:T(8,128)(2,1)} %design.5), custom_call_target="tpu_custom_call" | custom-call | tf_op jit(solution)/shard_map/pallas_call | solution.py:399
  7.5 4.5 %collective-permute-start = (s16[82,16,128]{2,1,0:T(8,128)(2,1)}, s16[82,16,128]{2,1,0:T(8,128)(2,1)S(1)}, u32[]{:S(2)}, u32[]{:S(2)}) collective-permute-start(s16[82,16,128]{2,1,0:T(8,128)(2,1)} %get-tuple-element.27), channel_id=1, source_target_pairs={{3,0},{2,4},{1,1},{0,5},{7,2},{6,6},{5,3},{4,7},{11,11},{10,15},{9... | collective-permute-start | bytes 1007624 | tf_op jit(solution)/shard_map/ppermute | solution.py:28
  13.5 5.6 %shard_map.69 = (s16[82,16,128]{2,1,0:T(8,128)(2,1)}, s16[82,16,128]{2,1,0:T(8,128)(2,1)}) custom-call(s32[1]{0:T(128)} %bitcast.place, s32[1,2048]{1,0:T(1,128)} %bitcast.6, bf16[512,2048]{1,0:T(8,128)(2,1)} %get-tuple-element.29.turned, bf16[2048,512]{1,0:T(8,128)(2,1)} %design.5), custom_call_target="tpu_custom_call" | custom-call | tf_op jit(solution)/shard_map/pallas_call | solution.py:399
  19.4 2.5 %collective-permute-start.4 = (f32[2,512]{1,0:T(2,128)S(1)}, f32[2,512]{1,0:T(2,128)S(1)}, u32[]{:S(2)}, u32[]{:S(2)}) collective-permute-start(f32[2,512]{1,0:T(2,128)S(1)} %pad_maximum_fusion), channel_id=1, source_target_pairs={{0,0},{1,4},{2,1},{3,5},{4,2},{5,6},{6,3},{7,7},{8,11},{9,15},{10,... | collective-permute-start | bytes 12296 | tf_op jit(solution)/shard_map/ppermute | solution.py:28
  21.9 4.1 %collective-permute-start.5 = (f32[1,512]{1,0:T(1,128)S(1)}, f32[1,512]{1,0:T(1,128)S(1)}, u32[]{:S(2)}, u32[]{:S(2)}) collective-permute-start(f32[1,512]{1,0:T(1,128)S(1)} %copy-done.21), channel_id=1, source_target_pairs={{0,4},{1,1},{2,5},{3,2},{4,6},{5,3},{6,7},{7,11},{8,15},{9,10},{10... | collective-permute-start | bytes 6152 | tf_op jit(solution)/shard_map/ppermute | solution.py:28
  26.0 5.9 %shard_map.74 = (s16[129,16,128]{2,1,0:T(8,128)(2,1)}, s16[129,16,128]{2,1,0:T(8,128)(2,1)}) custom-call(s32[1]{0:T(128)} %bitcast.place, s32[1,2048]{1,0:T(1,128)} %bitcast.7, bf16[512,2048]{1,0:T(8,128)(2,1)} %get-tuple-element.29.turned, bf16[2048,512]{1,0:T(8,128)(2,1)} %observed.3), custom_call_target="tpu_custom_call" | custom-call | tf_op jit(solution)/shard_map/pallas_call | solution.py:399
  31.9 5.9 %shard_map.73 = (s16[129,16,128]{2,1,0:T(8,128)(2,1)}, s16[129,16,128]{2,1,0:T(8,128)(2,1)}) custom-call(s32[1]{0:T(128)} %bitcast.place, s32[1,2048]{1,0:T(1,128)} %bitcast.8, bf16[512,2048]{1,0:T(8,128)(2,1)} %get-tuple-element.29.turned, bf16[2048,512]{1,0:T(8,128)(2,1)} %observed.3), custom_call_target="tpu_custom_call" | custom-call | tf_op jit(solution)/shard_map/pallas_call | solution.py:399
  37.9 5.4 %collective-permute-start.13 = (s16[129,16,128]{2,1,0:T(8,128)(2,1)}, s16[129,16,128]{2,1,0:T(8,128)(2,1)S(1)}, u32[]{:S(2)}, u32[]{:S(2)}) collective-permute-start(s16[129,16,128]{2,1,0:T(8,128)(2,1)} %get-tuple-element.42), channel_id=1, source_target_pairs={{0,0},{1,4},{2,1},{3,5},{4,2},{5,6},{6,3},{7,7},{8,11},{9,15},{10,... | collective-permute-start | bytes 1585160 | tf_op jit(solution)/shard_map/ppermute | solution.py:28
  43.4 1.9 collective-permute-start.10
  46.4 4.6 %collective-permute-start.3 = (s16[82,16,128]{2,1,0:T(8,128)(2,1)}, s16[82,16,128]{2,1,0:T(8,128)(2,1)S(1)}, u32[]{:S(2)}, u32[]{:S(2)}) collective-permute-start(s16[82,16,128]{2,1,0:T(8,128)(2,1)} %get-tuple-element.31), channel_id=1, source_target_pairs={{0,0},{1,4},{2,1},{3,5},{4,2},{5,6},{6,3},{7,7},{8,11},{9,15},{10,... | collective-permute-start | bytes 1007624 | tf_op jit(solution)/shard_map/ppermute | solution.py:28
  51.7 17.5 %collective-permute-done.3.four = s16[82,16,128]{2,1,0:T(8,128)(2,1)S(1)} collective-permute-done((s16[82,16,128]{2,1,0:T(8,128)(2,1)}, s16[82,16,128]{2,1,0:T(8,128)(2,1)S(1)}, u32[]{:S(2)}, u32[]{:S(2)}) %collective-permute-start.3) | collective-permute-done | bytes 335904 | tf_op jit(solution)/shard_map/ppermute | solution.py:28
  70.0 7.5 %shard_map.70 = (f32[512,512]{1,0:T(8,128)}, f32[512,512]{1,0:T(8,128)}, s16[82,16,128]{2,1,0:T(8,128)(2,1)}) custom-call(s16[82,16,128]{2,1,0:T(8,128)(2,1)} %copy-done.13, s16[82,16,128]{2,1,0:T(8,128)(2,1)} %copy-done.14, s16[82,16,128]{2,1,0:T(8,128)(2,1)} %copy-done.15, s16[82,16,128]{2,1,0:T(8,128)(2,1)} %copy-done.16, f32[8,512]{1,0:T(8,128)} %maximum_maximum_fusion.vec), custom_call_target="tpu_custom_call" | custom-call | tf_op jit(solution)/shard_map/pallas_call | solution.py:393
  78.8 4.5 %shard_map.75 = (f32[512,512]{1,0:T(8,128)}, s16[129,16,128]{2,1,0:T(8,128)(2,1)}) custom-call(f32[512,512]{1,0:T(8,128)} %get-tuple-element.38.x, s16[129,16,128]{2,1,0:T(8,128)(2,1)} %copy-done.6, s16[129,16,128]{2,1,0:T(8,128)(2,1)} %copy-done.7, s16[129,16,128]{2,1,0:T(8,128)(2,1)} %copy-done.4, s16[129,16,128]{2,1,0:T(8,128)(2,1)} %copy-done.5), custom_call_target="tpu_custom_call" | custom-call | tf_op jit(solution)/shard_map/pallas_call | solution.py:393
  85.2 3.1 %collective-permute-start.14 = (s16[129,16,128]{2,1,0:T(8,128)(2,1)}, s16[129,16,128]{2,1,0:T(8,128)(2,1)S(1)}, u32[]{:S(2)}, u32[]{:S(2)}) collective-permute-start(s16[129,16,128]{2,1,0:T(8,128)(2,1)} %get-tuple-element.44), channel_id=1, source_target_pairs={{0,4},{4,1},{1,5},{5,2},{2,6},{6,3},{3,7},{7,11},{11,15},{15,10},{... | collective-permute-start | bytes 1585160 | tf_op jit(solution)/shard_map/ppermute | solution.py:28
  88.3 2.5 %collective-permute-start.7 = (s16[82,16,128]{2,1,0:T(8,128)(2,1)S(1)}, s16[82,16,128]{2,1,0:T(8,128)(2,1)S(1)}, u32[]{:S(2)}, u32[]{:S(2)}) collective-permute-start(s16[82,16,128]{2,1,0:T(8,128)(2,1)S(1)} %copy-done.22), channel_id=1, source_target_pairs={{4,0},{1,4},{5,1},{2,5},{6,2},{3,6},{7,3},{11,7},{15,11},{10,15},{... | collective-permute-start | bytes 1007624 | tf_op jit(solution)/shard_map/ppermute | solution.py:28
  90.8 5.2 %collective-permute-start.6 = (s16[82,16,128]{2,1,0:T(8,128)(2,1)S(1)}, s16[82,16,128]{2,1,0:T(8,128)(2,1)S(1)}, u32[]{:S(2)}, u32[]{:S(2)}) collective-permute-start(s16[82,16,128]{2,1,0:T(8,128)(2,1)S(1)} %copy-done.22), channel_id=1, source_target_pairs={{0,4},{4,1},{1,5},{5,2},{2,6},{6,3},{3,7},{7,11},{11,15},{15,10},{... | collective-permute-start | bytes 1007624 | tf_op jit(solution)/shard_map/ppermute | solution.py:28
  96.0 3.6 %collective-permute-done.6.low = s16[82,16,128]{2,1,0:T(8,128)(2,1)S(1)} collective-permute-done((s16[82,16,128]{2,1,0:T(8,128)(2,1)S(1)}, s16[82,16,128]{2,1,0:T(8,128)(2,1)S(1)}, u32[]{:S(2)}, u32[]{:S(2)}) %collective-permute-start.6) | collective-permute-done | bytes 335904 | tf_op jit(solution)/shard_map/ppermute | solution.py:28
  100.3 7.8 %shard_map.71 = (f32[512,512]{1,0:T(8,128)}, f32[512,512]{1,0:T(8,128)}, s16[82,16,128]{2,1,0:T(8,128)(2,1)}, s16[82,16,128]{2,1,0:T(8,128)(2,1)}) custom-call(f32[512,512]{1,0:T(8,128)} %get-tuple-element.32.b, s16[82,16,128]{2,1,0:T(8,128)(2,1)} %copy-done.2, s16[82,16,128]{2,1,0:T(8,128)(2,1)} %copy-done.1, f32[8,512]{1,0:T(8,128)} %maximum_maximum_fusion.vec), custom_call_target="tpu_custom_call" | custom-call | tf_op jit(solution)/shard_map/pallas_call | solution.py:393
  109.1 4.9 %shard_map.76 = (f32[512,512]{1,0:T(8,128)}, s16[129,16,128]{2,1,0:T(8,128)(2,1)}, s16[129,16,128]{2,1,0:T(8,128)(2,1)}) custom-call(f32[512,512]{1,0:T(8,128)} %get-tuple-element.37.x, f32[512,512]{1,0:T(8,128)} %get-tuple-element.43.f, s16[129,16,128]{2,1,0:T(8,128)(2,1)} %copy-done.9, s16[129,16,128]{2,1,0:T(8,128)(2,1)} %copy-done.8, ...), custom_call_target="tpu_custom_call" | custom-call | tf_op jit(solution)/shard_map/pallas_call | solution.py:393
  114.0 10.7 %collective-permute-start.16 = (s16[129,16,128]{2,1,0:T(8,128)(2,1)}, s16[129,16,128]{2,1,0:T(8,128)(2,1)S(1)}, u32[]{:S(2)}, u32[]{:S(2)}) collective-permute-start(s16[129,16,128]{2,1,0:T(8,128)(2,1)} %get-tuple-element.46), channel_id=1, source_target_pairs={{0,1},{4,5},{1,2},{5,6},{2,3},{6,7},{3,11},{7,15},{11,10},{15,14},... | collective-permute-start | bytes 1585160 | tf_op jit(solution)/shard_map/ppermute | solution.py:28
  124.7 1.9 collective-permute-start.17
  126.6 6.0 %collective-permute-start.8 = (s16[82,16,128]{2,1,0:T(8,128)(2,1)S(1)}, s16[82,16,128]{2,1,0:T(8,128)(2,1)S(1)}, u32[]{:S(2)}, u32[]{:S(2)}) collective-permute-start(s16[82,16,128]{2,1,0:T(8,128)(2,1)S(1)} %copy-done.24), channel_id=1, source_target_pairs={{0,1},{4,5},{1,2},{5,6},{2,3},{6,7},{3,11},{7,15},{11,10},{15,14},... | collective-permute-start | bytes 1007624 | tf_op jit(solution)/shard_map/ppermute | solution.py:28
  132.7 2.1 %collective-permute-start.9 = (s16[82,16,128]{2,1,0:T(8,128)(2,1)S(1)}, s16[82,16,128]{2,1,0:T(8,128)(2,1)S(1)}, u32[]{:S(2)}, u32[]{:S(2)}) collective-permute-start(s16[82,16,128]{2,1,0:T(8,128)(2,1)S(1)} %copy-done.23), channel_id=1, source_target_pairs={{1,0},{5,4},{2,1},{6,5},{3,2},{7,6},{11,3},{15,7},{10,11},{14,15},... | collective-permute-start | bytes 1007624 | tf_op jit(solution)/shard_map/ppermute | solution.py:28
  134.8 4.5 %collective-permute-done.8.far_low = s16[82,16,128]{2,1,0:T(8,128)(2,1)S(1)} collective-permute-done((s16[82,16,128]{2,1,0:T(8,128)(2,1)S(1)}, s16[82,16,128]{2,1,0:T(8,128)(2,1)S(1)}, u32[]{:S(2)}, u32[]{:S(2)}) %collective-permute-start.8) | collective-permute-done | bytes 335904 | tf_op jit(solution)/shard_map/ppermute | solution.py:28
  139.3 6.2 %collective-permute-done.9.far_high = s16[82,16,128]{2,1,0:T(8,128)(2,1)S(1)} collective-permute-done((s16[82,16,128]{2,1,0:T(8,128)(2,1)S(1)}, s16[82,16,128]{2,1,0:T(8,128)(2,1)S(1)}, u32[]{:S(2)}, u32[]{:S(2)}) %collective-permute-start.9) | collective-permute-done | bytes 335904 | tf_op jit(solution)/shard_map/ppermute | solution.py:28
  146.3 10.3 %shard_map.72.x = f32[512,512]{1,0:T(8,128)} custom-call(f32[512,512]{1,0:T(8,128)} %get-tuple-element.34.b, s16[82,16,128]{2,1,0:T(8,128)(2,1)} %copy-done.2, s16[82,16,128]{2,1,0:T(8,128)(2,1)} %copy-done.1, s16[82,16,128]{2,1,0:T(8,128)(2,1)} %copy-done.17, s16[82,16,128]{2,1,0:T(8,128)(2,1)} %copy-done.18, f32[8,512]{1,0:T(8,128)} %maximum_maximum_fusion.vec), custom_call_target="tpu_custom_call" | custom-call | tf_op jit(solution)/shard_map/pallas_call | solution.py:393
  157.6 6.7 %shard_map.77 = (s16[129,16,128]{2,1,0:T(8,128)(2,1)}, bf16[512,512]{1,0:T(8,128)(2,1)}) custom-call(f32[512,512]{1,0:T(8,128)} %shard_map.72.x, f32[512,512]{1,0:T(8,128)} %get-tuple-element.45.f, s16[82,16,128]{2,1,0:T(8,128)(2,1)} %copy-done.2, s16[82,16,128]{2,1,0:T(8,128)(2,1)} %copy-done.1, s16[129,16,128]{2,1,0:T(8,128)(2,1)} %copy-done.10, ...), custom_call_target="tpu_custom_call" | custom-call | tf_op jit(solution)/shard_map/pallas_call | solution.py:393
  164.2 1.9 collective-permute-start.21
  166.2 7.5 %collective-permute-start.19 = (s16[129,16,128]{2,1,0:T(8,128)(2,1)}, s16[129,16,128]{2,1,0:T(8,128)(2,1)S(1)}, u32[]{:S(2)}, u32[]{:S(2)}) collective-permute-start(s16[129,16,128]{2,1,0:T(8,128)(2,1)} %get-tuple-element.49), channel_id=1, source_target_pairs={{0,0},{4,1},{1,2},{5,3},{2,4},{6,5},{3,6},{7,7},{11,8},{15,9},{10,... | collective-permute-start | bytes 1585160 | tf_op jit(solution)/shard_map/ppermute | solution.py:28
  175.1 13.8 %collective-permute-done.18 = bf16[512,512]{1,0:T(8,128)(2,1)} collective-permute-done((bf16[512,512]{1,0:T(8,128)(2,1)}, bf16[512,512]{1,0:T(8,128)(2,1)}, u32[]{:S(2)}, u32[]{:S(2)}) %collective-permute-start.18) | collective-permute-done | bytes 524320 | tf_op jit(solution)/shard_map/ppermute | solution.py:28
  188.9 4.3 %convert_subtract_fusion.partial = f32[2048,512]{1,0:T(8,128)} fusion(bf16[2048,512]{1,0:T(8,128)(2,1)} %observed.3, bf16[512,512]{1,0:T(8,128)(2,1)} %collective-permute-done.18, bf16[2048,512]{1,0:T(8,128)(2,1)S(1)} %copy-done, pred[2048]{0:T(1024)(128)(4,1)S(1)} %broadcast_compare_fusion), kind=kOutput, calls=%fused_computation | convolution fusion | flops 1076887552 | bytes 8914944 | tf_op jit(solution)/shard_map/dot_general | solution.py:468
  194.8 8.6 %shard_map.78 = (f32[512,512]{1,0:T(8,128)}, f32[2048,512]{1,0:T(8,128)}) custom-call(s32[1]{0:T(128)} %bitcast.place, s32[2048,1]{1,0:T(8,128)} %copy.7.column, bf16[2048,512]{1,0:T(8,128)(2,1)} %design.5, f32[2048,512]{1,0:T(8,128)} %convert_subtract_fusion.partial, s16[129,16,128]{2,1,0:T(8,128)(2,1)} %copy-done.3, ...), custom_call_target="tpu_custom_call" | custom-call | tf_op jit(solution)/shard_map/pallas_call | solution.py:472
  (81 shorter events, 13.9 us)
Async XLA Ops:
  7.5 35.8 %collective-permute-start = (s16[82,16,128]{2,1,0:T(8,128)(2,1)}, s16[82,16,128]{2,1,0:T(8,128)(2,1)S(1)}, u32[]{:S(2)}, u32[]{:S(2)}) collective-permute-start(s16[82,16,128]{2,1,0:T(8,128)(2,1)} %get-tuple-element.27), channel_id=1, source_target_pairs={{3,0},{2,4},{1,1},{0,5},{7,2},{6,6},{5,3},{4,7},{11,11},{10,15},{9... | collective-permute-start | bytes 1007624 | tf_op jit(solution)/shard_map/ppermute | solution.py:28
  12.1 33.2 %collective-permute-start.1 = (s16[82,16,128]{2,1,0:T(8,128)(2,1)}, s16[82,16,128]{2,1,0:T(8,128)(2,1)S(1)}, u32[]{:S(2)}, u32[]{:S(2)}) collective-permute-start(s16[82,16,128]{2,1,0:T(8,128)(2,1)} %get-tuple-element.28), channel_id=1, source_target_pairs={{2,0},{3,4},{0,1},{1,5},{6,2},{7,6},{4,3},{5,7},{10,11},{11,15},{8... | collective-permute-start | bytes 1007624 | tf_op jit(solution)/shard_map/ppermute | solution.py:28
  13.5 5.9 %copy-start.21 = (f32[1,512]{1,0:T(1,128)S(1)}, f32[1,512]{1,0:T(1,128)}, u32[]{:S(2)}) copy-start(f32[1,512]{1,0:T(1,128)} %param.9) | copy-start | bytes 6148
  19.1 27.3 %collective-permute-start.2 = (s16[82,16,128]{2,1,0:T(8,128)(2,1)}, s16[82,16,128]{2,1,0:T(8,128)(2,1)S(1)}, u32[]{:S(2)}, u32[]{:S(2)}) collective-permute-start(s16[82,16,128]{2,1,0:T(8,128)(2,1)} %get-tuple-element.30), channel_id=1, source_target_pairs={{1,0},{0,4},{3,1},{2,5},{5,2},{4,6},{7,3},{6,7},{9,11},{8,15},{11,... | collective-permute-start | bytes 1007624 | tf_op jit(solution)/shard_map/ppermute | solution.py:28
  19.4 18.6 %collective-permute-start.4 = (f32[2,512]{1,0:T(2,128)S(1)}, f32[2,512]{1,0:T(2,128)S(1)}, u32[]{:S(2)}, u32[]{:S(2)}) collective-permute-start(f32[2,512]{1,0:T(2,128)S(1)} %pad_maximum_fusion), channel_id=1, source_target_pairs={{0,0},{1,4},{2,1},{3,5},{4,2},{5,6},{6,3},{7,7},{8,11},{9,15},{10,... | collective-permute-start | bytes 12296 | tf_op jit(solution)/shard_map/ppermute | solution.py:28
  21.9 16.0 %collective-permute-start.5 = (f32[1,512]{1,0:T(1,128)S(1)}, f32[1,512]{1,0:T(1,128)S(1)}, u32[]{:S(2)}, u32[]{:S(2)}) collective-permute-start(f32[1,512]{1,0:T(1,128)S(1)} %copy-done.21), channel_id=1, source_target_pairs={{0,4},{1,1},{2,5},{3,2},{4,6},{5,3},{6,7},{7,11},{8,15},{9,10},{10... | collective-permute-start | bytes 6152 | tf_op jit(solution)/shard_map/ppermute | solution.py:28
  37.9 39.6 %collective-permute-start.12 = (s16[129,16,128]{2,1,0:T(8,128)(2,1)}, s16[129,16,128]{2,1,0:T(8,128)(2,1)S(1)}, u32[]{:S(2)}, u32[]{:S(2)}) collective-permute-start(s16[129,16,128]{2,1,0:T(8,128)(2,1)} %get-tuple-element.41), channel_id=1, source_target_pairs={{1,0},{0,4},{3,1},{2,5},{5,2},{4,6},{7,3},{6,7},{9,11},{8,15},{11,... | collective-permute-start | bytes 1585160 | tf_op jit(solution)/shard_map/ppermute | solution.py:28
  37.9 39.5 %collective-permute-start.13 = (s16[129,16,128]{2,1,0:T(8,128)(2,1)}, s16[129,16,128]{2,1,0:T(8,128)(2,1)S(1)}, u32[]{:S(2)}, u32[]{:S(2)}) collective-permute-start(s16[129,16,128]{2,1,0:T(8,128)(2,1)} %get-tuple-element.42), channel_id=1, source_target_pairs={{0,0},{1,4},{2,1},{3,5},{4,2},{5,6},{6,3},{7,7},{8,11},{9,15},{10,... | collective-permute-start | bytes 1585160 | tf_op jit(solution)/shard_map/ppermute | solution.py:28
  43.4 25.8 %copy-start.13 = (s16[82,16,128]{2,1,0:T(8,128)(2,1)}, s16[82,16,128]{2,1,0:T(8,128)(2,1)S(1)}, u32[]{:S(2)}) copy-start(s16[82,16,128]{2,1,0:T(8,128)(2,1)S(1)} %collective-permute-done.one) | copy-start | bytes 1007620
  43.4 34.1 %collective-permute-start.10 = (s16[129,16,128]{2,1,0:T(8,128)(2,1)}, s16[129,16,128]{2,1,0:T(8,128)(2,1)S(1)}, u32[]{:S(2)}, u32[]{:S(2)}) collective-permute-start(s16[129,16,128]{2,1,0:T(8,128)(2,1)} %get-tuple-element.39), channel_id=1, source_target_pairs={{3,0},{2,4},{1,1},{0,5},{7,2},{6,6},{5,3},{4,7},{11,11},{10,15},{9... | collective-permute-start | bytes 1585160 | tf_op jit(solution)/shard_map/ppermute | solution.py:28
  45.3 23.9 %copy-start.14 = (s16[82,16,128]{2,1,0:T(8,128)(2,1)}, s16[82,16,128]{2,1,0:T(8,128)(2,1)S(1)}, u32[]{:S(2)}) copy-start(s16[82,16,128]{2,1,0:T(8,128)(2,1)S(1)} %collective-permute-done.1.two) | copy-start | bytes 1007620
  45.4 32.1 %collective-permute-start.11 = (s16[129,16,128]{2,1,0:T(8,128)(2,1)}, s16[129,16,128]{2,1,0:T(8,128)(2,1)S(1)}, u32[]{:S(2)}, u32[]{:S(2)}) collective-permute-start(s16[129,16,128]{2,1,0:T(8,128)(2,1)} %get-tuple-element.40), channel_id=1, source_target_pairs={{2,0},{3,4},{0,1},{1,5},{6,2},{7,6},{4,3},{5,7},{10,11},{11,15},{8... | collective-permute-start | bytes 1585160 | tf_op jit(solution)/shard_map/ppermute | solution.py:28
  46.4 22.8 %copy-start.15 = (s16[82,16,128]{2,1,0:T(8,128)(2,1)}, s16[82,16,128]{2,1,0:T(8,128)(2,1)S(1)}, u32[]{:S(2)}) copy-start(s16[82,16,128]{2,1,0:T(8,128)(2,1)S(1)} %collective-permute-done.2.three) | copy-start | bytes 1007620
  46.4 22.8 %collective-permute-start.3 = (s16[82,16,128]{2,1,0:T(8,128)(2,1)}, s16[82,16,128]{2,1,0:T(8,128)(2,1)S(1)}, u32[]{:S(2)}, u32[]{:S(2)}) collective-permute-start(s16[82,16,128]{2,1,0:T(8,128)(2,1)} %get-tuple-element.31), channel_id=1, source_target_pairs={{0,0},{1,4},{2,1},{3,5},{4,2},{5,6},{6,3},{7,7},{8,11},{9,15},{10,... | collective-permute-start | bytes 1007624 | tf_op jit(solution)/shard_map/ppermute | solution.py:28
  77.4 10.8 %copy-start.22 = (s16[82,16,128]{2,1,0:T(8,128)(2,1)S(1)}, s16[82,16,128]{2,1,0:T(8,128)(2,1)}, u32[]{:S(2)}) copy-start(s16[82,16,128]{2,1,0:T(8,128)(2,1)} %get-tuple-element.33) | copy-start | bytes 1007620
  83.3 24.8 %collective-permute-start.15 = (s16[129,16,128]{2,1,0:T(8,128)(2,1)}, s16[129,16,128]{2,1,0:T(8,128)(2,1)S(1)}, u32[]{:S(2)}, u32[]{:S(2)}) collective-permute-start(s16[129,16,128]{2,1,0:T(8,128)(2,1)} %get-tuple-element.44), channel_id=1, source_target_pairs={{4,0},{1,4},{5,1},{2,5},{6,2},{3,6},{7,3},{11,7},{15,11},{10,15},{... | collective-permute-start | bytes 1585160 | tf_op jit(solution)/shard_map/ppermute | solution.py:28
  85.2 22.9 %collective-permute-start.14 = (s16[129,16,128]{2,1,0:T(8,128)(2,1)}, s16[129,16,128]{2,1,0:T(8,128)(2,1)S(1)}, u32[]{:S(2)}, u32[]{:S(2)}) collective-permute-start(s16[129,16,128]{2,1,0:T(8,128)(2,1)} %get-tuple-element.44), channel_id=1, source_target_pairs={{0,4},{4,1},{1,5},{5,2},{2,6},{6,3},{3,7},{7,11},{11,15},{15,10},{... | collective-permute-start | bytes 1585160 | tf_op jit(solution)/shard_map/ppermute | solution.py:28
  88.3 7.7 %collective-permute-start.7 = (s16[82,16,128]{2,1,0:T(8,128)(2,1)S(1)}, s16[82,16,128]{2,1,0:T(8,128)(2,1)S(1)}, u32[]{:S(2)}, u32[]{:S(2)}) collective-permute-start(s16[82,16,128]{2,1,0:T(8,128)(2,1)S(1)} %copy-done.22), channel_id=1, source_target_pairs={{4,0},{1,4},{5,1},{2,5},{6,2},{3,6},{7,3},{11,7},{15,11},{10,15},{... | collective-permute-start | bytes 1007624 | tf_op jit(solution)/shard_map/ppermute | solution.py:28
  90.8 8.8 %collective-permute-start.6 = (s16[82,16,128]{2,1,0:T(8,128)(2,1)S(1)}, s16[82,16,128]{2,1,0:T(8,128)(2,1)S(1)}, u32[]{:S(2)}, u32[]{:S(2)}) collective-permute-start(s16[82,16,128]{2,1,0:T(8,128)(2,1)S(1)} %copy-done.22), channel_id=1, source_target_pairs={{0,4},{4,1},{1,5},{5,2},{2,6},{6,3},{3,7},{7,11},{11,15},{15,10},{... | collective-permute-start | bytes 1007624 | tf_op jit(solution)/shard_map/ppermute | solution.py:28
  108.1 18.5 %copy-start.24 = (s16[82,16,128]{2,1,0:T(8,128)(2,1)S(1)}, s16[82,16,128]{2,1,0:T(8,128)(2,1)}, u32[]{:S(2)}) copy-start(s16[82,16,128]{2,1,0:T(8,128)(2,1)} %get-tuple-element.35) | copy-start | bytes 1007620
  108.1 24.6 %copy-start.23 = (s16[82,16,128]{2,1,0:T(8,128)(2,1)S(1)}, s16[82,16,128]{2,1,0:T(8,128)(2,1)}, u32[]{:S(2)}) copy-start(s16[82,16,128]{2,1,0:T(8,128)(2,1)} %get-tuple-element.36) | copy-start | bytes 1007620
  114.0 42.6 %collective-permute-start.16 = (s16[129,16,128]{2,1,0:T(8,128)(2,1)}, s16[129,16,128]{2,1,0:T(8,128)(2,1)S(1)}, u32[]{:S(2)}, u32[]{:S(2)}) collective-permute-start(s16[129,16,128]{2,1,0:T(8,128)(2,1)} %get-tuple-element.46), channel_id=1, source_target_pairs={{0,1},{4,5},{1,2},{5,6},{2,3},{6,7},{3,11},{7,15},{11,10},{15,14},... | collective-permute-start | bytes 1585160 | tf_op jit(solution)/shard_map/ppermute | solution.py:28
  124.7 31.9 %collective-permute-start.17 = (s16[129,16,128]{2,1,0:T(8,128)(2,1)}, s16[129,16,128]{2,1,0:T(8,128)(2,1)S(1)}, u32[]{:S(2)}, u32[]{:S(2)}) collective-permute-start(s16[129,16,128]{2,1,0:T(8,128)(2,1)} %get-tuple-element.47), channel_id=1, source_target_pairs={{1,0},{5,4},{2,1},{6,5},{3,2},{7,6},{11,3},{15,7},{10,11},{14,15},... | collective-permute-start | bytes 1585160 | tf_op jit(solution)/shard_map/ppermute | solution.py:28
  126.6 12.7 %collective-permute-start.8 = (s16[82,16,128]{2,1,0:T(8,128)(2,1)S(1)}, s16[82,16,128]{2,1,0:T(8,128)(2,1)S(1)}, u32[]{:S(2)}, u32[]{:S(2)}) collective-permute-start(s16[82,16,128]{2,1,0:T(8,128)(2,1)S(1)} %copy-done.24), channel_id=1, source_target_pairs={{0,1},{4,5},{1,2},{5,6},{2,3},{6,7},{3,11},{7,15},{11,10},{15,14},... | collective-permute-start | bytes 1007624 | tf_op jit(solution)/shard_map/ppermute | solution.py:28
  132.7 12.9 %collective-permute-start.9 = (s16[82,16,128]{2,1,0:T(8,128)(2,1)S(1)}, s16[82,16,128]{2,1,0:T(8,128)(2,1)S(1)}, u32[]{:S(2)}, u32[]{:S(2)}) collective-permute-start(s16[82,16,128]{2,1,0:T(8,128)(2,1)S(1)} %copy-done.23), channel_id=1, source_target_pairs={{1,0},{5,4},{2,1},{6,5},{3,2},{7,6},{11,3},{15,7},{10,11},{14,15},... | collective-permute-start | bytes 1007624 | tf_op jit(solution)/shard_map/ppermute | solution.py:28
  139.3 6.2 %copy-start.17 = (s16[82,16,128]{2,1,0:T(8,128)(2,1)}, s16[82,16,128]{2,1,0:T(8,128)(2,1)S(1)}, u32[]{:S(2)}) copy-start(s16[82,16,128]{2,1,0:T(8,128)(2,1)S(1)} %collective-permute-done.8.far_low) | copy-start | bytes 1007620
  156.6 17.1 %copy-start.19 = (s32[2048]{0:T(1024)S(1)}, s32[2048]{0:T(1024)}, u32[]{:S(2)}) copy-start(s32[2048]{0:T(1024)} %param.7) | copy-start | bytes 24580
  157.6 31.4 %copy-start = (bf16[2048,512]{1,0:T(8,128)(2,1)S(1)}, bf16[2048,512]{1,0:T(8,128)(2,1)}, u32[]{:S(2)}) copy-start(bf16[2048,512]{1,0:T(8,128)(2,1)} %design.5) | copy-start | bytes 6291460
  164.2 24.7 %collective-permute-start.18 = (bf16[512,512]{1,0:T(8,128)(2,1)}, bf16[512,512]{1,0:T(8,128)(2,1)}, u32[]{:S(2)}, u32[]{:S(2)}) collective-permute-start(bf16[512,512]{1,0:T(8,128)(2,1)} %get-tuple-element.48), channel_id=1, source_target_pairs={{0,1},{4,0},{1,3},{5,2},{2,5},{6,4},{3,7},{7,6},{11,9},{15,8},{10,... | collective-permute-start | bytes 1572872 | tf_op jit(solution)/shard_map/ppermute | solution.py:28
  164.2 29.0 %collective-permute-start.21 = (bf16[512,512]{1,0:T(8,128)(2,1)}, bf16[512,512]{1,0:T(8,128)(2,1)S(1)}, u32[]{:S(2)}, u32[]{:S(2)}) collective-permute-start(bf16[512,512]{1,0:T(8,128)(2,1)} %get-tuple-element.48), channel_id=1, source_target_pairs={{0,3},{4,2},{1,1},{5,0},{2,7},{6,6},{3,5},{7,4},{11,11},{15,10},{1... | collective-permute-start | bytes 1572872 | tf_op jit(solution)/shard_map/ppermute | solution.py:28
  166.1 27.1 %collective-permute-start.20 = (bf16[512,512]{1,0:T(8,128)(2,1)}, bf16[512,512]{1,0:T(8,128)(2,1)}, u32[]{:S(2)}, u32[]{:S(2)}) collective-permute-start(bf16[512,512]{1,0:T(8,128)(2,1)} %get-tuple-element.48), channel_id=1, source_target_pairs={{0,2},{4,3},{1,0},{5,1},{2,6},{6,7},{3,4},{7,5},{11,10},{15,11},{1... | collective-permute-start | bytes 1572872 | tf_op jit(solution)/shard_map/ppermute | solution.py:28
  166.2 27.0 %collective-permute-start.19 = (s16[129,16,128]{2,1,0:T(8,128)(2,1)}, s16[129,16,128]{2,1,0:T(8,128)(2,1)S(1)}, u32[]{:S(2)}, u32[]{:S(2)}) collective-permute-start(s16[129,16,128]{2,1,0:T(8,128)(2,1)} %get-tuple-element.49), channel_id=1, source_target_pairs={{0,0},{4,1},{1,2},{5,3},{2,4},{6,5},{3,6},{7,7},{11,8},{15,9},{10,... | collective-permute-start | bytes 1585160 | tf_op jit(solution)/shard_map/ppermute | solution.py:28
  (15 other events, 21.0 us)

commit v3 on v1

--- a/solution.py
+++ b/solution.py
@@ -18,7 +18,8 @@
 
 def seat(t):
     line, spot = t // LINE, t % LINE
-    return (2 * line + spot % 2) * SLOTS + spot // 2
+    chip = spot // 2 if line % 2 == 0 else SLOTS - 1 - spot // 2
+    return (2 * line + spot % 2) * SLOTS + chip
 
 
 def carry(value, source_of, target_of):
@@ -142,13 +143,12 @@
             q_rows[...] = slots[first, row, :]
             sign = (2 * first - 1).astype(F32)
 
-            def add(k, _):
-                slots[2 - first, row, :] += sign * dot_full(
-                    q_rows[:, rows_of(k, STEP)], slots[1 + first, rows_of(k, STEP), :]
-                )
+            def add(number, _):
+                k, j = rows_of(number // (n // STEP), STEP), rows_of(number % (n // STEP), STEP)
+                slots[2 - first, row, j] += sign * dot_full(q_rows[:, k], slots[1 + first, k, j])
                 return 0
 
-            lax.fori_loop(0, n // STEP, add, 0)
+            lax.fori_loop(0, (n // STEP) ** 2, add, 0)
             return total + jnp.where(first == 0, jnp.sum(slots[2, row, :] * slots[2, row, :]), 0.0)
 
         lax.while_loop(
@@ -167,7 +167,7 @@
 
 
 STEP = 128
-PART = 64
+PART = 32
 GRAIN = 1.0 / 128.0
 FULL = 32767.0
 FINE = 4194304.0
@@ -277,14 +277,16 @@
             pl.when(i == j)(lambda: out(j).start())
         return 0
 
-    lax.fori_loop(0, len(msgs), one, 0, unroll=2 if plan is MATRIX else 1)
+    lax.fori_loop(0, len(msgs), one, 0)
     for j in range(len(msgs)):
         out(j).wait()
 
 
-def gram_matrix(place, row_interval, design, turned, *rest):
+def gram_matrix(place, row_interval, design, turned, *msgs):
     turned[...] = design[...].T
-    each_round(3, place, row_interval, turned, MATRIX, design, rest[:-2], *rest[-2:])
+    for m, msg in zip(ROUNDS, msgs):
+        left = masked(place[0] ^ m, row_interval, turned)
+        encode(msg, MATRIX, lambda row, width: dot1(left[row : row + STEP, :], design[:, 0:width]))
 
 
 def gram_side(base, place, row_interval, turned, observed, *rest):
@@ -365,37 +367,38 @@
     out16[...] = t_ref[...].astype(BF16)
 
 
-def predict(place, column, design, partial, code, two, three, out, residual, x_ref):
+def predict(place, column, design, observed, code, one, two, three, out, residual, x_ref):
     n = out.shape[0]
 
     @pl.when(pl.program_id(0) == 0)
     def _():
         unpack((code,), SIDE, out)
         x_ref[0:n, :] = out[...].astype(BF16)
-        x_ref[n : 2 * n, :] = two[...]
-        x_ref[2 * n : 3 * n, :] = three[...]
+        x_ref[n : 2 * n, :] = one[...]
+        x_ref[2 * n : 3 * n, :] = two[...]
+        x_ref[3 * n : 4 * n, :] = three[...]
 
     d = design[...]
     picked = []
-    for m in (0, 2, 3):
+    for m in range(SLOTS):
         pick = jnp.where(column[...] == (place[0] ^ m), 1.0, 0.0)
         pick = jnp.broadcast_to(pick, (d.shape[0], STEP)).astype(BF16)
         picked.append(d * jnp.concatenate([pick] * (n // STEP), axis=1))
-    residual[...] = partial[...] - dot1(jnp.concatenate(picked, axis=1), x_ref[...])
+    residual[...] = observed[...].astype(F32) - dot1(jnp.concatenate(picked, axis=1), x_ref[...])
 
 
 def call(kernel, outs, scratch, *args):
     return pl.pallas_call(kernel, out_shape=outs, scratch_shapes=scratch)(*args)
 
 
-def gram(kernel, kept, msgs, place, *args):
+def gram(kernel, msgs, place, *args):
     space = pl.BlockSpec(memory_space=pltpu.VMEM)
     specs = [pl.BlockSpec(memory_space=pltpu.SMEM)] + [space] * len(args)
     return pl.pallas_call(
         kernel,
-        out_shape=kept + msgs,
+        out_shape=msgs,
         in_specs=specs,
-        out_specs=(space,) * len(kept) + (pl.BlockSpec(memory_space=pl.ANY),) * len(msgs),
+        out_specs=(pl.BlockSpec(memory_space=pl.ANY),) * len(msgs),
         scratch_shapes=[
             pltpu.VMEM((len(msgs),) + msgs[0].shape, jnp.int16),
             pltpu.SemaphoreType.DMA((len(msgs),)),
@@ -407,7 +410,8 @@
     row_count, n = design.shape
     count = lax.axis_size(PAIR)
     chain, place = lax.axis_index("chain"), lax.axis_index("arc")
-    time = LINE * (chain // 2) + 2 * place + chain % 2
+    line = chain // 2
+    time = LINE * line + 2 * jnp.where(line % 2 == 0, place, SLOTS - 1 - place) + chain % 2
     square = jax.ShapeDtypeStruct((n, n), F32)
     half = jax.ShapeDtypeStruct((n, n), BF16)
     matrix_msg = jax.ShapeDtypeStruct(MATRIX_MSG, jnp.int16)
@@ -417,15 +421,18 @@
     plain = [pltpu.VMEM((n, n), F32)]
     work = scratch_of(n)
 
-    turned, *parts = gram(
-        gram_matrix, (jax.ShapeDtypeStruct((n, row_count), BF16),), (matrix_msg,) * 4, where, flat, design
-    )
+    space = pl.BlockSpec(memory_space=pltpu.VMEM)
+    turned, *parts = pl.pallas_call(
+        gram_matrix,
+        out_shape=(jax.ShapeDtypeStruct((n, row_count), BF16),) + (matrix_msg,) * SLOTS,
+        in_specs=[pl.BlockSpec(memory_space=pltpu.SMEM), space, space],
+    )(where, flat, design)
     for i, m in enumerate(ROUNDS):
         parts[i] = to_seat(parts[i], m)
     side_parts = []
     for i in (0, 2):
         rounds = ROUNDS[i : i + 2]
-        msgs = gram(functools.partial(gram_side, 3 - i), (), (side_msg,) * 2, where, flat, turned, observed)
+        msgs = gram(functools.partial(gram_side, 3 - i), (side_msg,) * 2, where, flat, turned, observed)
         for j, m in enumerate(rounds):
             side_parts.append(to_seat(msgs[j], m))
     mine = carry(jnp.concatenate([prior_ridge, coupling], axis=0), home, seat)
@@ -451,8 +458,6 @@
     states = []
     for m in range(SLOTS):
         states.append(to_arc(rounded if m else code, m))
-    picked = jnp.where((row_interval == (place ^ 1))[:, None], design, jnp.zeros((), design.dtype))
-    partial = observed.astype(F32) - jnp.dot(picked, states[1], preferred_element_type=F32)
     chunk = row_count // SLOTS
     whole = pl.BlockSpec(memory_space=pltpu.VMEM)
     rows = lambda width: pl.BlockSpec((chunk, width), lambda i: (i, 0))
@@ -460,10 +465,10 @@
         predict,
         grid=(SLOTS,),
         out_shape=(square, jax.ShapeDtypeStruct((row_count, n), F32)),
-        in_specs=[pl.BlockSpec(memory_space=pltpu.SMEM), rows(1), rows(n), rows(n), whole, whole, whole],
+        in_specs=[pl.BlockSpec(memory_space=pltpu.SMEM), rows(1), rows(n), rows(n)] + [whole] * SLOTS,
         out_specs=(pl.BlockSpec((n, n), lambda i: (0, 0)), rows(n)),
-        scratch_shapes=[pltpu.VMEM((3 * n, n), BF16)],
-    )(where, row_interval.reshape(row_count, 1), design, partial, states[0], states[2], states[3])
+        scratch_shapes=[pltpu.VMEM((SLOTS * n, n), BF16)],
+    )(where, row_interval.reshape(row_count, 1), design, observed, *states)
     return (solution[None], residual)
 
 

time: 197 us -> 204 us (1.036)
  waiting for transfers between devices: 45.2 us -> 59.6 us
  matrix products: 4.99 us -> 0 us
  starting transfers between devices: 63.8 us -> 61.6 us
    ppermute x22, waiting for transfers between devices: 45.2 us -> 59.6 us  [carry(): lax.ppermute(value, PAIR, [pair for pair in pairs if pair[1] is not None])]
    dot_general x1 -> x0, matrix products: 4.99 us -> none  [step_of(): jnp.dot(picked, states[1], preferred_element_type=F32)]
    pallas_call x3, Pallas kernels: 20.8 us -> 18.3 us  [the longest x2 11.9 us: gram(): pl.pallas_call(kernel, out_shape=msgs, in_specs=specs, out_specs=(pl.Bloc...]
    ppermute x22, starting transfers between devices: 63.8 us -> 61.6 us  [carry(): lax.ppermute(value, PAIR, [pair for pair in pairs if pair[1] is not None])]
    unnamed x50 -> x52, local copies, waits for them, and re-layouts: 6.27 us -> 7.2 us
  transfers between devices with their start and end apart: 22 -> 22, of which waited for: 6 -> 7; matrix products, arithmetic and copies ran while one was open for 4% -> 1% of each run, Pallas kernels for 19% -> 19%
where the time goes in v3:
time: 204 us; the launch traced here: 201 us
  Pallas kernels  69.1 us (34%)
  starting transfers between devices  61.6 us (30%)
  waiting for transfers between devices  59.6 us (29%)
  local copies, waits for them, and re-layouts  8.67 us (4%)
    ppermute x22, starting transfers between devices, carry(): lax.ppermute(value, PAIR, [pair for pair in pairs if pair[1] is not None])  61.6 us
    ppermute x22, waiting for transfers between devices, carry(): lax.ppermute(value, PAIR, [pair for pair in pairs if pair[1] is not None])  59.6 us
    pallas_call x6, Pallas kernels, call(): return pl.pallas_call(kernel, out_shape=outs, scratch_shapes=scratch)(*args)  41.5 us
    pallas_call x2, Pallas kernels, gram(): pl.pallas_call(kernel, out_shape=msgs, in_specs=specs, out_specs=(pl.Bloc...  11.9 us
    pallas_call x1, Pallas kernels, step_of(): pl.pallas_call(predict, grid=(SLOTS,), out_shape=(square, jax.ShapeDtypeS...  9.34 us
    unnamed x52, local copies, waits for them, and re-layouts  7.2 us
    pallas_call x1, Pallas kernels, step_of(): pl.pallas_call(gram_matrix, out_shape=(jax.ShapeDtypeStruct((n, row_count...  6.44 us
  transfers between devices with their start and end apart: 22, of which 7 were waited for; matrix products, arithmetic and copies ran while one was open for 1% of the time, Pallas kernels for 19%

profile of v3, /device:TPU:1, one launch (start us, length us, event | category | flops | bytes accessed | tf_op | source)
XLA Modules:
  0.0 200.7 jit_solution(11109278815216511704)
XLA Ops:
  0.7 6.4 %shard_map.68 = (bf16[512,2048]{1,0:T(8,128)(2,1)}, s16[82,16,128]{2,1,0:T(8,128)(2,1)}, s16[82,16,128]{2,1,0:T(8,128)(2,1)}, s16[82,16,128]{2,1,0:T(8,128)(2,1)}, s16[82,16,128]{2,1,0:T(8,128)(2,1)}) custom-call(s32[1]{0:T(128)} %bitcast.place, s32[1,2048]{1,0:T(1,128)} %bitcast.4, bf16[2048,512]{1,0:T(8,128)(2,1)} %design.3), custom_call_target="tpu_custom_call" | custom-call | tf_op jit(solution)/shard_map/pallas_call | solution.py:425
  7.1 5.4 %collective-permute-start = (s16[82,16,128]{2,1,0:T(8,128)(2,1)}, s16[82,16,128]{2,1,0:T(8,128)(2,1)S(1)}, u32[]{:S(2)}, u32[]{:S(2)}) collective-permute-start(s16[82,16,128]{2,1,0:T(8,128)(2,1)} %get-tuple-element.27), channel_id=1, source_target_pairs={{3,0},{2,4},{1,1},{0,5},{7,2},{6,6},{5,3},{4,7},{11,11},{10,15},{9... | collective-permute-start | bytes 1007624 | tf_op jit(solution)/shard_map/ppermute | solution.py:28
  13.5 4.7 %collective-permute-start.4 = (f32[2,512]{1,0:T(2,128)S(1)}, f32[2,512]{1,0:T(2,128)S(1)}, u32[]{:S(2)}, u32[]{:S(2)}) collective-permute-start(f32[2,512]{1,0:T(2,128)S(1)} %pad_maximum_fusion), channel_id=1, source_target_pairs={{0,0},{1,4},{2,1},{3,5},{4,2},{5,6},{6,3},{7,7},{8,11},{9,15},{10,... | collective-permute-start | bytes 12296 | tf_op jit(solution)/shard_map/ppermute | solution.py:28
  18.2 3.6 %collective-permute-start.5 = (f32[1,512]{1,0:T(1,128)S(1)}, f32[1,512]{1,0:T(1,128)S(1)}, u32[]{:S(2)}, u32[]{:S(2)}) collective-permute-start(f32[1,512]{1,0:T(1,128)S(1)} %copy-done.22), channel_id=1, source_target_pairs={{0,4},{1,1},{2,5},{3,2},{4,6},{5,3},{6,7},{7,11},{8,15},{9,10},{10... | collective-permute-start | bytes 6152 | tf_op jit(solution)/shard_map/ppermute | solution.py:28
  21.9 5.9 %shard_map.72 = (s16[129,16,128]{2,1,0:T(8,128)(2,1)}, s16[129,16,128]{2,1,0:T(8,128)(2,1)}) custom-call(s32[1]{0:T(128)} %bitcast.place, s32[1,2048]{1,0:T(1,128)} %bitcast.5, bf16[512,2048]{1,0:T(8,128)(2,1)} %get-tuple-element.38.turned, bf16[2048,512]{1,0:T(8,128)(2,1)} %observed.5), custom_call_target="tpu_custom_call" | custom-call | tf_op jit(solution)/shard_map/pallas_call | solution.py:397
  27.8 5.9 %shard_map.73 = (s16[129,16,128]{2,1,0:T(8,128)(2,1)}, s16[129,16,128]{2,1,0:T(8,128)(2,1)}) custom-call(s32[1]{0:T(128)} %bitcast.place, s32[1,2048]{1,0:T(1,128)} %bitcast.6, bf16[512,2048]{1,0:T(8,128)(2,1)} %get-tuple-element.38.turned, bf16[2048,512]{1,0:T(8,128)(2,1)} %observed.5), custom_call_target="tpu_custom_call" | custom-call | tf_op jit(solution)/shard_map/pallas_call | solution.py:397
  33.8 2.3 %collective-permute-start.10 = (s16[129,16,128]{2,1,0:T(8,128)(2,1)}, s16[129,16,128]{2,1,0:T(8,128)(2,1)S(1)}, u32[]{:S(2)}, u32[]{:S(2)}) collective-permute-start(s16[129,16,128]{2,1,0:T(8,128)(2,1)} %get-tuple-element.39), channel_id=1, source_target_pairs={{3,0},{2,4},{1,1},{0,5},{7,2},{6,6},{5,3},{4,7},{11,11},{10,15},{9... | collective-permute-start | bytes 1585160 | tf_op jit(solution)/shard_map/ppermute | solution.py:28
  37.4 1.7 collective-permute-start.12
  39.1 1.9 collective-permute-start.13
  41.2 2.3 %collective-permute-start.3 = (s16[82,16,128]{2,1,0:T(8,128)(2,1)}, s16[82,16,128]{2,1,0:T(8,128)(2,1)S(1)}, u32[]{:S(2)}, u32[]{:S(2)}) collective-permute-start(s16[82,16,128]{2,1,0:T(8,128)(2,1)} %get-tuple-element.30), channel_id=1, source_target_pairs={{0,0},{1,4},{2,1},{3,5},{4,2},{5,6},{6,3},{7,7},{8,11},{9,15},{10,... | collective-permute-start | bytes 1007624 | tf_op jit(solution)/shard_map/ppermute | solution.py:28
  44.2 18.8 %collective-permute-done.3.four = s16[82,16,128]{2,1,0:T(8,128)(2,1)S(1)} collective-permute-done((s16[82,16,128]{2,1,0:T(8,128)(2,1)}, s16[82,16,128]{2,1,0:T(8,128)(2,1)S(1)}, u32[]{:S(2)}, u32[]{:S(2)}) %collective-permute-start.3) | collective-permute-done | bytes 335904 | tf_op jit(solution)/shard_map/ppermute | solution.py:28
  63.7 7.5 %shard_map.69 = (f32[512,512]{1,0:T(8,128)}, f32[512,512]{1,0:T(8,128)}, s16[82,16,128]{2,1,0:T(8,128)(2,1)}) custom-call(s16[82,16,128]{2,1,0:T(8,128)(2,1)} %copy-done.14, s16[82,16,128]{2,1,0:T(8,128)(2,1)} %copy-done.15, s16[82,16,128]{2,1,0:T(8,128)(2,1)} %copy-done.16, s16[82,16,128]{2,1,0:T(8,128)(2,1)} %copy-done.17, f32[8,512]{1,0:T(8,128)} %maximum_maximum_fusion.vec), custom_call_target="tpu_custom_call" | custom-call | tf_op jit(solution)/shard_map/pallas_call | solution.py:391
  72.6 4.5 %shard_map.74 = (f32[512,512]{1,0:T(8,128)}, s16[129,16,128]{2,1,0:T(8,128)(2,1)}) custom-call(f32[512,512]{1,0:T(8,128)} %get-tuple-element.37.x, s16[129,16,128]{2,1,0:T(8,128)(2,1)} %copy-done.3, s16[129,16,128]{2,1,0:T(8,128)(2,1)} %copy-done.4, s16[129,16,128]{2,1,0:T(8,128)(2,1)} %copy-done.5, s16[129,16,128]{2,1,0:T(8,128)(2,1)} %copy-done.6), custom_call_target="tpu_custom_call" | custom-call | tf_op jit(solution)/shard_map/pallas_call | solution.py:391
  77.1 9.6 %collective-permute-start.14 = (s16[129,16,128]{2,1,0:T(8,128)(2,1)}, s16[129,16,128]{2,1,0:T(8,128)(2,1)S(1)}, u32[]{:S(2)}, u32[]{:S(2)}) collective-permute-start(s16[129,16,128]{2,1,0:T(8,128)(2,1)} %get-tuple-element.44), channel_id=1, source_target_pairs={{0,4},{4,1},{1,5},{5,2},{2,6},{6,3},{3,7},{7,11},{11,15},{15,10},{... | collective-permute-start | bytes 1585160 | tf_op jit(solution)/shard_map/ppermute | solution.py:28
  86.6 1.9 collective-permute-start.15
  88.6 3.6 %collective-permute-start.6 = (s16[82,16,128]{2,1,0:T(8,128)(2,1)S(1)}, s16[82,16,128]{2,1,0:T(8,128)(2,1)S(1)}, u32[]{:S(2)}, u32[]{:S(2)}) collective-permute-start(s16[82,16,128]{2,1,0:T(8,128)(2,1)S(1)} %copy-done.23), channel_id=1, source_target_pairs={{0,4},{4,1},{1,5},{5,2},{2,6},{6,3},{3,7},{7,11},{11,15},{15,10},{... | collective-permute-start | bytes 1007624 | tf_op jit(solution)/shard_map/ppermute | solution.py:28
  92.2 1.9 collective-permute-start.7
  94.2 2.4 %collective-permute-done.6.low = s16[82,16,128]{2,1,0:T(8,128)(2,1)S(1)} collective-permute-done((s16[82,16,128]{2,1,0:T(8,128)(2,1)S(1)}, s16[82,16,128]{2,1,0:T(8,128)(2,1)S(1)}, u32[]{:S(2)}, u32[]{:S(2)}) %collective-permute-start.6) | collective-permute-done | bytes 335904 | tf_op jit(solution)/shard_map/ppermute | solution.py:28
  96.6 4.4 %collective-permute-done.7.high = s16[82,16,128]{2,1,0:T(8,128)(2,1)S(1)} collective-permute-done((s16[82,16,128]{2,1,0:T(8,128)(2,1)S(1)}, s16[82,16,128]{2,1,0:T(8,128)(2,1)S(1)}, u32[]{:S(2)}, u32[]{:S(2)}) %collective-permute-start.7) | collective-permute-done | bytes 335904 | tf_op jit(solution)/shard_map/ppermute | solution.py:28
  101.7 7.8 %shard_map.70 = (f32[512,512]{1,0:T(8,128)}, f32[512,512]{1,0:T(8,128)}, s16[82,16,128]{2,1,0:T(8,128)(2,1)}, s16[82,16,128]{2,1,0:T(8,128)(2,1)}) custom-call(f32[512,512]{1,0:T(8,128)} %get-tuple-element.31.b, s16[82,16,128]{2,1,0:T(8,128)(2,1)} %copy-done, s16[82,16,128]{2,1,0:T(8,128)(2,1)} %copy-done.1, f32[8,512]{1,0:T(8,128)} %maximum_maximum_fusion.vec), custom_call_target="tpu_custom_call" | custom-call | tf_op jit(solution)/shard_map/pallas_call | solution.py:391
  110.5 4.9 %shard_map.75 = (f32[512,512]{1,0:T(8,128)}, s16[129,16,128]{2,1,0:T(8,128)(2,1)}, s16[129,16,128]{2,1,0:T(8,128)(2,1)}) custom-call(f32[512,512]{1,0:T(8,128)} %get-tuple-element.36.x, f32[512,512]{1,0:T(8,128)} %get-tuple-element.43.f, s16[129,16,128]{2,1,0:T(8,128)(2,1)} %copy-done.7, s16[129,16,128]{2,1,0:T(8,128)(2,1)} %copy-done.8, ...), custom_call_target="tpu_custom_call" | custom-call | tf_op jit(solution)/shard_map/pallas_call | solution.py:391
  118.1 5.3 %collective-permute-start.8 = (s16[82,16,128]{2,1,0:T(8,128)(2,1)S(1)}, s16[82,16,128]{2,1,0:T(8,128)(2,1)S(1)}, u32[]{:S(2)}, u32[]{:S(2)}) collective-permute-start(s16[82,16,128]{2,1,0:T(8,128)(2,1)S(1)} %copy-done.25), channel_id=1, source_target_pairs={{0,1},{4,5},{1,2},{5,6},{2,3},{6,7},{3,11},{7,15},{11,10},{15,14},... | collective-permute-start | bytes 1007624 | tf_op jit(solution)/shard_map/ppermute | solution.py:28
  124.9 10.0 %collective-permute-done.8.far_low = s16[82,16,128]{2,1,0:T(8,128)(2,1)S(1)} collective-permute-done((s16[82,16,128]{2,1,0:T(8,128)(2,1)S(1)}, s16[82,16,128]{2,1,0:T(8,128)(2,1)S(1)}, u32[]{:S(2)}, u32[]{:S(2)}) %collective-permute-start.8) | collective-permute-done | bytes 335904 | tf_op jit(solution)/shard_map/ppermute | solution.py:28
  134.9 6.4 %collective-permute-done.9.far_high = s16[82,16,128]{2,1,0:T(8,128)(2,1)S(1)} collective-permute-done((s16[82,16,128]{2,1,0:T(8,128)(2,1)S(1)}, s16[82,16,128]{2,1,0:T(8,128)(2,1)S(1)}, u32[]{:S(2)}, u32[]{:S(2)}) %collective-permute-start.9) | collective-permute-done | bytes 335904 | tf_op jit(solution)/shard_map/ppermute | solution.py:28
  142.1 10.3 %shard_map.71.x = f32[512,512]{1,0:T(8,128)} custom-call(f32[512,512]{1,0:T(8,128)} %get-tuple-element.33.b, s16[82,16,128]{2,1,0:T(8,128)(2,1)} %copy-done, s16[82,16,128]{2,1,0:T(8,128)(2,1)} %copy-done.1, s16[82,16,128]{2,1,0:T(8,128)(2,1)} %copy-done.18, s16[82,16,128]{2,1,0:T(8,128)(2,1)} %copy-done.19, f32[8,512]{1,0:T(8,128)} %maximum_maximum_fusion.vec), custom_call_target="tpu_custom_call" | custom-call | tf_op jit(solution)/shard_map/pallas_call | solution.py:391
  153.4 6.5 %shard_map.76 = (s16[129,16,128]{2,1,0:T(8,128)(2,1)}, bf16[512,512]{1,0:T(8,128)(2,1)}) custom-call(f32[512,512]{1,0:T(8,128)} %shard_map.71.x, f32[512,512]{1,0:T(8,128)} %get-tuple-element.45.f, s16[82,16,128]{2,1,0:T(8,128)(2,1)} %copy-done, s16[82,16,128]{2,1,0:T(8,128)(2,1)} %copy-done.1, s16[129,16,128]{2,1,0:T(8,128)(2,1)} %copy-done.9, ...), custom_call_target="tpu_custom_call" | custom-call | tf_op jit(solution)/shard_map/pallas_call | solution.py:391
  159.9 1.9 collective-permute-start.18
  161.9 4.4 %collective-permute-start.20 = (bf16[512,512]{1,0:T(8,128)(2,1)}, bf16[512,512]{1,0:T(8,128)(2,1)S(1)}, u32[]{:S(2)}, u32[]{:S(2)}) collective-permute-start(bf16[512,512]{1,0:T(8,128)(2,1)} %get-tuple-element.49), channel_id=1, source_target_pairs={{0,2},{4,3},{1,0},{5,1},{2,6},{6,7},{3,4},{7,5},{11,10},{15,11},{1... | collective-permute-start | bytes 1572872 | tf_op jit(solution)/shard_map/ppermute | solution.py:28
  166.3 4.3 %collective-permute-start.21 = (bf16[512,512]{1,0:T(8,128)(2,1)}, bf16[512,512]{1,0:T(8,128)(2,1)S(1)}, u32[]{:S(2)}, u32[]{:S(2)}) collective-permute-start(bf16[512,512]{1,0:T(8,128)(2,1)} %get-tuple-element.49), channel_id=1, source_target_pairs={{0,3},{4,2},{1,1},{5,0},{2,7},{6,6},{3,5},{7,4},{11,11},{15,10},{1... | collective-permute-start | bytes 1572872 | tf_op jit(solution)/shard_map/ppermute | solution.py:28
  172.1 6.1 %collective-permute-done.19.one = bf16[512,512]{1,0:T(8,128)(2,1)S(1)} collective-permute-done((bf16[512,512]{1,0:T(8,128)(2,1)}, bf16[512,512]{1,0:T(8,128)(2,1)S(1)}, u32[]{:S(2)}, u32[]{:S(2)}) %collective-permute-start.19) | collective-permute-done | bytes 524320 | tf_op jit(solution)/shard_map/ppermute | solution.py:28
  178.1 11.4 %collective-permute-done.20.two = bf16[512,512]{1,0:T(8,128)(2,1)S(1)} collective-permute-done((bf16[512,512]{1,0:T(8,128)(2,1)}, bf16[512,512]{1,0:T(8,128)(2,1)S(1)}, u32[]{:S(2)}, u32[]{:S(2)}) %collective-permute-start.20) | collective-permute-done | bytes 524320 | tf_op jit(solution)/shard_map/ppermute | solution.py:28
  191.3 9.3 %shard_map.77 = (f32[512,512]{1,0:T(8,128)}, f32[2048,512]{1,0:T(8,128)}) custom-call(s32[1]{0:T(128)} %bitcast.place, s32[2048,1]{1,0:T(8,128)} %copy.7.column, bf16[2048,512]{1,0:T(8,128)(2,1)} %design.3, bf16[2048,512]{1,0:T(8,128)(2,1)} %observed.5, s16[129,16,128]{2,1,0:T(8,128)(2,1)} %copy-done.2, bf16[512,512]{1,0:T(8,128)(2,1)} %copy-done.11, ...), custom_call_target="tpu_custom_call" | custom-call | tf_op jit(solution)/shard_map/pallas_call | solution.py:464
  (80 shorter events, 16.0 us)
Async XLA Ops:
  0.6 12.9 %copy-start.21 = (f32[1,512]{1,0:T(1,128)S(1)}, f32[1,512]{1,0:T(1,128)}, u32[]{:S(2)}) copy-start(f32[1,512]{1,0:T(1,128)} %param.8) | copy-start | bytes 6148
  0.6 12.9 %copy-start.22 = (f32[1,512]{1,0:T(1,128)S(1)}, f32[1,512]{1,0:T(1,128)}, u32[]{:S(2)}) copy-start(f32[1,512]{1,0:T(1,128)} %param.9) | copy-start | bytes 6148
  7.1 30.3 %collective-permute-start = (s16[82,16,128]{2,1,0:T(8,128)(2,1)}, s16[82,16,128]{2,1,0:T(8,128)(2,1)S(1)}, u32[]{:S(2)}, u32[]{:S(2)}) collective-permute-start(s16[82,16,128]{2,1,0:T(8,128)(2,1)} %get-tuple-element.27), channel_id=1, source_target_pairs={{3,0},{2,4},{1,1},{0,5},{7,2},{6,6},{5,3},{4,7},{11,11},{10,15},{9... | collective-permute-start | bytes 1007624 | tf_op jit(solution)/shard_map/ppermute | solution.py:28
  12.6 26.6 %collective-permute-start.1 = (s16[82,16,128]{2,1,0:T(8,128)(2,1)}, s16[82,16,128]{2,1,0:T(8,128)(2,1)S(1)}, u32[]{:S(2)}, u32[]{:S(2)}) collective-permute-start(s16[82,16,128]{2,1,0:T(8,128)(2,1)} %get-tuple-element.28), channel_id=1, source_target_pairs={{2,0},{3,4},{0,1},{1,5},{6,2},{7,6},{4,3},{5,7},{10,11},{11,15},{8... | collective-permute-start | bytes 1007624 | tf_op jit(solution)/shard_map/ppermute | solution.py:28
  13.3 27.9 %collective-permute-start.2 = (s16[82,16,128]{2,1,0:T(8,128)(2,1)}, s16[82,16,128]{2,1,0:T(8,128)(2,1)S(1)}, u32[]{:S(2)}, u32[]{:S(2)}) collective-permute-start(s16[82,16,128]{2,1,0:T(8,128)(2,1)} %get-tuple-element.29), channel_id=1, source_target_pairs={{1,0},{0,4},{3,1},{2,5},{5,2},{4,6},{7,3},{6,7},{9,11},{8,15},{11,... | collective-permute-start | bytes 1007624 | tf_op jit(solution)/shard_map/ppermute | solution.py:28
  13.5 22.5 %collective-permute-start.4 = (f32[2,512]{1,0:T(2,128)S(1)}, f32[2,512]{1,0:T(2,128)S(1)}, u32[]{:S(2)}, u32[]{:S(2)}) collective-permute-start(f32[2,512]{1,0:T(2,128)S(1)} %pad_maximum_fusion), channel_id=1, source_target_pairs={{0,0},{1,4},{2,1},{3,5},{4,2},{5,6},{6,3},{7,7},{8,11},{9,15},{10,... | collective-permute-start | bytes 12296 | tf_op jit(solution)/shard_map/ppermute | solution.py:28
  18.2 15.5 %collective-permute-start.5 = (f32[1,512]{1,0:T(1,128)S(1)}, f32[1,512]{1,0:T(1,128)S(1)}, u32[]{:S(2)}, u32[]{:S(2)}) collective-permute-start(f32[1,512]{1,0:T(1,128)S(1)} %copy-done.22), channel_id=1, source_target_pairs={{0,4},{1,1},{2,5},{3,2},{4,6},{5,3},{6,7},{7,11},{8,15},{9,10},{10... | collective-permute-start | bytes 6152 | tf_op jit(solution)/shard_map/ppermute | solution.py:28
  33.8 37.5 %collective-permute-start.10 = (s16[129,16,128]{2,1,0:T(8,128)(2,1)}, s16[129,16,128]{2,1,0:T(8,128)(2,1)S(1)}, u32[]{:S(2)}, u32[]{:S(2)}) collective-permute-start(s16[129,16,128]{2,1,0:T(8,128)(2,1)} %get-tuple-element.39), channel_id=1, source_target_pairs={{3,0},{2,4},{1,1},{0,5},{7,2},{6,6},{5,3},{4,7},{11,11},{10,15},{9... | collective-permute-start | bytes 1585160 | tf_op jit(solution)/shard_map/ppermute | solution.py:28
  36.0 35.2 %collective-permute-start.11 = (s16[129,16,128]{2,1,0:T(8,128)(2,1)}, s16[129,16,128]{2,1,0:T(8,128)(2,1)S(1)}, u32[]{:S(2)}, u32[]{:S(2)}) collective-permute-start(s16[129,16,128]{2,1,0:T(8,128)(2,1)} %get-tuple-element.40), channel_id=1, source_target_pairs={{2,0},{3,4},{0,1},{1,5},{6,2},{7,6},{4,3},{5,7},{10,11},{11,15},{8... | collective-permute-start | bytes 1585160 | tf_op jit(solution)/shard_map/ppermute | solution.py:28
  37.4 25.6 %copy-start.14 = (s16[82,16,128]{2,1,0:T(8,128)(2,1)}, s16[82,16,128]{2,1,0:T(8,128)(2,1)S(1)}, u32[]{:S(2)}) copy-start(s16[82,16,128]{2,1,0:T(8,128)(2,1)S(1)} %collective-permute-done.one) | copy-start | bytes 1007620
  37.4 33.9 %collective-permute-start.12 = (s16[129,16,128]{2,1,0:T(8,128)(2,1)}, s16[129,16,128]{2,1,0:T(8,128)(2,1)S(1)}, u32[]{:S(2)}, u32[]{:S(2)}) collective-permute-start(s16[129,16,128]{2,1,0:T(8,128)(2,1)} %get-tuple-element.41), channel_id=1, source_target_pairs={{1,0},{0,4},{3,1},{2,5},{5,2},{4,6},{7,3},{6,7},{9,11},{8,15},{11,... | collective-permute-start | bytes 1585160 | tf_op jit(solution)/shard_map/ppermute | solution.py:28
  39.1 23.9 %copy-start.15 = (s16[82,16,128]{2,1,0:T(8,128)(2,1)}, s16[82,16,128]{2,1,0:T(8,128)(2,1)S(1)}, u32[]{:S(2)}) copy-start(s16[82,16,128]{2,1,0:T(8,128)(2,1)S(1)} %collective-permute-done.1.two) | copy-start | bytes 1007620
  39.1 32.1 %collective-permute-start.13 = (s16[129,16,128]{2,1,0:T(8,128)(2,1)}, s16[129,16,128]{2,1,0:T(8,128)(2,1)S(1)}, u32[]{:S(2)}, u32[]{:S(2)}) collective-permute-start(s16[129,16,128]{2,1,0:T(8,128)(2,1)} %get-tuple-element.42), channel_id=1, source_target_pairs={{0,0},{1,4},{2,1},{3,5},{4,2},{5,6},{6,3},{7,7},{8,11},{9,15},{10,... | collective-permute-start | bytes 1585160 | tf_op jit(solution)/shard_map/ppermute | solution.py:28
  41.2 21.8 %copy-start.16 = (s16[82,16,128]{2,1,0:T(8,128)(2,1)}, s16[82,16,128]{2,1,0:T(8,128)(2,1)S(1)}, u32[]{:S(2)}) copy-start(s16[82,16,128]{2,1,0:T(8,128)(2,1)S(1)} %collective-permute-done.2.three) | copy-start | bytes 1007620
  41.2 21.8 %collective-permute-start.3 = (s16[82,16,128]{2,1,0:T(8,128)(2,1)}, s16[82,16,128]{2,1,0:T(8,128)(2,1)S(1)}, u32[]{:S(2)}, u32[]{:S(2)}) collective-permute-start(s16[82,16,128]{2,1,0:T(8,128)(2,1)} %get-tuple-element.30), channel_id=1, source_target_pairs={{0,0},{1,4},{2,1},{3,5},{4,2},{5,6},{6,3},{7,7},{8,11},{9,15},{10,... | collective-permute-start | bytes 1007624 | tf_op jit(solution)/shard_map/ppermute | solution.py:28
  71.2 17.3 %copy-start.23 = (s16[82,16,128]{2,1,0:T(8,128)(2,1)S(1)}, s16[82,16,128]{2,1,0:T(8,128)(2,1)}, u32[]{:S(2)}) copy-start(s16[82,16,128]{2,1,0:T(8,128)(2,1)} %get-tuple-element.32) | copy-start | bytes 1007620
  77.1 32.5 %collective-permute-start.14 = (s16[129,16,128]{2,1,0:T(8,128)(2,1)}, s16[129,16,128]{2,1,0:T(8,128)(2,1)S(1)}, u32[]{:S(2)}, u32[]{:S(2)}) collective-permute-start(s16[129,16,128]{2,1,0:T(8,128)(2,1)} %get-tuple-element.44), channel_id=1, source_target_pairs={{0,4},{4,1},{1,5},{5,2},{2,6},{6,3},{3,7},{7,11},{11,15},{15,10},{... | collective-permute-start | bytes 1585160 | tf_op jit(solution)/shard_map/ppermute | solution.py:28
  86.6 22.9 %collective-permute-start.15 = (s16[129,16,128]{2,1,0:T(8,128)(2,1)}, s16[129,16,128]{2,1,0:T(8,128)(2,1)S(1)}, u32[]{:S(2)}, u32[]{:S(2)}) collective-permute-start(s16[129,16,128]{2,1,0:T(8,128)(2,1)} %get-tuple-element.44), channel_id=1, source_target_pairs={{4,0},{1,4},{5,1},{2,5},{6,2},{3,6},{7,3},{11,7},{15,11},{10,15},{... | collective-permute-start | bytes 1585160 | tf_op jit(solution)/shard_map/ppermute | solution.py:28
  88.6 8.0 %collective-permute-start.6 = (s16[82,16,128]{2,1,0:T(8,128)(2,1)S(1)}, s16[82,16,128]{2,1,0:T(8,128)(2,1)S(1)}, u32[]{:S(2)}, u32[]{:S(2)}) collective-permute-start(s16[82,16,128]{2,1,0:T(8,128)(2,1)S(1)} %copy-done.23), channel_id=1, source_target_pairs={{0,4},{4,1},{1,5},{5,2},{2,6},{6,3},{3,7},{7,11},{11,15},{15,10},{... | collective-permute-start | bytes 1007624 | tf_op jit(solution)/shard_map/ppermute | solution.py:28
  92.2 8.8 %collective-permute-start.7 = (s16[82,16,128]{2,1,0:T(8,128)(2,1)S(1)}, s16[82,16,128]{2,1,0:T(8,128)(2,1)S(1)}, u32[]{:S(2)}, u32[]{:S(2)}) collective-permute-start(s16[82,16,128]{2,1,0:T(8,128)(2,1)S(1)} %copy-done.23), channel_id=1, source_target_pairs={{4,0},{1,4},{5,1},{2,5},{6,2},{3,6},{7,3},{11,7},{15,11},{10,15},{... | collective-permute-start | bytes 1007624 | tf_op jit(solution)/shard_map/ppermute | solution.py:28
  109.5 8.5 %copy-start.25 = (s16[82,16,128]{2,1,0:T(8,128)(2,1)S(1)}, s16[82,16,128]{2,1,0:T(8,128)(2,1)}, u32[]{:S(2)}) copy-start(s16[82,16,128]{2,1,0:T(8,128)(2,1)} %get-tuple-element.34) | copy-start | bytes 1007620
  109.5 13.8 %copy-start.24 = (s16[82,16,128]{2,1,0:T(8,128)(2,1)S(1)}, s16[82,16,128]{2,1,0:T(8,128)(2,1)}, u32[]{:S(2)}) copy-start(s16[82,16,128]{2,1,0:T(8,128)(2,1)} %get-tuple-element.35) | copy-start | bytes 1007620
  115.4 37.0 %collective-permute-start.16 = (s16[129,16,128]{2,1,0:T(8,128)(2,1)}, s16[129,16,128]{2,1,0:T(8,128)(2,1)S(1)}, u32[]{:S(2)}, u32[]{:S(2)}) collective-permute-start(s16[129,16,128]{2,1,0:T(8,128)(2,1)} %get-tuple-element.46), channel_id=1, source_target_pairs={{0,1},{4,5},{1,2},{5,6},{2,3},{6,7},{3,11},{7,15},{11,10},{15,14},... | collective-permute-start | bytes 1585160 | tf_op jit(solution)/shard_map/ppermute | solution.py:28
  116.7 35.6 %collective-permute-start.17 = (s16[129,16,128]{2,1,0:T(8,128)(2,1)}, s16[129,16,128]{2,1,0:T(8,128)(2,1)S(1)}, u32[]{:S(2)}, u32[]{:S(2)}) collective-permute-start(s16[129,16,128]{2,1,0:T(8,128)(2,1)} %get-tuple-element.47), channel_id=1, source_target_pairs={{1,0},{5,4},{2,1},{6,5},{3,2},{7,6},{11,3},{15,7},{10,11},{14,15},... | collective-permute-start | bytes 1585160 | tf_op jit(solution)/shard_map/ppermute | solution.py:28
  118.1 16.9 %collective-permute-start.8 = (s16[82,16,128]{2,1,0:T(8,128)(2,1)S(1)}, s16[82,16,128]{2,1,0:T(8,128)(2,1)S(1)}, u32[]{:S(2)}, u32[]{:S(2)}) collective-permute-start(s16[82,16,128]{2,1,0:T(8,128)(2,1)S(1)} %copy-done.25), channel_id=1, source_target_pairs={{0,1},{4,5},{1,2},{5,6},{2,3},{6,7},{3,11},{7,15},{11,10},{15,14},... | collective-permute-start | bytes 1007624 | tf_op jit(solution)/shard_map/ppermute | solution.py:28
  123.4 18.0 %collective-permute-start.9 = (s16[82,16,128]{2,1,0:T(8,128)(2,1)S(1)}, s16[82,16,128]{2,1,0:T(8,128)(2,1)S(1)}, u32[]{:S(2)}, u32[]{:S(2)}) collective-permute-start(s16[82,16,128]{2,1,0:T(8,128)(2,1)S(1)} %copy-done.24), channel_id=1, source_target_pairs={{1,0},{5,4},{2,1},{6,5},{3,2},{7,6},{11,3},{15,7},{10,11},{14,15},... | collective-permute-start | bytes 1007624 | tf_op jit(solution)/shard_map/ppermute | solution.py:28
  152.4 18.3 %copy-start.20 = (s32[2048]{0:T(1024)S(1)}, s32[2048]{0:T(1024)}, u32[]{:S(2)}) copy-start(s32[2048]{0:T(1024)} %param.7) | copy-start | bytes 24580
  159.9 29.7 %collective-permute-start.18 = (s16[129,16,128]{2,1,0:T(8,128)(2,1)}, s16[129,16,128]{2,1,0:T(8,128)(2,1)S(1)}, u32[]{:S(2)}, u32[]{:S(2)}) collective-permute-start(s16[129,16,128]{2,1,0:T(8,128)(2,1)} %get-tuple-element.48), channel_id=1, source_target_pairs={{0,0},{4,1},{1,2},{5,3},{2,4},{6,5},{3,6},{7,7},{11,8},{15,9},{10,... | collective-permute-start | bytes 1585160 | tf_op jit(solution)/shard_map/ppermute | solution.py:28
  161.8 16.3 %collective-permute-start.19 = (bf16[512,512]{1,0:T(8,128)(2,1)}, bf16[512,512]{1,0:T(8,128)(2,1)S(1)}, u32[]{:S(2)}, u32[]{:S(2)}) collective-permute-start(bf16[512,512]{1,0:T(8,128)(2,1)} %get-tuple-element.49), channel_id=1, source_target_pairs={{0,1},{4,0},{1,3},{5,2},{2,5},{6,4},{3,7},{7,6},{11,9},{15,8},{10,... | collective-permute-start | bytes 1572872 | tf_op jit(solution)/shard_map/ppermute | solution.py:28
  161.9 27.6 %collective-permute-start.20 = (bf16[512,512]{1,0:T(8,128)(2,1)}, bf16[512,512]{1,0:T(8,128)(2,1)S(1)}, u32[]{:S(2)}, u32[]{:S(2)}) collective-permute-start(bf16[512,512]{1,0:T(8,128)(2,1)} %get-tuple-element.49), channel_id=1, source_target_pairs={{0,2},{4,3},{1,0},{5,1},{2,6},{6,7},{3,4},{7,5},{11,10},{15,11},{1... | collective-permute-start | bytes 1572872 | tf_op jit(solution)/shard_map/ppermute | solution.py:28
  166.3 23.2 %collective-permute-start.21 = (bf16[512,512]{1,0:T(8,128)(2,1)}, bf16[512,512]{1,0:T(8,128)(2,1)S(1)}, u32[]{:S(2)}, u32[]{:S(2)}) collective-permute-start(bf16[512,512]{1,0:T(8,128)(2,1)} %get-tuple-element.49), channel_id=1, source_target_pairs={{0,3},{4,2},{1,1},{5,0},{2,7},{6,6},{3,5},{7,4},{11,11},{15,10},{1... | collective-permute-start | bytes 1572872 | tf_op jit(solution)/shard_map/ppermute | solution.py:28
  178.1 11.4 %copy-start.11 = (bf16[512,512]{1,0:T(8,128)(2,1)}, bf16[512,512]{1,0:T(8,128)(2,1)S(1)}, u32[]{:S(2)}) copy-start(bf16[512,512]{1,0:T(8,128)(2,1)S(1)} %collective-permute-done.19.one) | copy-start | bytes 1572868
  (16 other events, 23.3 us)

commit v4 on v3

--- a/solution.py
+++ b/solution.py
@@ -367,24 +367,23 @@
     out16[...] = t_ref[...].astype(BF16)
 
 
-def predict(place, column, design, observed, code, one, two, three, out, residual, x_ref):
+def predict(place, column, design, partial, code, two, three, out, residual, x_ref):
     n = out.shape[0]
 
     @pl.when(pl.program_id(0) == 0)
     def _():
         unpack((code,), SIDE, out)
         x_ref[0:n, :] = out[...].astype(BF16)
-        x_ref[n : 2 * n, :] = one[...]
-        x_ref[2 * n : 3 * n, :] = two[...]
-        x_ref[3 * n : 4 * n, :] = three[...]
+        x_ref[n : 2 * n, :] = two[...]
+        x_ref[2 * n : 3 * n, :] = three[...]
 
     d = design[...]
     picked = []
-    for m in range(SLOTS):
+    for m in (0, 2, 3):
         pick = jnp.where(column[...] == (place[0] ^ m), 1.0, 0.0)
         pick = jnp.broadcast_to(pick, (d.shape[0], STEP)).astype(BF16)
         picked.append(d * jnp.concatenate([pick] * (n // STEP), axis=1))
-    residual[...] = observed[...].astype(F32) - dot1(jnp.concatenate(picked, axis=1), x_ref[...])
+    residual[...] = partial[...] - dot1(jnp.concatenate(picked, axis=1), x_ref[...])
 
 
 def call(kernel, outs, scratch, *args):
@@ -429,12 +428,9 @@
     )(where, flat, design)
     for i, m in enumerate(ROUNDS):
         parts[i] = to_seat(parts[i], m)
-    side_parts = []
-    for i in (0, 2):
-        rounds = ROUNDS[i : i + 2]
-        msgs = gram(functools.partial(gram_side, 3 - i), (side_msg,) * 2, where, flat, turned, observed)
-        for j, m in enumerate(rounds):
-            side_parts.append(to_seat(msgs[j], m))
+    side_parts = list(gram(functools.partial(gram_side, 3), (side_msg,) * SLOTS, where, flat, turned, observed))
+    for i, m in enumerate(ROUNDS):
+        side_parts[i] = to_seat(side_parts[i], m)
     mine = carry(jnp.concatenate([prior_ridge, coupling], axis=0), home, seat)
     left_link = carry(coupling, home, lambda t: seat(t + 1) if t + 1 < count else None)
     right_link = jnp.where(time == count - 1, 0.0, mine[1:2])
@@ -458,17 +454,19 @@
     states = []
     for m in range(SLOTS):
         states.append(to_arc(rounded if m else code, m))
-    chunk = row_count // SLOTS
+    picked = jnp.where((row_interval == (place ^ 1))[:, None], design, jnp.zeros((), design.dtype))
+    partial = observed.astype(F32) - jnp.dot(picked, states[1], preferred_element_type=F32)
+    chunk = row_count // 2
     whole = pl.BlockSpec(memory_space=pltpu.VMEM)
     rows = lambda width: pl.BlockSpec((chunk, width), lambda i: (i, 0))
     solution, residual = pl.pallas_call(
         predict,
-        grid=(SLOTS,),
+        grid=(2,),
         out_shape=(square, jax.ShapeDtypeStruct((row_count, n), F32)),
-        in_specs=[pl.BlockSpec(memory_space=pltpu.SMEM), rows(1), rows(n), rows(n)] + [whole] * SLOTS,
+        in_specs=[pl.BlockSpec(memory_space=pltpu.SMEM), rows(1), rows(n), rows(n), whole, whole, whole],
         out_specs=(pl.BlockSpec((n, n), lambda i: (0, 0)), rows(n)),
-        scratch_shapes=[pltpu.VMEM((SLOTS * n, n), BF16)],
-    )(where, row_interval.reshape(row_count, 1), design, observed, *states)
+        scratch_shapes=[pltpu.VMEM((3 * n, n), BF16)],
+    )(where, row_interval.reshape(row_count, 1), design, partial, states[0], states[2], states[3])
     return (solution[None], residual)
 
 

time: 204 us -> 200 us (0.980)
  the two profiles are of different devices: /device:TPU:1 before, /device:TPU:96 now
where the time goes in v4:
time: 200 us; the launch traced here: 199 us
  starting transfers between devices  65.6 us (33%)
  Pallas kernels  65.2 us (33%)
  waiting for transfers between devices  53.9 us (27%)
  local copies, waits for them, and re-layouts  8.51 us (4%)
  matrix products  4.29 us (2%)
    ppermute x22, starting transfers between devices, carry(): lax.ppermute(value, PAIR, [pair for pair in pairs if pair[1] is not None])  65.6 us
    ppermute x22, waiting for transfers between devices, carry(): lax.ppermute(value, PAIR, [pair for pair in pairs if pair[1] is not None])  53.9 us
    pallas_call x6, Pallas kernels, call(): return pl.pallas_call(kernel, out_shape=outs, scratch_shapes=scratch)(*args)  41.6 us
    pallas_call x1, Pallas kernels, gram(): pl.pallas_call(kernel, out_shape=msgs, in_specs=specs, out_specs=(pl.Bloc...  8.84 us
    pallas_call x1, Pallas kernels, step_of(): pl.pallas_call(predict, grid=(2,), out_shape=(square, jax.ShapeDtypeStruc...  8.28 us
    unnamed x50, local copies, waits for them, and re-layouts  7.07 us
    pallas_call x1, Pallas kernels, step_of(): pl.pallas_call(gram_matrix, out_shape=(jax.ShapeDtypeStruct((n, row_count...  6.46 us
    dot_general x1, matrix products, step_of(): jnp.dot(picked, states[1], preferred_element_type=F32)  4.29 us
  transfers between devices with their start and end apart: 22, of which 6 were waited for; matrix products, arithmetic and copies ran while one was open for 3% of the time, Pallas kernels for 17%

profile of v4, /device:TPU:96, one launch (start us, length us, event | category | flops | bytes accessed | tf_op | source)
XLA Modules:
  0.0 199.3 jit_solution(2134676099738227312)
XLA Ops:
  0.7 6.5 %shard_map.68 = (bf16[512,2048]{1,0:T(8,128)(2,1)}, s16[82,16,128]{2,1,0:T(8,128)(2,1)}, s16[82,16,128]{2,1,0:T(8,128)(2,1)}, s16[82,16,128]{2,1,0:T(8,128)(2,1)}, s16[82,16,128]{2,1,0:T(8,128)(2,1)}) custom-call(s32[1]{0:T(128)} %bitcast.place, s32[1,2048]{1,0:T(1,128)} %bitcast.5, bf16[2048,512]{1,0:T(8,128)(2,1)} %design.3), custom_call_target="tpu_custom_call" | custom-call | tf_op jit(solution)/shard_map/pallas_call | solution.py:424
  7.1 4.5 %collective-permute-start = (s16[82,16,128]{2,1,0:T(8,128)(2,1)}, s16[82,16,128]{2,1,0:T(8,128)(2,1)S(1)}, u32[]{:S(2)}, u32[]{:S(2)}) collective-permute-start(s16[82,16,128]{2,1,0:T(8,128)(2,1)} %get-tuple-element.27), channel_id=1, source_target_pairs={{3,0},{2,4},{1,1},{0,5},{7,2},{6,6},{5,3},{4,7},{11,11},{10,15},{9... | collective-permute-start | bytes 1007624 | tf_op jit(solution)/shard_map/ppermute | solution.py:28
  13.3 2.5 %collective-permute-start.4 = (f32[2,512]{1,0:T(2,128)S(1)}, f32[2,512]{1,0:T(2,128)S(1)}, u32[]{:S(2)}, u32[]{:S(2)}) collective-permute-start(f32[2,512]{1,0:T(2,128)S(1)} %pad_maximum_fusion), channel_id=1, source_target_pairs={{0,0},{1,4},{2,1},{3,5},{4,2},{5,6},{6,3},{7,7},{8,11},{9,15},{10,... | collective-permute-start | bytes 12296 | tf_op jit(solution)/shard_map/ppermute | solution.py:28
  15.7 4.1 %collective-permute-start.5 = (f32[1,512]{1,0:T(1,128)S(1)}, f32[1,512]{1,0:T(1,128)S(1)}, u32[]{:S(2)}, u32[]{:S(2)}) collective-permute-start(f32[1,512]{1,0:T(1,128)S(1)} %copy-done.21), channel_id=1, source_target_pairs={{0,4},{1,1},{2,5},{3,2},{4,6},{5,3},{6,7},{7,11},{8,15},{9,10},{10... | collective-permute-start | bytes 6152 | tf_op jit(solution)/shard_map/ppermute | solution.py:28
  19.8 8.8 %shard_map.72 = (s16[129,16,128]{2,1,0:T(8,128)(2,1)}, s16[129,16,128]{2,1,0:T(8,128)(2,1)}, s16[129,16,128]{2,1,0:T(8,128)(2,1)}, s16[129,16,128]{2,1,0:T(8,128)(2,1)}) custom-call(s32[1]{0:T(128)} %bitcast.place, s32[1,2048]{1,0:T(1,128)} %bitcast.6, bf16[512,2048]{1,0:T(8,128)(2,1)} %get-tuple-element.38.turned, bf16[2048,512]{1,0:T(8,128)(2,1)} %observed.1), custom_call_target="tpu_custom_call" | custom-call | tf_op jit(solution)/shard_map/pallas_call | solution.py:396
  28.7 3.2 %collective-permute-start.10 = (s16[129,16,128]{2,1,0:T(8,128)(2,1)}, s16[129,16,128]{2,1,0:T(8,128)(2,1)S(1)}, u32[]{:S(2)}, u32[]{:S(2)}) collective-permute-start(s16[129,16,128]{2,1,0:T(8,128)(2,1)} %get-tuple-element.39), channel_id=1, source_target_pairs={{3,0},{2,4},{1,1},{0,5},{7,2},{6,6},{5,3},{4,7},{11,11},{10,15},{9... | collective-permute-start | bytes 1585160 | tf_op jit(solution)/shard_map/ppermute | solution.py:28
  32.4 2.4 %collective-permute-start.12 = (s16[129,16,128]{2,1,0:T(8,128)(2,1)}, s16[129,16,128]{2,1,0:T(8,128)(2,1)S(1)}, u32[]{:S(2)}, u32[]{:S(2)}) collective-permute-start(s16[129,16,128]{2,1,0:T(8,128)(2,1)} %get-tuple-element.41), channel_id=1, source_target_pairs={{1,0},{0,4},{3,1},{2,5},{5,2},{4,6},{7,3},{6,7},{9,11},{8,15},{11,... | collective-permute-start | bytes 1585160 | tf_op jit(solution)/shard_map/ppermute | solution.py:28
  34.8 3.0 %collective-permute-start.13 = (s16[129,16,128]{2,1,0:T(8,128)(2,1)}, s16[129,16,128]{2,1,0:T(8,128)(2,1)S(1)}, u32[]{:S(2)}, u32[]{:S(2)}) collective-permute-start(s16[129,16,128]{2,1,0:T(8,128)(2,1)} %get-tuple-element.42), channel_id=1, source_target_pairs={{0,0},{1,4},{2,1},{3,5},{4,2},{5,6},{6,3},{7,7},{8,11},{9,15},{10,... | collective-permute-start | bytes 1585160 | tf_op jit(solution)/shard_map/ppermute | solution.py:28
  38.0 1.9 collective-permute-start.3
  40.6 25.4 %collective-permute-done.3.four = s16[82,16,128]{2,1,0:T(8,128)(2,1)S(1)} collective-permute-done((s16[82,16,128]{2,1,0:T(8,128)(2,1)}, s16[82,16,128]{2,1,0:T(8,128)(2,1)S(1)}, u32[]{:S(2)}, u32[]{:S(2)}) %collective-permute-start.3) | collective-permute-done | bytes 335904 | tf_op jit(solution)/shard_map/ppermute | solution.py:28
  66.7 7.5 %shard_map.69 = (f32[512,512]{1,0:T(8,128)}, f32[512,512]{1,0:T(8,128)}, s16[82,16,128]{2,1,0:T(8,128)(2,1)}) custom-call(s16[82,16,128]{2,1,0:T(8,128)(2,1)} %copy-done.13, s16[82,16,128]{2,1,0:T(8,128)(2,1)} %copy-done.14, s16[82,16,128]{2,1,0:T(8,128)(2,1)} %copy-done.15, s16[82,16,128]{2,1,0:T(8,128)(2,1)} %copy-done.16, f32[8,512]{1,0:T(8,128)} %maximum_maximum_fusion.vec), custom_call_target="tpu_custom_call" | custom-call | tf_op jit(solution)/shard_map/pallas_call | solution.py:390
  75.6 4.5 %shard_map.73 = (f32[512,512]{1,0:T(8,128)}, s16[129,16,128]{2,1,0:T(8,128)(2,1)}) custom-call(f32[512,512]{1,0:T(8,128)} %get-tuple-element.37.x, s16[129,16,128]{2,1,0:T(8,128)(2,1)} %copy-done.4, s16[129,16,128]{2,1,0:T(8,128)(2,1)} %copy-done.5, s16[129,16,128]{2,1,0:T(8,128)(2,1)} %copy-done.6, s16[129,16,128]{2,1,0:T(8,128)(2,1)} %copy-done.7), custom_call_target="tpu_custom_call" | custom-call | tf_op jit(solution)/shard_map/pallas_call | solution.py:390
  80.1 1.9 collective-permute-start.15
  82.0 2.4 %collective-permute-start.14 = (s16[129,16,128]{2,1,0:T(8,128)(2,1)}, s16[129,16,128]{2,1,0:T(8,128)(2,1)S(1)}, u32[]{:S(2)}, u32[]{:S(2)}) collective-permute-start(s16[129,16,128]{2,1,0:T(8,128)(2,1)} %get-tuple-element.44), channel_id=1, source_target_pairs={{0,4},{4,1},{1,5},{5,2},{2,6},{6,3},{3,7},{7,11},{11,15},{15,10},{... | collective-permute-start | bytes 1585160 | tf_op jit(solution)/shard_map/ppermute | solution.py:28
  84.4 3.1 %collective-permute-start.7 = (s16[82,16,128]{2,1,0:T(8,128)(2,1)S(1)}, s16[82,16,128]{2,1,0:T(8,128)(2,1)S(1)}, u32[]{:S(2)}, u32[]{:S(2)}) collective-permute-start(s16[82,16,128]{2,1,0:T(8,128)(2,1)S(1)} %copy-done.22), channel_id=1, source_target_pairs={{4,0},{1,4},{5,1},{2,5},{6,2},{3,6},{7,3},{11,7},{15,11},{10,15},{... | collective-permute-start | bytes 1007624 | tf_op jit(solution)/shard_map/ppermute | solution.py:28
  87.6 4.5 %collective-permute-start.6 = (s16[82,16,128]{2,1,0:T(8,128)(2,1)S(1)}, s16[82,16,128]{2,1,0:T(8,128)(2,1)S(1)}, u32[]{:S(2)}, u32[]{:S(2)}) collective-permute-start(s16[82,16,128]{2,1,0:T(8,128)(2,1)S(1)} %copy-done.22), channel_id=1, source_target_pairs={{0,4},{4,1},{1,5},{5,2},{2,6},{6,3},{3,7},{7,11},{11,15},{15,10},{... | collective-permute-start | bytes 1007624 | tf_op jit(solution)/shard_map/ppermute | solution.py:28
  92.5 3.8 %collective-permute-done.6.low = s16[82,16,128]{2,1,0:T(8,128)(2,1)S(1)} collective-permute-done((s16[82,16,128]{2,1,0:T(8,128)(2,1)S(1)}, s16[82,16,128]{2,1,0:T(8,128)(2,1)S(1)}, u32[]{:S(2)}, u32[]{:S(2)}) %collective-permute-start.6) | collective-permute-done | bytes 335904 | tf_op jit(solution)/shard_map/ppermute | solution.py:28
  97.1 7.8 %shard_map.70 = (f32[512,512]{1,0:T(8,128)}, f32[512,512]{1,0:T(8,128)}, s16[82,16,128]{2,1,0:T(8,128)(2,1)}, s16[82,16,128]{2,1,0:T(8,128)(2,1)}) custom-call(f32[512,512]{1,0:T(8,128)} %get-tuple-element.31.b, s16[82,16,128]{2,1,0:T(8,128)(2,1)} %copy-done.2, s16[82,16,128]{2,1,0:T(8,128)(2,1)} %copy-done.1, f32[8,512]{1,0:T(8,128)} %maximum_maximum_fusion.vec), custom_call_target="tpu_custom_call" | custom-call | tf_op jit(solution)/shard_map/pallas_call | solution.py:390
  105.9 4.9 %shard_map.74 = (f32[512,512]{1,0:T(8,128)}, s16[129,16,128]{2,1,0:T(8,128)(2,1)}, s16[129,16,128]{2,1,0:T(8,128)(2,1)}) custom-call(f32[512,512]{1,0:T(8,128)} %get-tuple-element.36.x, f32[512,512]{1,0:T(8,128)} %get-tuple-element.43.f, s16[129,16,128]{2,1,0:T(8,128)(2,1)} %copy-done.9, s16[129,16,128]{2,1,0:T(8,128)(2,1)} %copy-done.8, ...), custom_call_target="tpu_custom_call" | custom-call | tf_op jit(solution)/shard_map/pallas_call | solution.py:390
  110.8 10.1 %collective-permute-start.16 = (s16[129,16,128]{2,1,0:T(8,128)(2,1)}, s16[129,16,128]{2,1,0:T(8,128)(2,1)S(1)}, u32[]{:S(2)}, u32[]{:S(2)}) collective-permute-start(s16[129,16,128]{2,1,0:T(8,128)(2,1)} %get-tuple-element.46), channel_id=1, source_target_pairs={{0,1},{4,5},{1,2},{5,6},{2,3},{6,7},{3,11},{7,15},{11,10},{15,14},... | collective-permute-start | bytes 1585160 | tf_op jit(solution)/shard_map/ppermute | solution.py:28
  120.9 1.9 collective-permute-start.17
  122.8 6.0 %collective-permute-start.8 = (s16[82,16,128]{2,1,0:T(8,128)(2,1)S(1)}, s16[82,16,128]{2,1,0:T(8,128)(2,1)S(1)}, u32[]{:S(2)}, u32[]{:S(2)}) collective-permute-start(s16[82,16,128]{2,1,0:T(8,128)(2,1)S(1)} %copy-done.24), channel_id=1, source_target_pairs={{0,1},{4,5},{1,2},{5,6},{2,3},{6,7},{3,11},{7,15},{11,10},{15,14},... | collective-permute-start | bytes 1007624 | tf_op jit(solution)/shard_map/ppermute | solution.py:28
  128.8 2.1 %collective-permute-start.9 = (s16[82,16,128]{2,1,0:T(8,128)(2,1)S(1)}, s16[82,16,128]{2,1,0:T(8,128)(2,1)S(1)}, u32[]{:S(2)}, u32[]{:S(2)}) collective-permute-start(s16[82,16,128]{2,1,0:T(8,128)(2,1)S(1)} %copy-done.23), channel_id=1, source_target_pairs={{1,0},{5,4},{2,1},{6,5},{3,2},{7,6},{11,3},{15,7},{10,11},{14,15},... | collective-permute-start | bytes 1007624 | tf_op jit(solution)/shard_map/ppermute | solution.py:28
  131.0 4.5 %collective-permute-done.8.far_low = s16[82,16,128]{2,1,0:T(8,128)(2,1)S(1)} collective-permute-done((s16[82,16,128]{2,1,0:T(8,128)(2,1)S(1)}, s16[82,16,128]{2,1,0:T(8,128)(2,1)S(1)}, u32[]{:S(2)}, u32[]{:S(2)}) %collective-permute-start.8) | collective-permute-done | bytes 335904 | tf_op jit(solution)/shard_map/ppermute | solution.py:28
  135.5 6.2 %collective-permute-done.9.far_high = s16[82,16,128]{2,1,0:T(8,128)(2,1)S(1)} collective-permute-done((s16[82,16,128]{2,1,0:T(8,128)(2,1)S(1)}, s16[82,16,128]{2,1,0:T(8,128)(2,1)S(1)}, u32[]{:S(2)}, u32[]{:S(2)}) %collective-permute-start.9) | collective-permute-done | bytes 335904 | tf_op jit(solution)/shard_map/ppermute | solution.py:28
  142.5 10.3 %shard_map.71.x = f32[512,512]{1,0:T(8,128)} custom-call(f32[512,512]{1,0:T(8,128)} %get-tuple-element.33.b, s16[82,16,128]{2,1,0:T(8,128)(2,1)} %copy-done.2, s16[82,16,128]{2,1,0:T(8,128)(2,1)} %copy-done.1, s16[82,16,128]{2,1,0:T(8,128)(2,1)} %copy-done.17, s16[82,16,128]{2,1,0:T(8,128)(2,1)} %copy-done.18, f32[8,512]{1,0:T(8,128)} %maximum_maximum_fusion.vec), custom_call_target="tpu_custom_call" | custom-call | tf_op jit(solution)/shard_map/pallas_call | solution.py:390
  153.7 6.7 %shard_map.75 = (s16[129,16,128]{2,1,0:T(8,128)(2,1)}, bf16[512,512]{1,0:T(8,128)(2,1)}) custom-call(f32[512,512]{1,0:T(8,128)} %shard_map.71.x, f32[512,512]{1,0:T(8,128)} %get-tuple-element.45.f, s16[82,16,128]{2,1,0:T(8,128)(2,1)} %copy-done.2, s16[82,16,128]{2,1,0:T(8,128)(2,1)} %copy-done.1, s16[129,16,128]{2,1,0:T(8,128)(2,1)} %copy-done.10, ...), custom_call_target="tpu_custom_call" | custom-call | tf_op jit(solution)/shard_map/pallas_call | solution.py:390
  160.4 1.9 collective-permute-start.21
  162.4 7.7 %collective-permute-start.19 = (s16[129,16,128]{2,1,0:T(8,128)(2,1)}, s16[129,16,128]{2,1,0:T(8,128)(2,1)S(1)}, u32[]{:S(2)}, u32[]{:S(2)}) collective-permute-start(s16[129,16,128]{2,1,0:T(8,128)(2,1)} %get-tuple-element.49), channel_id=1, source_target_pairs={{0,0},{4,1},{1,2},{5,3},{2,4},{6,5},{3,6},{7,7},{11,8},{15,9},{10,... | collective-permute-start | bytes 1585160 | tf_op jit(solution)/shard_map/ppermute | solution.py:28
  171.5 13.6 %collective-permute-done.18 = bf16[512,512]{1,0:T(8,128)(2,1)} collective-permute-done((bf16[512,512]{1,0:T(8,128)(2,1)}, bf16[512,512]{1,0:T(8,128)(2,1)}, u32[]{:S(2)}, u32[]{:S(2)}) %collective-permute-start.18) | collective-permute-done | bytes 524320 | tf_op jit(solution)/shard_map/ppermute | solution.py:28
  185.1 4.3 %convert_subtract_fusion.partial = f32[2048,512]{1,0:T(8,128)} fusion(bf16[2048,512]{1,0:T(8,128)(2,1)} %observed.1, bf16[512,512]{1,0:T(8,128)(2,1)} %collective-permute-done.18, bf16[2048,512]{1,0:T(8,128)(2,1)S(1)} %copy-done, pred[2048]{0:T(1024)(128)(4,1)S(1)} %broadcast_compare_fusion), kind=kOutput, calls=%fused_computation | convolution fusion | flops 1076887552 | bytes 8914944 | tf_op jit(solution)/shard_map/dot_general | solution.py:458
  191.0 8.3 %shard_map.76 = (f32[512,512]{1,0:T(8,128)}, f32[2048,512]{1,0:T(8,128)}) custom-call(s32[1]{0:T(128)} %bitcast.place, s32[2048,1]{1,0:T(8,128)} %copy.7.column, bf16[2048,512]{1,0:T(8,128)(2,1)} %design.3, f32[2048,512]{1,0:T(8,128)} %convert_subtract_fusion.partial, s16[129,16,128]{2,1,0:T(8,128)(2,1)} %copy-done.3, ...), custom_call_target="tpu_custom_call" | custom-call | tf_op jit(solution)/shard_map/pallas_call | solution.py:462
  (79 shorter events, 11.8 us)
Async XLA Ops:
  0.6 12.6 %copy-start.21 = (f32[1,512]{1,0:T(1,128)S(1)}, f32[1,512]{1,0:T(1,128)}, u32[]{:S(2)}) copy-start(f32[1,512]{1,0:T(1,128)} %param.9) | copy-start | bytes 6148
  0.6 12.6 %copy-start.20 = (f32[1,512]{1,0:T(1,128)S(1)}, f32[1,512]{1,0:T(1,128)}, u32[]{:S(2)}) copy-start(f32[1,512]{1,0:T(1,128)} %param.8) | copy-start | bytes 6148
  7.1 25.3 %collective-permute-start = (s16[82,16,128]{2,1,0:T(8,128)(2,1)}, s16[82,16,128]{2,1,0:T(8,128)(2,1)S(1)}, u32[]{:S(2)}, u32[]{:S(2)}) collective-permute-start(s16[82,16,128]{2,1,0:T(8,128)(2,1)} %get-tuple-element.27), channel_id=1, source_target_pairs={{3,0},{2,4},{1,1},{0,5},{7,2},{6,6},{5,3},{4,7},{11,11},{10,15},{9... | collective-permute-start | bytes 1007624 | tf_op jit(solution)/shard_map/ppermute | solution.py:28
  11.7 23.2 %collective-permute-start.1 = (s16[82,16,128]{2,1,0:T(8,128)(2,1)}, s16[82,16,128]{2,1,0:T(8,128)(2,1)S(1)}, u32[]{:S(2)}, u32[]{:S(2)}) collective-permute-start(s16[82,16,128]{2,1,0:T(8,128)(2,1)} %get-tuple-element.28), channel_id=1, source_target_pairs={{2,0},{3,4},{0,1},{1,5},{6,2},{7,6},{4,3},{5,7},{10,11},{11,15},{8... | collective-permute-start | bytes 1007624 | tf_op jit(solution)/shard_map/ppermute | solution.py:28
  13.0 25.0 %collective-permute-start.2 = (s16[82,16,128]{2,1,0:T(8,128)(2,1)}, s16[82,16,128]{2,1,0:T(8,128)(2,1)S(1)}, u32[]{:S(2)}, u32[]{:S(2)}) collective-permute-start(s16[82,16,128]{2,1,0:T(8,128)(2,1)} %get-tuple-element.29), channel_id=1, source_target_pairs={{1,0},{0,4},{3,1},{2,5},{5,2},{4,6},{7,3},{6,7},{9,11},{8,15},{11,... | collective-permute-start | bytes 1007624 | tf_op jit(solution)/shard_map/ppermute | solution.py:28
  13.3 18.7 %collective-permute-start.4 = (f32[2,512]{1,0:T(2,128)S(1)}, f32[2,512]{1,0:T(2,128)S(1)}, u32[]{:S(2)}, u32[]{:S(2)}) collective-permute-start(f32[2,512]{1,0:T(2,128)S(1)} %pad_maximum_fusion), channel_id=1, source_target_pairs={{0,0},{1,4},{2,1},{3,5},{4,2},{5,6},{6,3},{7,7},{8,11},{9,15},{10,... | collective-permute-start | bytes 12296 | tf_op jit(solution)/shard_map/ppermute | solution.py:28
  15.7 13.0 %collective-permute-start.5 = (f32[1,512]{1,0:T(1,128)S(1)}, f32[1,512]{1,0:T(1,128)S(1)}, u32[]{:S(2)}, u32[]{:S(2)}) collective-permute-start(f32[1,512]{1,0:T(1,128)S(1)} %copy-done.21), channel_id=1, source_target_pairs={{0,4},{1,1},{2,5},{3,2},{4,6},{5,3},{6,7},{7,11},{8,15},{9,10},{10... | collective-permute-start | bytes 6152 | tf_op jit(solution)/shard_map/ppermute | solution.py:28
  28.7 45.5 %collective-permute-start.10 = (s16[129,16,128]{2,1,0:T(8,128)(2,1)}, s16[129,16,128]{2,1,0:T(8,128)(2,1)S(1)}, u32[]{:S(2)}, u32[]{:S(2)}) collective-permute-start(s16[129,16,128]{2,1,0:T(8,128)(2,1)} %get-tuple-element.39), channel_id=1, source_target_pairs={{3,0},{2,4},{1,1},{0,5},{7,2},{6,6},{5,3},{4,7},{11,11},{10,15},{9... | collective-permute-start | bytes 1585160 | tf_op jit(solution)/shard_map/ppermute | solution.py:28
  31.9 42.3 %collective-permute-start.11 = (s16[129,16,128]{2,1,0:T(8,128)(2,1)}, s16[129,16,128]{2,1,0:T(8,128)(2,1)S(1)}, u32[]{:S(2)}, u32[]{:S(2)}) collective-permute-start(s16[129,16,128]{2,1,0:T(8,128)(2,1)} %get-tuple-element.40), channel_id=1, source_target_pairs={{2,0},{3,4},{0,1},{1,5},{6,2},{7,6},{4,3},{5,7},{10,11},{11,15},{8... | collective-permute-start | bytes 1585160 | tf_op jit(solution)/shard_map/ppermute | solution.py:28
  32.4 33.6 %copy-start.13 = (s16[82,16,128]{2,1,0:T(8,128)(2,1)}, s16[82,16,128]{2,1,0:T(8,128)(2,1)S(1)}, u32[]{:S(2)}) copy-start(s16[82,16,128]{2,1,0:T(8,128)(2,1)S(1)} %collective-permute-done.one) | copy-start | bytes 1007620
  32.4 41.9 %collective-permute-start.12 = (s16[129,16,128]{2,1,0:T(8,128)(2,1)}, s16[129,16,128]{2,1,0:T(8,128)(2,1)S(1)}, u32[]{:S(2)}, u32[]{:S(2)}) collective-permute-start(s16[129,16,128]{2,1,0:T(8,128)(2,1)} %get-tuple-element.41), channel_id=1, source_target_pairs={{1,0},{0,4},{3,1},{2,5},{5,2},{4,6},{7,3},{6,7},{9,11},{8,15},{11,... | collective-permute-start | bytes 1585160 | tf_op jit(solution)/shard_map/ppermute | solution.py:28
  34.8 31.1 %copy-start.14 = (s16[82,16,128]{2,1,0:T(8,128)(2,1)}, s16[82,16,128]{2,1,0:T(8,128)(2,1)S(1)}, u32[]{:S(2)}) copy-start(s16[82,16,128]{2,1,0:T(8,128)(2,1)S(1)} %collective-permute-done.1.two) | copy-start | bytes 1007620
  34.8 39.4 %collective-permute-start.13 = (s16[129,16,128]{2,1,0:T(8,128)(2,1)}, s16[129,16,128]{2,1,0:T(8,128)(2,1)S(1)}, u32[]{:S(2)}, u32[]{:S(2)}) collective-permute-start(s16[129,16,128]{2,1,0:T(8,128)(2,1)} %get-tuple-element.42), channel_id=1, source_target_pairs={{0,0},{1,4},{2,1},{3,5},{4,2},{5,6},{6,3},{7,7},{8,11},{9,15},{10,... | collective-permute-start | bytes 1585160 | tf_op jit(solution)/shard_map/ppermute | solution.py:28
  38.0 28.0 %copy-start.15 = (s16[82,16,128]{2,1,0:T(8,128)(2,1)}, s16[82,16,128]{2,1,0:T(8,128)(2,1)S(1)}, u32[]{:S(2)}) copy-start(s16[82,16,128]{2,1,0:T(8,128)(2,1)S(1)} %collective-permute-done.2.three) | copy-start | bytes 1007620
  38.0 28.0 %collective-permute-start.3 = (s16[82,16,128]{2,1,0:T(8,128)(2,1)}, s16[82,16,128]{2,1,0:T(8,128)(2,1)S(1)}, u32[]{:S(2)}, u32[]{:S(2)}) collective-permute-start(s16[82,16,128]{2,1,0:T(8,128)(2,1)} %get-tuple-element.30), channel_id=1, source_target_pairs={{0,0},{1,4},{2,1},{3,5},{4,2},{5,6},{6,3},{7,7},{8,11},{9,15},{10,... | collective-permute-start | bytes 1007624 | tf_op jit(solution)/shard_map/ppermute | solution.py:28
  74.2 10.2 %copy-start.22 = (s16[82,16,128]{2,1,0:T(8,128)(2,1)S(1)}, s16[82,16,128]{2,1,0:T(8,128)(2,1)}, u32[]{:S(2)}) copy-start(s16[82,16,128]{2,1,0:T(8,128)(2,1)} %get-tuple-element.32) | copy-start | bytes 1007620
  80.1 24.8 %collective-permute-start.15 = (s16[129,16,128]{2,1,0:T(8,128)(2,1)}, s16[129,16,128]{2,1,0:T(8,128)(2,1)S(1)}, u32[]{:S(2)}, u32[]{:S(2)}) collective-permute-start(s16[129,16,128]{2,1,0:T(8,128)(2,1)} %get-tuple-element.44), channel_id=1, source_target_pairs={{4,0},{1,4},{5,1},{2,5},{6,2},{3,6},{7,3},{11,7},{15,11},{10,15},{... | collective-permute-start | bytes 1585160 | tf_op jit(solution)/shard_map/ppermute | solution.py:28
  82.0 22.9 %collective-permute-start.14 = (s16[129,16,128]{2,1,0:T(8,128)(2,1)}, s16[129,16,128]{2,1,0:T(8,128)(2,1)S(1)}, u32[]{:S(2)}, u32[]{:S(2)}) collective-permute-start(s16[129,16,128]{2,1,0:T(8,128)(2,1)} %get-tuple-element.44), channel_id=1, source_target_pairs={{0,4},{4,1},{1,5},{5,2},{2,6},{6,3},{3,7},{7,11},{11,15},{15,10},{... | collective-permute-start | bytes 1585160 | tf_op jit(solution)/shard_map/ppermute | solution.py:28
  84.4 8.1 %collective-permute-start.7 = (s16[82,16,128]{2,1,0:T(8,128)(2,1)S(1)}, s16[82,16,128]{2,1,0:T(8,128)(2,1)S(1)}, u32[]{:S(2)}, u32[]{:S(2)}) collective-permute-start(s16[82,16,128]{2,1,0:T(8,128)(2,1)S(1)} %copy-done.22), channel_id=1, source_target_pairs={{4,0},{1,4},{5,1},{2,5},{6,2},{3,6},{7,3},{11,7},{15,11},{10,15},{... | collective-permute-start | bytes 1007624 | tf_op jit(solution)/shard_map/ppermute | solution.py:28
  87.6 8.8 %collective-permute-start.6 = (s16[82,16,128]{2,1,0:T(8,128)(2,1)S(1)}, s16[82,16,128]{2,1,0:T(8,128)(2,1)S(1)}, u32[]{:S(2)}, u32[]{:S(2)}) collective-permute-start(s16[82,16,128]{2,1,0:T(8,128)(2,1)S(1)} %copy-done.22), channel_id=1, source_target_pairs={{0,4},{4,1},{1,5},{5,2},{2,6},{6,3},{3,7},{7,11},{11,15},{15,10},{... | collective-permute-start | bytes 1007624 | tf_op jit(solution)/shard_map/ppermute | solution.py:28
  104.9 17.9 %copy-start.24 = (s16[82,16,128]{2,1,0:T(8,128)(2,1)S(1)}, s16[82,16,128]{2,1,0:T(8,128)(2,1)}, u32[]{:S(2)}) copy-start(s16[82,16,128]{2,1,0:T(8,128)(2,1)} %get-tuple-element.34) | copy-start | bytes 1007620
  104.9 23.9 %copy-start.23 = (s16[82,16,128]{2,1,0:T(8,128)(2,1)S(1)}, s16[82,16,128]{2,1,0:T(8,128)(2,1)}, u32[]{:S(2)}) copy-start(s16[82,16,128]{2,1,0:T(8,128)(2,1)} %get-tuple-element.35) | copy-start | bytes 1007620
  110.8 42.0 %collective-permute-start.16 = (s16[129,16,128]{2,1,0:T(8,128)(2,1)}, s16[129,16,128]{2,1,0:T(8,128)(2,1)S(1)}, u32[]{:S(2)}, u32[]{:S(2)}) collective-permute-start(s16[129,16,128]{2,1,0:T(8,128)(2,1)} %get-tuple-element.46), channel_id=1, source_target_pairs={{0,1},{4,5},{1,2},{5,6},{2,3},{6,7},{3,11},{7,15},{11,10},{15,14},... | collective-permute-start | bytes 1585160 | tf_op jit(solution)/shard_map/ppermute | solution.py:28
  120.9 31.9 %collective-permute-start.17 = (s16[129,16,128]{2,1,0:T(8,128)(2,1)}, s16[129,16,128]{2,1,0:T(8,128)(2,1)S(1)}, u32[]{:S(2)}, u32[]{:S(2)}) collective-permute-start(s16[129,16,128]{2,1,0:T(8,128)(2,1)} %get-tuple-element.47), channel_id=1, source_target_pairs={{1,0},{5,4},{2,1},{6,5},{3,2},{7,6},{11,3},{15,7},{10,11},{14,15},... | collective-permute-start | bytes 1585160 | tf_op jit(solution)/shard_map/ppermute | solution.py:28
  122.8 12.7 %collective-permute-start.8 = (s16[82,16,128]{2,1,0:T(8,128)(2,1)S(1)}, s16[82,16,128]{2,1,0:T(8,128)(2,1)S(1)}, u32[]{:S(2)}, u32[]{:S(2)}) collective-permute-start(s16[82,16,128]{2,1,0:T(8,128)(2,1)S(1)} %copy-done.24), channel_id=1, source_target_pairs={{0,1},{4,5},{1,2},{5,6},{2,3},{6,7},{3,11},{7,15},{11,10},{15,14},... | collective-permute-start | bytes 1007624 | tf_op jit(solution)/shard_map/ppermute | solution.py:28
  128.8 12.9 %collective-permute-start.9 = (s16[82,16,128]{2,1,0:T(8,128)(2,1)S(1)}, s16[82,16,128]{2,1,0:T(8,128)(2,1)S(1)}, u32[]{:S(2)}, u32[]{:S(2)}) collective-permute-start(s16[82,16,128]{2,1,0:T(8,128)(2,1)S(1)} %copy-done.23), channel_id=1, source_target_pairs={{1,0},{5,4},{2,1},{6,5},{3,2},{7,6},{11,3},{15,7},{10,11},{14,15},... | collective-permute-start | bytes 1007624 | tf_op jit(solution)/shard_map/ppermute | solution.py:28
  152.8 17.4 %copy-start.19 = (s32[2048]{0:T(1024)S(1)}, s32[2048]{0:T(1024)}, u32[]{:S(2)}) copy-start(s32[2048]{0:T(1024)} %param.7) | copy-start | bytes 24580
  153.7 31.4 %copy-start = (bf16[2048,512]{1,0:T(8,128)(2,1)S(1)}, bf16[2048,512]{1,0:T(8,128)(2,1)}, u32[]{:S(2)}) copy-start(bf16[2048,512]{1,0:T(8,128)(2,1)} %design.3) | copy-start | bytes 6291460
  160.4 24.7 %collective-permute-start.18 = (bf16[512,512]{1,0:T(8,128)(2,1)}, bf16[512,512]{1,0:T(8,128)(2,1)}, u32[]{:S(2)}, u32[]{:S(2)}) collective-permute-start(bf16[512,512]{1,0:T(8,128)(2,1)} %get-tuple-element.48), channel_id=1, source_target_pairs={{0,1},{4,0},{1,3},{5,2},{2,5},{6,4},{3,7},{7,6},{11,9},{15,8},{10,... | collective-permute-start | bytes 1572872 | tf_op jit(solution)/shard_map/ppermute | solution.py:28
  160.4 29.0 %collective-permute-start.21 = (bf16[512,512]{1,0:T(8,128)(2,1)}, bf16[512,512]{1,0:T(8,128)(2,1)S(1)}, u32[]{:S(2)}, u32[]{:S(2)}) collective-permute-start(bf16[512,512]{1,0:T(8,128)(2,1)} %get-tuple-element.48), channel_id=1, source_target_pairs={{0,3},{4,2},{1,1},{5,0},{2,7},{6,6},{3,5},{7,4},{11,11},{15,10},{1... | collective-permute-start | bytes 1572872 | tf_op jit(solution)/shard_map/ppermute | solution.py:28
  162.3 27.1 %collective-permute-start.20 = (bf16[512,512]{1,0:T(8,128)(2,1)}, bf16[512,512]{1,0:T(8,128)(2,1)}, u32[]{:S(2)}, u32[]{:S(2)}) collective-permute-start(bf16[512,512]{1,0:T(8,128)(2,1)} %get-tuple-element.48), channel_id=1, source_target_pairs={{0,2},{4,3},{1,0},{5,1},{2,6},{6,7},{3,4},{7,5},{11,10},{15,11},{1... | collective-permute-start | bytes 1572872 | tf_op jit(solution)/shard_map/ppermute | solution.py:28
  162.4 27.0 %collective-permute-start.19 = (s16[129,16,128]{2,1,0:T(8,128)(2,1)}, s16[129,16,128]{2,1,0:T(8,128)(2,1)S(1)}, u32[]{:S(2)}, u32[]{:S(2)}) collective-permute-start(s16[129,16,128]{2,1,0:T(8,128)(2,1)} %get-tuple-element.49), channel_id=1, source_target_pairs={{0,0},{4,1},{1,2},{5,3},{2,4},{6,5},{3,6},{7,7},{11,8},{15,9},{10,... | collective-permute-start | bytes 1585160 | tf_op jit(solution)/shard_map/ppermute | solution.py:28
  (15 other events, 21.6 us)
